TPU v7x, 32 devices: a whole 2x2x4 slice. The times are simulated.
32 devices in a mesh: grp: 8 (over z, core), sub: 4 (over y, x).
Axes of the slice: x: 2, y: 2, z: 4, core: 2. Of those that a mesh axis runs over, the one named last changes fastest.
Arguments:
- right_side: float32 [8, 4, 512, 128], P('grp', 'sub'), may hold values from -6 to 6
- live_rows: int32 [8, 4], P('grp', 'sub'), may hold values from 384 to 512, as said below
- margin_blocks: int32 [8, 4, 2], P('grp', 'sub'), may hold values from 0 to 5, as said below
- local_operator: bfloat16 [8, 4, 640, 640], P('grp', 'sub'), may hold values from -0.25 to 0.25
- local_inverse: bfloat16 [8, 4, 640, 640], P('grp', 'sub'), may hold values from -0.25 to 0.25
- deflation: bfloat16 [8, 4, 640, 16], P('grp', 'sub'), may hold values from -0.5 to 0.5
- coarse_inverse: bfloat16 [512, 512], P('grp', 'sub'), may hold values from -0.25 to 0.25
Outputs:
- solution_field: float32 [8, 4, 512, 128], P('grp', 'sub')
- residual: float32 [8, 4, 512, 128], P('grp', 'sub')
Inputs may be any that keep to these rules, and one draw needn't show every extreme that they name: `live_rows`: some subdomain has 512 live rows and some has 384. `margin_blocks`: the two blocks a subdomain lends differ.
All inputs are finite; a program needn't handle non-finite values.
Results may differ from a plain program's by a relative error of at most 0.015.
Values may be sent and summed in bfloat16 or wider, within the bound.
No kernel may reach another device: no remote copies, remote signals or barrier semaphores. Data moves between devices by JAX's collectives and lax.ppermute only.
A program may use at most 64 MiB of HBM per device.

v0:
```python
import jax
import jax.numpy as jnp
from jax import lax
from jax.sharding import PartitionSpec as P

ITERS = 3


STEP_SIZES = (0.8, 0.9, 1.0)
MOMENTUM = (0.0, 0.3, 0.3)


def with_halo(block, sides, width):
    for axis, dim in sides:
        count = lax.axis_size(axis)
        forward = [(i, i + 1) for i in range(count - 1)]
        backward = [(target, source) for source, target in forward]
        low = lax.ppermute(
            lax.slice_in_dim(block, block.shape[dim] - width, None, axis=dim), axis, forward
        )
        high = lax.ppermute(lax.slice_in_dim(block, 0, width, axis=dim), axis, backward)
        block = jnp.concatenate([low, block, high], axis=dim)
    return block


def take_block(vector, block_index, block_rows):
    return lax.dynamic_slice_in_dim(vector, block_index * block_rows, block_rows, 0)


def add_block(vector, block_index, addend, block_rows):
    first_row = block_index * block_rows
    current = lax.dynamic_slice_in_dim(vector, first_row, block_rows, 0)
    return lax.dynamic_update_slice_in_dim(vector, current + addend, first_row, 0)


def body(
    right_side, live_rows, margin_blocks, local_operator, local_inverse, deflation, coarse_inverse
):
    source = right_side[0, 0]
    owned_rows = source.shape[0]
    block_rows = (local_operator.shape[2] - owned_rows) // 2
    live_mask = (jnp.arange(owned_rows, dtype=jnp.int32)[:, None] < live_rows[0, 0]).astype(
        jnp.float32
    )
    give_right = margin_blocks[0, 0, 0]
    give_left = margin_blocks[0, 0, 1]
    operator = local_operator[0, 0]
    inverse = local_inverse[0, 0]
    vectors = deflation[0, 0]
    position = lax.axis_index("sub")
    has_left = (position > 0).astype(jnp.float32)
    has_right = (position < lax.axis_size("sub") - 1).astype(jnp.float32)

    def joined(local):
        own_part = local[:owned_rows]
        left_rows = local[owned_rows : owned_rows + block_rows]
        right_rows = local[owned_rows + block_rows :]
        outgoing = jnp.concatenate(
            [
                left_rows,
                take_block(own_part, give_left, block_rows),
                take_block(own_part, give_right, block_rows),
                right_rows,
            ],
            axis=0,
        )
        extended = with_halo(outgoing.astype(jnp.bfloat16), (("sub", 0),), 2 * block_rows).astype(
            outgoing.dtype
        )
        assembled = own_part * live_mask
        assembled = add_block(
            assembled, give_left, extended[block_rows : 2 * block_rows], block_rows
        )
        assembled = add_block(
            assembled, give_right, extended[6 * block_rows : 7 * block_rows], block_rows
        )
        left_slot = (extended[:block_rows] + left_rows) * has_left
        right_slot = (extended[7 * block_rows :] + right_rows) * has_right
        return (assembled, jnp.concatenate([left_slot, right_slot], axis=0))

    residual = source * live_mask
    solution = jnp.zeros_like(residual)
    direction = jnp.zeros_like(residual)
    outgoing = jnp.concatenate(
        [take_block(residual, give_left, block_rows), take_block(residual, give_right, block_rows)],
        axis=0,
    )
    extended = with_halo(outgoing.astype(jnp.bfloat16), (("sub", 0),), block_rows).astype(
        outgoing.dtype
    )
    resid_rim = jnp.concatenate([extended[:block_rows], extended[3 * block_rows :]], axis=0)
    direction_rim = jnp.zeros_like(resid_rim)
    for turn_index in range(ITERS):
        local_resid = jnp.concatenate([residual, resid_rim], axis=0).astype(jnp.bfloat16)
        fine_part = jnp.dot(inverse, local_resid, preferred_element_type=jnp.float32)
        coarse_resid = lax.dot_general(
            vectors, local_resid, (((0,), (0,)), ((), ())), preferred_element_type=jnp.float32
        ).astype(jnp.bfloat16)
        column = lax.all_gather(coarse_resid, "grp", axis=0, tiled=True)
        correction = lax.psum_scatter(
            jnp.dot(coarse_inverse, column, preferred_element_type=jnp.float32).astype(
                jnp.bfloat16
            ),
            "sub",
            scatter_dimension=0,
            tiled=True,
        )
        update, update_rim = joined(
            fine_part + jnp.dot(vectors, correction, preferred_element_type=jnp.float32)
        )
        direction = update + MOMENTUM[turn_index] * direction
        direction_rim = update_rim + MOMENTUM[turn_index] * direction_rim
        solution = solution + STEP_SIZES[turn_index] * direction
        local_dir = jnp.concatenate([direction, direction_rim], axis=0).astype(jnp.bfloat16)
        applied, applied_rim = joined(
            jnp.dot(operator, local_dir, preferred_element_type=jnp.float32)
        )
        residual = residual - STEP_SIZES[turn_index] * applied
        resid_rim = resid_rim - STEP_SIZES[turn_index] * applied_rim
    return (solution[None, None], residual[None, None])


def solution(mesh):
    return jax.shard_map(
        body,
        mesh=mesh,
        in_specs=(
            P("grp", "sub", None, None),
            P("grp", "sub"),
            P("grp", "sub", None),
            P("grp", "sub", None, None),
            P("grp", "sub", None, None),
            P("grp", "sub", None, None),
            P("grp", "sub"),
        ),
        out_specs=(P("grp", "sub", None, None), P("grp", "sub", None, None)),
        check_vma=False,
    )
```

profile of v0, /device:TPU:0, one launch (start us, length us, event | category | flops | bytes accessed | tf_op | source)
XLA Modules:
  0.0 190.7 jit_solution(5329523645962224355)
XLA Ops:
  0.6 1.3 fusion.83
  3.9 1.1 copy.12
  5.2 5.0 %collective-permute-start = (bf16[64,128]{0,1:T(8,128)(2,1)S(1)}, bf16[64,128]{0,1:T(8,128)(2,1)S(1)}, u32[]{:S(2)}, u32[]{:S(2)}) collective-permute-start(bf16[64,128]{0,1:T(8,128)(2,1)S(1)} %get-tuple-element.43), channel_id=1, source_target_pairs={{0,1},{1,2},{2,3},{4,5},{5,6},{6,7},{8,9},{9,10},{10,11},{12,13},{... | collective-permute-start | bytes 49160 | tf_op jit(solution)/shard_map/ppermute | solution.py:18
  10.2 1.3 collective-permute-start.1
  12.8 3.2 %collective-permute-done.1 = bf16[64,128]{0,1:T(8,128)(2,1)S(1)} collective-permute-done((bf16[64,128]{0,1:T(8,128)(2,1)S(1)}, bf16[64,128]{0,1:T(8,128)(2,1)S(1)}, u32[]{:S(2)}, u32[]{:S(2)}) %collective-permute-start.1) | collective-permute-done | bytes 16416 | tf_op jit(solution)/shard_map/ppermute | solution.py:21
  16.4 14.5 %all_gather.9 = bf16[128,128]{1,0:T(8,128)(2,1)S(1)} all-gather(bf16[16,128]{1,0:T(8,128)(2,1)S(1)} %fusion.6), channel_id=1, replica_groups=mesh['grp'=8,'sub'=4] {'grp'}, dimensions={0}, use_global_device_ids=true | all-gather | bytes 36864 | tf_op jit(solution)/shard_map/all_gather | solution.py:99
  31.1 16.3 %all-reduce = bf16[64,128]{0,1:T(8,128)(2,1)S(1)} all-reduce(bf16[64,128]{0,1:T(8,128)(2,1)S(1)} %fusion.3), channel_id=2, replica_groups=mesh['grp'=8,'sub'=4] {'sub'}, use_global_device_ids=true, to_apply=%region_0.0.clone | all-reduce | flops 8192 | bytes 32768
  48.3 1.7 collective-permute-start.2
  50.1 1.3 collective-permute-start.3
  51.6 5.5 %collective-permute-done.3 = bf16[128,128]{0,1:T(8,128)(2,1)S(1)} collective-permute-done((bf16[128,128]{0,1:T(8,128)(2,1)S(1)}, bf16[128,128]{0,1:T(8,128)(2,1)S(1)}, u32[]{:S(2)}, u32[]{:S(2)}) %collective-permute-start.3) | collective-permute-done | bytes 32800 | tf_op jit(solution)/shard_map/ppermute | solution.py:21
  58.1 0.8 dynamic_update_slice.37
  59.7 4.8 %collective-permute-start.4 = (bf16[128,128]{0,1:T(8,128)(2,1)S(1)}, bf16[128,128]{0,1:T(8,128)(2,1)S(1)}, u32[]{:S(2)}, u32[]{:S(2)}) collective-permute-start(bf16[128,128]{0,1:T(8,128)(2,1)S(1)} %pad_maximum_fusion.11), channel_id=1, source_target_pairs={{0,1},{1,2},{2,3},{4,5},{5,6},{6,7},{8,9},{9,10},{10,11},{12,13},{... | collective-permute-start | bytes 98312 | tf_op jit(solution)/shard_map/ppermute | solution.py:18
  64.6 1.3 collective-permute-start.5
  66.1 4.3 %collective-permute-done.5 = bf16[128,128]{0,1:T(8,128)(2,1)S(1)} collective-permute-done((bf16[128,128]{0,1:T(8,128)(2,1)S(1)}, bf16[128,128]{0,1:T(8,128)(2,1)S(1)}, u32[]{:S(2)}, u32[]{:S(2)}) %collective-permute-start.5) | collective-permute-done | bytes 32800 | tf_op jit(solution)/shard_map/ppermute | solution.py:21
  71.4 0.8 dynamic_update_slice.39
  72.3 0.7 fusion.69
  73.2 14.1 %all_gather.10 = bf16[128,128]{1,0:T(8,128)(2,1)S(1)} all-gather(bf16[16,128]{1,0:T(8,128)(2,1)S(1)} %fusion.7), channel_id=1, replica_groups=mesh['grp'=8,'sub'=4] {'grp'}, dimensions={0}, use_global_device_ids=true | all-gather | bytes 36864 | tf_op jit(solution)/shard_map/all_gather | solution.py:99
  87.5 14.8 %all-reduce.1 = bf16[64,128]{0,1:T(8,128)(2,1)S(1)} all-reduce(bf16[64,128]{0,1:T(8,128)(2,1)S(1)} %fusion.4), channel_id=3, replica_groups=mesh['grp'=8,'sub'=4] {'sub'}, use_global_device_ids=true, to_apply=%region_1.0.clone | all-reduce | flops 8192 | bytes 32768
  103.2 2.8 %collective-permute-start.6 = (bf16[128,128]{0,1:T(8,128)(2,1)S(1)}, bf16[128,128]{0,1:T(8,128)(2,1)S(1)}, u32[]{:S(2)}, u32[]{:S(2)}) collective-permute-start(bf16[128,128]{0,1:T(8,128)(2,1)S(1)} %pad_maximum_fusion.13), channel_id=1, source_target_pairs={{0,1},{1,2},{2,3},{4,5},{5,6},{6,7},{8,9},{9,10},{10,11},{12,13},{... | collective-permute-start | bytes 98312 | tf_op jit(solution)/shard_map/ppermute | solution.py:18
  106.2 1.3 collective-permute-start.7
  107.7 4.3 %collective-permute-done.7 = bf16[128,128]{0,1:T(8,128)(2,1)S(1)} collective-permute-done((bf16[128,128]{0,1:T(8,128)(2,1)S(1)}, bf16[128,128]{0,1:T(8,128)(2,1)S(1)}, u32[]{:S(2)}, u32[]{:S(2)}) %collective-permute-start.7) | collective-permute-done | bytes 32800 | tf_op jit(solution)/shard_map/ppermute | solution.py:21
  112.9 0.7 fusion.34
  113.7 0.8 dynamic_update_slice.41
  114.5 0.8 copy-done.6
  115.3 0.7 fusion.68
  116.7 4.8 %collective-permute-start.8 = (bf16[128,128]{0,1:T(8,128)(2,1)S(1)}, bf16[128,128]{0,1:T(8,128)(2,1)S(1)}, u32[]{:S(2)}, u32[]{:S(2)}) collective-permute-start(bf16[128,128]{0,1:T(8,128)(2,1)S(1)} %pad_maximum_fusion.15), channel_id=1, source_target_pairs={{0,1},{1,2},{2,3},{4,5},{5,6},{6,7},{8,9},{9,10},{10,11},{12,13},{... | collective-permute-start | bytes 98312 | tf_op jit(solution)/shard_map/ppermute | solution.py:18
  121.5 1.3 collective-permute-start.9
  123.0 4.3 %collective-permute-done.9 = bf16[128,128]{0,1:T(8,128)(2,1)S(1)} collective-permute-done((bf16[128,128]{0,1:T(8,128)(2,1)S(1)}, bf16[128,128]{0,1:T(8,128)(2,1)S(1)}, u32[]{:S(2)}, u32[]{:S(2)}) %collective-permute-start.9) | collective-permute-done | bytes 32800 | tf_op jit(solution)/shard_map/ppermute | solution.py:21
  127.3 0.8 concatenate.142
  128.1 0.9 convert_element_type.99
  129.0 0.7 slice_add_fusion.9
  129.8 1.2 dynamic_update_slice.42
  131.0 0.8 fusion.32
  131.8 1.4 dynamic_update_slice.43
  133.3 0.7 copy-done.3
  135.0 14.1 %all_gather.11 = bf16[128,128]{1,0:T(8,128)(2,1)S(1)} all-gather(bf16[16,128]{1,0:T(8,128)(2,1)S(1)} %fusion.8), channel_id=1, replica_groups=mesh['grp'=8,'sub'=4] {'grp'}, dimensions={0}, use_global_device_ids=true | all-gather | bytes 36864 | tf_op jit(solution)/shard_map/all_gather | solution.py:99
  149.3 14.8 %all-reduce.2 = bf16[64,128]{0,1:T(8,128)(2,1)S(1)} all-reduce(bf16[64,128]{0,1:T(8,128)(2,1)S(1)} %fusion.5), channel_id=4, replica_groups=mesh['grp'=8,'sub'=4] {'sub'}, use_global_device_ids=true, to_apply=%region_2.0.clone | all-reduce | flops 8192 | bytes 32768
  165.0 2.9 %collective-permute-start.10 = (bf16[128,128]{0,1:T(8,128)(2,1)S(1)}, bf16[128,128]{0,1:T(8,128)(2,1)S(1)}, u32[]{:S(2)}, u32[]{:S(2)}) collective-permute-start(bf16[128,128]{0,1:T(8,128)(2,1)S(1)} %pad_maximum_fusion.17), channel_id=1, source_target_pairs={{0,1},{1,2},{2,3},{4,5},{5,6},{6,7},{8,9},{9,10},{10,11},{12,13},{... | collective-permute-start | bytes 98312 | tf_op jit(solution)/shard_map/ppermute | solution.py:18
  168.0 1.3 collective-permute-start.11
  169.4 4.3 %collective-permute-done.11 = bf16[128,128]{0,1:T(8,128)(2,1)S(1)} collective-permute-done((bf16[128,128]{0,1:T(8,128)(2,1)S(1)}, bf16[128,128]{0,1:T(8,128)(2,1)S(1)}, u32[]{:S(2)}, u32[]{:S(2)}) %collective-permute-start.11) | collective-permute-done | bytes 32800 | tf_op jit(solution)/shard_map/ppermute | solution.py:21
  174.8 0.8 dynamic_update_slice.45
  175.8 0.7 copy-done.2
  177.3 4.8 %collective-permute-start.12 = (bf16[128,128]{0,1:T(8,128)(2,1)S(1)}, bf16[128,128]{0,1:T(8,128)(2,1)S(1)}, u32[]{:S(2)}, u32[]{:S(2)}) collective-permute-start(bf16[128,128]{0,1:T(8,128)(2,1)S(1)} %pad_maximum_fusion.19), channel_id=1, source_target_pairs={{0,1},{1,2},{2,3},{4,5},{5,6},{6,7},{8,9},{9,10},{10,11},{12,13},{... | collective-permute-start | bytes 98312 | tf_op jit(solution)/shard_map/ppermute | solution.py:18
  182.1 1.3 collective-permute-start.13
  183.4 0.8 copy.13
  184.3 3.6 %collective-permute-done.13 = bf16[128,128]{0,1:T(8,128)(2,1)S(1)} collective-permute-done((bf16[128,128]{0,1:T(8,128)(2,1)S(1)}, bf16[128,128]{0,1:T(8,128)(2,1)S(1)}, u32[]{:S(2)}, u32[]{:S(2)}) %collective-permute-start.13) | collective-permute-done | bytes 32800 | tf_op jit(solution)/shard_map/ppermute | solution.py:21
  188.9 0.8 dynamic_update_slice.47
  189.9 0.8 copy.14
  (121 shorter events, 14.1 us)
Async XLA Ops:
  0.6 58.3 %copy-start = (bf16[1,1,640,640]{3,2,1,0:T(8,128)(2,1)S(1)}, bf16[1,1,640,640]{3,2,1,0:T(8,128)(2,1)}, u32[]{:S(2)}) copy-start(bf16[1,1,640,640]{3,2,1,0:T(8,128)(2,1)} %param.10) | copy-start | bytes 2457604
  3.9 103.6 %copy-start.10 = (f32[512]{0:T(512)}, f32[512]{0:T(512)S(1)}, u32[]{:S(2)}) copy-start(f32[512]{0:T(512)S(1)} %fusion.54) | copy-start | bytes 6148
  5.0 6.5 %copy-start.13 = (u32[32]{0:T(128)S(1)}, u32[32]{0:T(128)}, u32[]{:S(2)}) copy-start(u32[32]{0:T(128)} %constant.31) | copy-start | bytes 388
  5.1 11.2 %copy-start.7 = (bf16[1,1,640,16]{2,3,1,0:T(8,128)(2,1)S(1)}, bf16[1,1,640,16]{2,3,1,0:T(8,128)(2,1)}, u32[]{:S(2)}) copy-start(bf16[1,1,640,16]{2,3,1,0:T(8,128)(2,1)} %param.12) | copy-start | bytes 61444
  5.1 42.5 %copy-start.1 = (bf16[1,1,640,640]{3,2,1,0:T(8,128)(2,1)S(1)}, bf16[1,1,640,640]{3,2,1,0:T(8,128)(2,1)}, u32[]{:S(2)}) copy-start(bf16[1,1,640,640]{3,2,1,0:T(8,128)(2,1)} %param.11) | copy-start | bytes 2457604
  5.2 7.6 %collective-permute-start = (bf16[64,128]{0,1:T(8,128)(2,1)S(1)}, bf16[64,128]{0,1:T(8,128)(2,1)S(1)}, u32[]{:S(2)}, u32[]{:S(2)}) collective-permute-start(bf16[64,128]{0,1:T(8,128)(2,1)S(1)} %get-tuple-element.43), channel_id=1, source_target_pairs={{0,1},{1,2},{2,3},{4,5},{5,6},{6,7},{8,9},{9,10},{10,11},{12,13},{... | collective-permute-start | bytes 49160 | tf_op jit(solution)/shard_map/ppermute | solution.py:18
  10.2 5.8 %collective-permute-start.1 = (bf16[64,128]{0,1:T(8,128)(2,1)S(1)}, bf16[64,128]{0,1:T(8,128)(2,1)S(1)}, u32[]{:S(2)}, u32[]{:S(2)}) collective-permute-start(bf16[64,128]{0,1:T(8,128)(2,1)S(1)} %get-tuple-element.44), channel_id=1, source_target_pairs={{1,0},{2,1},{3,2},{5,4},{6,5},{7,6},{9,8},{10,9},{11,10},{13,12},{... | collective-permute-start | bytes 49160 | tf_op jit(solution)/shard_map/ppermute | solution.py:21
  16.4 14.5 %copy-start.9 = (bf16[64,128]{1,0:T(8,128)(2,1)S(1)}, bf16[64,128]{1,0:T(8,128)(2,1)}, u32[]{:S(2)}) copy-start(bf16[64,128]{1,0:T(8,128)(2,1)} %param.13) | copy-start | bytes 49156
  48.3 3.2 %collective-permute-start.2 = (bf16[128,128]{0,1:T(8,128)(2,1)S(1)}, bf16[128,128]{0,1:T(8,128)(2,1)S(1)}, u32[]{:S(2)}, u32[]{:S(2)}) collective-permute-start(bf16[128,128]{0,1:T(8,128)(2,1)S(1)} %pad_maximum_fusion.9), channel_id=1, source_target_pairs={{0,1},{1,2},{2,3},{4,5},{5,6},{6,7},{8,9},{9,10},{10,11},{12,13},{... | collective-permute-start | bytes 98312 | tf_op jit(solution)/shard_map/ppermute | solution.py:18
  50.1 6.9 %collective-permute-start.3 = (bf16[128,128]{0,1:T(8,128)(2,1)S(1)}, bf16[128,128]{0,1:T(8,128)(2,1)S(1)}, u32[]{:S(2)}, u32[]{:S(2)}) collective-permute-start(bf16[128,128]{0,1:T(8,128)(2,1)S(1)} %pad_maximum_fusion.10), channel_id=1, source_target_pairs={{1,0},{2,1},{3,2},{5,4},{6,5},{7,6},{9,8},{10,9},{11,10},{13,12},{... | collective-permute-start | bytes 98312 | tf_op jit(solution)/shard_map/ppermute | solution.py:21
  59.7 6.4 %collective-permute-start.4 = (bf16[128,128]{0,1:T(8,128)(2,1)S(1)}, bf16[128,128]{0,1:T(8,128)(2,1)S(1)}, u32[]{:S(2)}, u32[]{:S(2)}) collective-permute-start(bf16[128,128]{0,1:T(8,128)(2,1)S(1)} %pad_maximum_fusion.11), channel_id=1, source_target_pairs={{0,1},{1,2},{2,3},{4,5},{5,6},{6,7},{8,9},{9,10},{10,11},{12,13},{... | collective-permute-start | bytes 98312 | tf_op jit(solution)/shard_map/ppermute | solution.py:18
  64.6 5.8 %collective-permute-start.5 = (bf16[128,128]{0,1:T(8,128)(2,1)S(1)}, bf16[128,128]{0,1:T(8,128)(2,1)S(1)}, u32[]{:S(2)}, u32[]{:S(2)}) collective-permute-start(bf16[128,128]{0,1:T(8,128)(2,1)S(1)} %pad_maximum_fusion.12), channel_id=1, source_target_pairs={{1,0},{2,1},{3,2},{5,4},{6,5},{7,6},{9,8},{10,9},{11,10},{13,12},{... | collective-permute-start | bytes 98312 | tf_op jit(solution)/shard_map/ppermute | solution.py:21
  103.2 4.4 %collective-permute-start.6 = (bf16[128,128]{0,1:T(8,128)(2,1)S(1)}, bf16[128,128]{0,1:T(8,128)(2,1)S(1)}, u32[]{:S(2)}, u32[]{:S(2)}) collective-permute-start(bf16[128,128]{0,1:T(8,128)(2,1)S(1)} %pad_maximum_fusion.13), channel_id=1, source_target_pairs={{0,1},{1,2},{2,3},{4,5},{5,6},{6,7},{8,9},{9,10},{10,11},{12,13},{... | collective-permute-start | bytes 98312 | tf_op jit(solution)/shard_map/ppermute | solution.py:18
  106.2 5.8 %collective-permute-start.7 = (bf16[128,128]{0,1:T(8,128)(2,1)S(1)}, bf16[128,128]{0,1:T(8,128)(2,1)S(1)}, u32[]{:S(2)}, u32[]{:S(2)}) collective-permute-start(bf16[128,128]{0,1:T(8,128)(2,1)S(1)} %pad_maximum_fusion.14), channel_id=1, source_target_pairs={{1,0},{2,1},{3,2},{5,4},{6,5},{7,6},{9,8},{10,9},{11,10},{13,12},{... | collective-permute-start | bytes 98312 | tf_op jit(solution)/shard_map/ppermute | solution.py:21
  114.4 0.8 copy-start.6
  116.7 6.3 %collective-permute-start.8 = (bf16[128,128]{0,1:T(8,128)(2,1)S(1)}, bf16[128,128]{0,1:T(8,128)(2,1)S(1)}, u32[]{:S(2)}, u32[]{:S(2)}) collective-permute-start(bf16[128,128]{0,1:T(8,128)(2,1)S(1)} %pad_maximum_fusion.15), channel_id=1, source_target_pairs={{0,1},{1,2},{2,3},{4,5},{5,6},{6,7},{8,9},{9,10},{10,11},{12,13},{... | collective-permute-start | bytes 98312 | tf_op jit(solution)/shard_map/ppermute | solution.py:18
  121.4 1.4 copy-start.11
  121.5 5.8 %collective-permute-start.9 = (bf16[128,128]{0,1:T(8,128)(2,1)S(1)}, bf16[128,128]{0,1:T(8,128)(2,1)S(1)}, u32[]{:S(2)}, u32[]{:S(2)}) collective-permute-start(bf16[128,128]{0,1:T(8,128)(2,1)S(1)} %pad_maximum_fusion.16), channel_id=1, source_target_pairs={{1,0},{2,1},{3,2},{5,4},{6,5},{7,6},{9,8},{10,9},{11,10},{13,12},{... | collective-permute-start | bytes 98312 | tf_op jit(solution)/shard_map/ppermute | solution.py:21
  133.2 0.8 copy-start.3
  133.2 0.9 copy-start.4
  133.2 0.9 copy-start.5
  134.1 0.7 copy-start.8
  165.0 4.4 %collective-permute-start.10 = (bf16[128,128]{0,1:T(8,128)(2,1)S(1)}, bf16[128,128]{0,1:T(8,128)(2,1)S(1)}, u32[]{:S(2)}, u32[]{:S(2)}) collective-permute-start(bf16[128,128]{0,1:T(8,128)(2,1)S(1)} %pad_maximum_fusion.17), channel_id=1, source_target_pairs={{0,1},{1,2},{2,3},{4,5},{5,6},{6,7},{8,9},{9,10},{10,11},{12,13},{... | collective-permute-start | bytes 98312 | tf_op jit(solution)/shard_map/ppermute | solution.py:18
  167.9 1.4 copy-start.12
  168.0 5.8 %collective-permute-start.11 = (bf16[128,128]{0,1:T(8,128)(2,1)S(1)}, bf16[128,128]{0,1:T(8,128)(2,1)S(1)}, u32[]{:S(2)}, u32[]{:S(2)}) collective-permute-start(bf16[128,128]{0,1:T(8,128)(2,1)S(1)} %pad_maximum_fusion.18), channel_id=1, source_target_pairs={{1,0},{2,1},{3,2},{5,4},{6,5},{7,6},{9,8},{10,9},{11,10},{13,12},{... | collective-permute-start | bytes 98312 | tf_op jit(solution)/shard_map/ppermute | solution.py:21
  175.7 0.8 copy-start.2
  177.3 7.0 %collective-permute-start.12 = (bf16[128,128]{0,1:T(8,128)(2,1)S(1)}, bf16[128,128]{0,1:T(8,128)(2,1)S(1)}, u32[]{:S(2)}, u32[]{:S(2)}) collective-permute-start(bf16[128,128]{0,1:T(8,128)(2,1)S(1)} %pad_maximum_fusion.19), channel_id=1, source_target_pairs={{0,1},{1,2},{2,3},{4,5},{5,6},{6,7},{8,9},{9,10},{10,11},{12,13},{... | collective-permute-start | bytes 98312 | tf_op jit(solution)/shard_map/ppermute | solution.py:18
  182.1 5.8 %collective-permute-start.13 = (bf16[128,128]{0,1:T(8,128)(2,1)S(1)}, bf16[128,128]{0,1:T(8,128)(2,1)S(1)}, u32[]{:S(2)}, u32[]{:S(2)}) collective-permute-start(bf16[128,128]{0,1:T(8,128)(2,1)S(1)} %pad_maximum_fusion.20), channel_id=1, source_target_pairs={{1,0},{2,1},{3,2},{5,4},{6,5},{7,6},{9,8},{10,9},{11,10},{13,12},{... | collective-permute-start | bytes 98312 | tf_op jit(solution)/shard_map/ppermute | solution.py:21
where the time goes:
time: 191 us
  blocking collectives  88.7 us (46%)
  starting transfers between devices  35.7 us (19%)
  waiting for transfers between devices  30.3 us (16%)
  local copies, waits for them, and re-layouts  20.4 us (11%)
  other arithmetic  7.52 us (4%)
  between operations  4.11 us (2%)
  matrix products  3.98 us (2%)
    unnamed x3, blocking collectives  45.9 us
    all_gather x3, blocking collectives, body(): column = lax.all_gather(coarse_resid, 'grp', axis=0, tiled=True)  42.8 us
    ppermute x7, waiting for transfers between devices, with_halo(): lax.ppermute(lax.slice_in_dim(block, 0, width, axis=dim), axis, backward)  29.6 us
    ppermute x7, starting transfers between devices, with_halo(): lax.ppermute(lax.slice_in_dim(block, block.shape[dim] - width, None, axis...  26.7 us
    dynamic_update_slice x12, local copies, waits for them, and re-layouts, add_block(): lax.dynamic_update_slice_in_dim(vector, current + addend, first_row, 0)  10 us
    ppermute x7, starting transfers between devices, with_halo(): lax.ppermute(lax.slice_in_dim(block, 0, width, axis=dim), axis, backward)  9.04 us
    unnamed x32, local copies, waits for them, and re-layouts  6.34 us
  transfers between devices with their start and end apart: 14, of which 12 were waited for; matrix products, arithmetic and copies ran while one was open for 1% of the time, Pallas kernels for 0%

commit v1 on v0

v1 whole, which is shorter than its diff:
```python
import jax
import jax.numpy as jnp
from jax import lax
from jax.sharding import PartitionSpec as P

ITERS = 3


STEP_SIZES = (0.8, 0.9, 1.0)
MOMENTUM = (0.0, 0.3, 0.3)


def body(
    right_side, live_rows, margin_blocks, local_operator, local_inverse, deflation, coarse_inverse
):
    bf16 = jnp.bfloat16
    f32 = jnp.float32
    source = right_side[0, 0]
    owned, loads = source.shape
    operator = local_operator[0, 0]
    inverse = local_inverse[0, 0]
    vectors = deflation[0, 0]
    order, modes = vectors.shape
    blk = (order - owned) // 2
    blocks = owned // blk
    groups = lax.axis_size("grp")
    subs = lax.axis_size("sub")
    position = lax.axis_index("sub")
    has_left = position > 0
    has_right = position < subs - 1
    mask = jnp.arange(owned, dtype=jnp.int32)[:, None] < live_rows[0, 0]
    give_right = margin_blocks[0, 0, 0]
    give_left = margin_blocks[0, 0, 1]
    forward = [(i, (i + 1) % subs) for i in range(subs)]
    backward = [(target, origin) for origin, target in forward]

    def lent(rows, index):
        return lax.dynamic_slice_in_dim(rows, index * blk, blk, 0)

    ids = jnp.arange(blocks, dtype=jnp.int32)[:, None, None]

    def add_lent(owned_part, from_left, from_right):
        tall = owned_part.reshape(blocks, blk, loads)
        tall = tall + jnp.where(ids == give_left, from_left[None], 0.0)
        tall = tall + jnp.where(ids == give_right, from_right[None], 0.0)
        return tall.reshape(owned, loads)

    def swap(rows):
        to_right = jnp.concatenate([rows[owned + blk :], lent(rows, give_right)], axis=0)
        to_left = jnp.concatenate([rows[owned : owned + blk], lent(rows, give_left)], axis=0)
        return (
            lax.ppermute(to_right.astype(bf16), "sub", forward),
            lax.ppermute(to_left.astype(bf16), "sub", backward),
        )

    def joined(rows, from_left, from_right):
        own = add_lent(jnp.where(mask, rows[:owned], 0.0), from_left[:blk], from_right[:blk])
        left = jnp.where(has_left, rows[owned : owned + blk] + from_left[blk:], 0.0)
        right = jnp.where(has_right, rows[owned + blk :] + from_right[blk:], 0.0)
        return jnp.concatenate([own, left, right], axis=0)

    residual = jnp.where(mask, source, 0.0)
    near = min(subs, 3)
    starts = [min(max(k - 1, 0), subs - near) for k in range(subs)]
    columns = coarse_inverse.shape[1]
    wide = near * modes * columns // loads
    panels = [
        coarse_inverse[first * modes : (first + near) * modes].reshape(wide, loads)
        for first in starts
    ]
    to_right = jnp.concatenate(
        [
            vectors[owned + blk :].T,
            lent(vectors, give_right).T,
        ],
        axis=1,
    )
    to_left = jnp.concatenate(
        [
            vectors[owned : owned + blk].T,
            lent(vectors, give_left).T,
        ],
        axis=1,
    )
    ahead = jnp.concatenate([to_right, lent(residual, give_right).astype(bf16)], axis=0)
    behind = jnp.concatenate([to_left, lent(residual, give_left).astype(bf16)], axis=0)
    slots = jnp.arange(subs, dtype=jnp.int32)[:, None, None]
    slots = jnp.where(slots > position, ahead[None], behind[None])
    slots = jnp.concatenate([jnp.stack(panels), slots], axis=1)
    slots = lax.all_to_all(slots, "sub", 0, 0, tiled=True)
    coarse = slots[:, :wide].reshape(subs, near * modes, columns)
    base = jnp.clip(position - 1, 0, subs - near)
    left_slot = jnp.where(
        has_left, lax.dynamic_index_in_dim(slots, jnp.maximum(position - 1, 0), 0, False), 0
    )
    right_slot = jnp.where(
        has_right, lax.dynamic_index_in_dim(slots, jnp.minimum(position + 1, subs - 1), 0, False), 0
    )
    left_vectors = left_slot[wide : wide + modes].T
    right_vectors = right_slot[wide : wide + modes].T
    residual = jnp.concatenate(
        [residual, left_slot[wide + modes :].astype(f32), right_slot[wide + modes :].astype(f32)],
        axis=0,
    )
    solution = jnp.zeros_like(source)
    direction = 0.0
    for turn in range(ITERS):
        local_resid = residual.astype(bf16)
        fine = jnp.dot(inverse, local_resid, preferred_element_type=f32)
        coarse_resid = lax.dot_general(
            vectors, local_resid, (((0,), (0,)), ((), ())), preferred_element_type=f32
        ).astype(bf16)
        from_left, from_right = swap(fine)
        every = jnp.broadcast_to(coarse_resid[None], (subs * groups, modes, loads))
        every = lax.all_to_all(every, ("sub", "grp"), 0, 0, tiled=True).reshape(
            subs, groups * modes, loads
        )
        corrections = sum(
            jnp.dot(coarse[k], every[k], preferred_element_type=f32) for k in range(subs)
        ).astype(bf16)

        def correction(offset):
            row = jnp.clip(position + offset - base, 0, near - 1) * modes
            return lax.dynamic_slice_in_dim(corrections, row, modes, 0)

        update = joined(
            fine + jnp.dot(vectors, correction(0), preferred_element_type=f32),
            jnp.where(has_left, from_left.astype(f32), 0.0)
            + jnp.dot(left_vectors, correction(-1), preferred_element_type=f32),
            jnp.where(has_right, from_right.astype(f32), 0.0)
            + jnp.dot(right_vectors, correction(1), preferred_element_type=f32),
        )
        direction = update + MOMENTUM[turn] * direction
        solution = solution + STEP_SIZES[turn] * direction[:owned]
        applied = jnp.dot(operator, direction.astype(bf16), preferred_element_type=f32)
        from_left, from_right = swap(applied)
        applied = joined(
            applied,
            jnp.where(has_left, from_left.astype(f32), 0.0),
            jnp.where(has_right, from_right.astype(f32), 0.0),
        )
        residual = residual - STEP_SIZES[turn] * applied
    return (solution[None, None], residual[None, None, :owned])


def solution(mesh):
    return jax.shard_map(
        body,
        mesh=mesh,
        in_specs=(
            P("grp", "sub", None, None),
            P("grp", "sub"),
            P("grp", "sub", None),
            P("grp", "sub", None, None),
            P("grp", "sub", None, None),
            P("grp", "sub", None, None),
            P("grp", "sub"),
        ),
        out_specs=(P("grp", "sub", None, None), P("grp", "sub", None, None)),
        check_vma=False,
    )
```

time: 191 us -> 99.8 us (0.52)
  blocking collectives: 88.7 us -> 0 us
  starting transfers between devices: 35.7 us -> 29.1 us
  matrix products: 3.98 us -> 7.09 us
    unnamed x3 -> x0, blocking collectives: 45.9 us -> none
    all_gather x3 -> x0, blocking collectives: 42.8 us -> none  [body(): column = lax.all_gather(coarse_resid, 'grp', axis=0, tiled=True)]
    ppermute x14 -> x12, starting transfers between devices: 35.7 us -> 14.5 us  [the longest x6 11 us: swap(): lax.ppermute(to_left.astype(bf16), 'sub', backward)]
    ppermute x14 -> x12, waiting for transfers between devices: 30.3 us -> 11.2 us  [the longest x6 6.07 us: swap(): lax.ppermute(to_right.astype(bf16), 'sub', forward)]
    all_to_all x0 -> x4, waiting for transfers between devices: none -> 18.2 us  [the longest x3 14.7 us: body(): lax.all_to_all(every, ('sub', 'grp'), 0, 0, tiled=True)]
    all_to_all x0 -> x4, starting transfers between devices: none -> 14.7 us  [the longest x3 9.47 us: body(): lax.all_to_all(every, ('sub', 'grp'), 0, 0, tiled=True)]
    dynamic_update_slice x12 -> x0, local copies, waits for them, and re-layouts: 10 us -> none  [add_block(): lax.dynamic_update_slice_in_dim(vector, current + addend, first_row, 0)]
    broadcast_in_dim x0 -> x31, local copies, waits for them, and re-layouts: none -> 8.37 us  [the longest x14 5.1 us: add_lent(): tall = tall + jnp.where(ids == give_right, from_right[None], 0.0)]
  transfers between devices with their start and end apart: 14 -> 16, of which waited for: 12 -> 10; matrix products, arithmetic and copies ran while one was open for 1% -> 8% of each run, Pallas kernels for 0% -> 0%
where the time goes in v1:
time: 99.8 us; the launch traced here: 98.6 us
  waiting for transfers between devices  29.4 us (29%)
  starting transfers between devices  29.1 us (29%)
  local copies, waits for them, and re-layouts  21.7 us (22%)
  other arithmetic  7.82 us (8%)
  matrix products  7.09 us (7%)
  between operations  3.53 us (4%)
    all_to_all x3, waiting for transfers between devices, body(): lax.all_to_all(every, ('sub', 'grp'), 0, 0, tiled=True)  14.7 us
    ppermute x6, starting transfers between devices, swap(): lax.ppermute(to_left.astype(bf16), 'sub', backward)  11 us
    unnamed x61, local copies, waits for them, and re-layouts  9.68 us
    all_to_all x3, starting transfers between devices, body(): lax.all_to_all(every, ('sub', 'grp'), 0, 0, tiled=True)  9.47 us
    ppermute x6, waiting for transfers between devices, swap(): lax.ppermute(to_right.astype(bf16), 'sub', forward)  6.07 us
    all_to_all x1, starting transfers between devices, body(): slots = lax.all_to_all(slots, 'sub', 0, 0, tiled=True)  5.19 us
    ppermute x6, waiting for transfers between devices, swap(): lax.ppermute(to_left.astype(bf16), 'sub', backward)  5.13 us
    broadcast_in_dim x14, local copies, waits for them, and re-layouts, add_lent(): tall = tall + jnp.where(ids == give_right, from_right[None], 0.0)  5.1 us
  transfers between devices with their start and end apart: 16, of which 10 were waited for; matrix products, arithmetic and copies ran while one was open for 8% of the time, Pallas kernels for 0%

profile of v1, /device:TPU:0, one launch (start us, length us, event | category | flops | bytes accessed | tf_op | source)
XLA Modules:
  0.0 98.6 jit_solution(18344991514839777503)
XLA Ops:
  0.7 0.7 copy-done.28
  3.9 0.7 copy-done.8
  5.7 0.8 pad_maximum_fusion.4
  6.5 5.2 %all-to-all-start = ((bf16[4,128,128]{1,2,0:T(8,128)(2,1)}), bf16[4,128,128]{1,2,0:T(8,128)(2,1)S(1)}, u32[]{:S(2)}, u32[]{:S(2)}) async-start(bf16[4,128,128]{1,2,0:T(8,128)(2,1)} %pad_maximum_fusion.4), calls=%async_computation | async-start | bytes 262144 | tf_op jit(solution)/shard_map/all_to_all | solution.py:90
  11.7 0.6 iota_compare_fusion.1
  13.3 3.5 %all-to-all-done = bf16[4,128,128]{1,2,0:T(8,128)(2,1)S(1)} async-done(((bf16[4,128,128]{1,2,0:T(8,128)(2,1)}), bf16[4,128,128]{1,2,0:T(8,128)(2,1)S(1)}, u32[]{:S(2)}, u32[]{:S(2)}) %all-to-all-start) | async-done | bytes 131104 | tf_op jit(solution)/shard_map/all_to_all | solution.py:90
  17.1 0.7 broadcast_in_dim.293
  17.8 4.3 %all-to-all-start.1 = ((bf16[32,16,128]{2,1,0:T(8,128)(2,1)}), bf16[32,16,128]{2,1,0:T(8,128)(2,1)S(1)}, u32[]{:S(2)}, u32[]{:S(2)}) async-start(bf16[32,16,128]{2,1,0:T(8,128)(2,1)} %broadcast_in_dim.293), calls=%async_computation.1 | async-start | bytes 262144 | tf_op jit(solution)/shard_map/all_to_all | solution.py:115
  22.9 2.7 %collective-permute-start.1 = (bf16[128,128]{0,1:T(8,128)(2,1)S(1)}, bf16[128,128]{0,1:T(8,128)(2,1)S(1)}, u32[]{:S(2)}, u32[]{:S(2)}) collective-permute-start(bf16[128,128]{0,1:T(8,128)(2,1)S(1)} %pad_maximum_fusion.9), channel_id=1, source_target_pairs={{1,0},{2,1},{3,2},{0,3},{5,4},{6,5},{7,6},{4,7},{9,8},{10,9},{11,1... | collective-permute-start | bytes 98312 | tf_op jit(solution)/shard_map/ppermute | solution.py:53
  25.8 4.5 %all-to-all-done.1 = bf16[32,16,128]{2,1,0:T(8,128)(2,1)S(1)} async-done(((bf16[32,16,128]{2,1,0:T(8,128)(2,1)}), bf16[32,16,128]{2,1,0:T(8,128)(2,1)S(1)}, u32[]{:S(2)}, u32[]{:S(2)}) %all-to-all-start.1) | async-done | bytes 131104 | tf_op jit(solution)/shard_map/all_to_all | solution.py:115
  32.6 0.9 copy-done.1
  34.2 1.0 %collective-permute-start.3 = (bf16[128,128]{0,1:T(8,128)(2,1)S(1)}, bf16[128,128]{0,1:T(8,128)(2,1)S(1)}, u32[]{:S(2)}, u32[]{:S(2)}) collective-permute-start(bf16[128,128]{0,1:T(8,128)(2,1)S(1)} %pad_maximum_fusion.11), channel_id=1, source_target_pairs={{1,0},{2,1},{3,2},{0,3},{5,4},{6,5},{7,6},{4,7},{9,8},{10,9},{11,1... | collective-permute-start | bytes 98312 | tf_op jit(solution)/shard_map/ppermute | solution.py:53
  35.3 1.1 %collective-permute-start.2 = (bf16[128,128]{0,1:T(8,128)(2,1)S(1)}, bf16[128,128]{0,1:T(8,128)(2,1)S(1)}, u32[]{:S(2)}, u32[]{:S(2)}) collective-permute-start(bf16[128,128]{0,1:T(8,128)(2,1)S(1)} %pad_maximum_fusion.10), channel_id=1, source_target_pairs={{0,1},{1,2},{2,3},{3,0},{4,5},{5,6},{6,7},{7,4},{8,9},{9,10},{10,1... | collective-permute-start | bytes 98312 | tf_op jit(solution)/shard_map/ppermute | solution.py:52
  36.4 2.1 %collective-permute-done.3 = bf16[128,128]{0,1:T(8,128)(2,1)S(1)} collective-permute-done((bf16[128,128]{0,1:T(8,128)(2,1)S(1)}, bf16[128,128]{0,1:T(8,128)(2,1)S(1)}, u32[]{:S(2)}, u32[]{:S(2)}) %collective-permute-start.3) | collective-permute-done | bytes 32800 | tf_op jit(solution)/shard_map/ppermute | solution.py:53
  38.5 1.6 %collective-permute-done.2 = bf16[128,128]{0,1:T(8,128)(2,1)S(1)} collective-permute-done((bf16[128,128]{0,1:T(8,128)(2,1)S(1)}, bf16[128,128]{0,1:T(8,128)(2,1)S(1)}, u32[]{:S(2)}, u32[]{:S(2)}) %collective-permute-start.2) | collective-permute-done | bytes 32800 | tf_op jit(solution)/shard_map/ppermute | solution.py:52
  40.1 0.8 fusion.56
  41.5 0.7 copy-done.16
  42.5 0.6 copy-done.9
  43.6 0.7 broadcast_in_dim.310
  44.3 2.6 %all-to-all-start.2 = ((bf16[32,16,128]{2,1,0:T(8,128)(2,1)}), bf16[32,16,128]{2,1,0:T(8,128)(2,1)S(1)}, u32[]{:S(2)}, u32[]{:S(2)}) async-start(bf16[32,16,128]{2,1,0:T(8,128)(2,1)} %broadcast_in_dim.310), calls=%async_computation.2 | async-start | bytes 262144 | tf_op jit(solution)/shard_map/all_to_all | solution.py:115
  47.2 2.6 %collective-permute-start.5 = (bf16[128,128]{0,1:T(8,128)(2,1)S(1)}, bf16[128,128]{0,1:T(8,128)(2,1)S(1)}, u32[]{:S(2)}, u32[]{:S(2)}) collective-permute-start(bf16[128,128]{0,1:T(8,128)(2,1)S(1)} %pad_maximum_fusion.13), channel_id=1, source_target_pairs={{1,0},{2,1},{3,2},{0,3},{5,4},{6,5},{7,6},{4,7},{9,8},{10,9},{11,1... | collective-permute-start | bytes 98312 | tf_op jit(solution)/shard_map/ppermute | solution.py:53
  49.9 5.1 %all-to-all-done.2 = bf16[32,16,128]{2,1,0:T(8,128)(2,1)S(1)} async-done(((bf16[32,16,128]{2,1,0:T(8,128)(2,1)}), bf16[32,16,128]{2,1,0:T(8,128)(2,1)S(1)}, u32[]{:S(2)}, u32[]{:S(2)}) %all-to-all-start.2) | async-done | bytes 131104 | tf_op jit(solution)/shard_map/all_to_all | solution.py:115
  57.0 0.8 fusion.54
  58.4 0.7 copy-done.12
  60.0 1.0 %collective-permute-start.7 = (bf16[128,128]{0,1:T(8,128)(2,1)S(1)}, bf16[128,128]{0,1:T(8,128)(2,1)S(1)}, u32[]{:S(2)}, u32[]{:S(2)}) collective-permute-start(bf16[128,128]{0,1:T(8,128)(2,1)S(1)} %pad_maximum_fusion.15), channel_id=1, source_target_pairs={{1,0},{2,1},{3,2},{0,3},{5,4},{6,5},{7,6},{4,7},{9,8},{10,9},{11,1... | collective-permute-start | bytes 98312 | tf_op jit(solution)/shard_map/ppermute | solution.py:53
  61.1 1.1 %collective-permute-start.6 = (bf16[128,128]{0,1:T(8,128)(2,1)S(1)}, bf16[128,128]{0,1:T(8,128)(2,1)S(1)}, u32[]{:S(2)}, u32[]{:S(2)}) collective-permute-start(bf16[128,128]{0,1:T(8,128)(2,1)S(1)} %pad_maximum_fusion.14), channel_id=1, source_target_pairs={{0,1},{1,2},{2,3},{3,0},{4,5},{5,6},{6,7},{7,4},{8,9},{9,10},{10,1... | collective-permute-start | bytes 98312 | tf_op jit(solution)/shard_map/ppermute | solution.py:52
  62.2 2.1 %collective-permute-done.7 = bf16[128,128]{0,1:T(8,128)(2,1)S(1)} collective-permute-done((bf16[128,128]{0,1:T(8,128)(2,1)S(1)}, bf16[128,128]{0,1:T(8,128)(2,1)S(1)}, u32[]{:S(2)}, u32[]{:S(2)}) %collective-permute-start.7) | collective-permute-done | bytes 32800 | tf_op jit(solution)/shard_map/ppermute | solution.py:53
  64.3 1.7 %collective-permute-done.6 = bf16[128,128]{0,1:T(8,128)(2,1)S(1)} collective-permute-done((bf16[128,128]{0,1:T(8,128)(2,1)S(1)}, bf16[128,128]{0,1:T(8,128)(2,1)S(1)}, u32[]{:S(2)}, u32[]{:S(2)}) %collective-permute-start.6) | collective-permute-done | bytes 32800 | tf_op jit(solution)/shard_map/ppermute | solution.py:52
  66.0 0.8 fusion.52
  66.7 0.7 copy.85
  67.7 1.5 %broadcast_in_dim.317 = f32[8,64,128]{2,1,0:T(8,128)} broadcast(f32[64,128]{1,0:T(8,128)} %copy.85), dimensions={1,2} | broadcast | bytes 294912 | tf_op jit(solution)/shard_map/jit(_where)/broadcast_in_dim | solution.py:45
  69.2 1.1 %copy.86 = f32[512,128]{0,1:T(8,128)S(1)} copy(f32[512,128]{1,0:T(8,128)} %bitcast.206) | data formatting | bytes 524288 | tf_op jit(solution)/shard_map/jit(_where)/broadcast_in_dim | solution.py:45
  70.3 0.8 copy-done.23
  71.2 0.6 copy-done.10
  72.4 0.7 broadcast_in_dim.319
  73.1 2.6 %all-to-all-start.3 = ((bf16[32,16,128]{2,1,0:T(8,128)(2,1)}), bf16[32,16,128]{2,1,0:T(8,128)(2,1)S(1)}, u32[]{:S(2)}, u32[]{:S(2)}) async-start(bf16[32,16,128]{2,1,0:T(8,128)(2,1)} %broadcast_in_dim.319), calls=%async_computation.3 | async-start | bytes 262144 | tf_op jit(solution)/shard_map/all_to_all | solution.py:115
  75.9 2.6 %collective-permute-start.9 = (bf16[128,128]{0,1:T(8,128)(2,1)S(1)}, bf16[128,128]{0,1:T(8,128)(2,1)S(1)}, u32[]{:S(2)}, u32[]{:S(2)}) collective-permute-start(bf16[128,128]{0,1:T(8,128)(2,1)S(1)} %pad_maximum_fusion.17), channel_id=1, source_target_pairs={{1,0},{2,1},{3,2},{0,3},{5,4},{6,5},{7,6},{4,7},{9,8},{10,9},{11,1... | collective-permute-start | bytes 98312 | tf_op jit(solution)/shard_map/ppermute | solution.py:53
  78.7 5.1 %all-to-all-done.3 = bf16[32,16,128]{2,1,0:T(8,128)(2,1)S(1)} async-done(((bf16[32,16,128]{2,1,0:T(8,128)(2,1)}), bf16[32,16,128]{2,1,0:T(8,128)(2,1)S(1)}, u32[]{:S(2)}, u32[]{:S(2)}) %all-to-all-start.3) | async-done | bytes 131104 | tf_op jit(solution)/shard_map/all_to_all | solution.py:115
  85.8 0.7 fusion.50
  86.9 0.7 broadcast_in_dim.322
  87.6 1.1 %copy.92 = f32[512,128]{0,1:T(8,128)S(1)} copy(f32[512,128]{1,0:T(8,128)} %bitcast.208) | data formatting | bytes 524288 | tf_op jit(solution)/shard_map/jit(_where)/broadcast_in_dim | solution.py:45
  88.8 0.8 copy-done.25
  90.3 1.0 %collective-permute-start.11 = (bf16[128,128]{0,1:T(8,128)(2,1)S(1)}, bf16[128,128]{0,1:T(8,128)(2,1)S(1)}, u32[]{:S(2)}, u32[]{:S(2)}) collective-permute-start(bf16[128,128]{0,1:T(8,128)(2,1)S(1)} %pad_maximum_fusion.19), channel_id=1, source_target_pairs={{1,0},{2,1},{3,2},{0,3},{5,4},{6,5},{7,6},{4,7},{9,8},{10,9},{11,1... | collective-permute-start | bytes 98312 | tf_op jit(solution)/shard_map/ppermute | solution.py:53
  91.4 0.8 copy.97
  92.3 1.1 %collective-permute-start.10 = (bf16[128,128]{0,1:T(8,128)(2,1)S(1)}, bf16[128,128]{0,1:T(8,128)(2,1)S(1)}, u32[]{:S(2)}, u32[]{:S(2)}) collective-permute-start(bf16[128,128]{0,1:T(8,128)(2,1)S(1)} %pad_maximum_fusion.18), channel_id=1, source_target_pairs={{0,1},{1,2},{2,3},{3,0},{4,5},{5,6},{6,7},{7,4},{8,9},{9,10},{10,1... | collective-permute-start | bytes 98312 | tf_op jit(solution)/shard_map/ppermute | solution.py:52
  93.3 1.0 collective-permute-done.11
  94.3 2.8 %collective-permute-done.10 = bf16[128,128]{0,1:T(8,128)(2,1)S(1)} collective-permute-done((bf16[128,128]{0,1:T(8,128)(2,1)S(1)}, bf16[128,128]{0,1:T(8,128)(2,1)S(1)}, u32[]{:S(2)}, u32[]{:S(2)}) %collective-permute-start.10) | collective-permute-done | bytes 32800 | tf_op jit(solution)/shard_map/ppermute | solution.py:52
  97.8 0.8 copy.98
  (193 shorter events, 17.0 us)
Async XLA Ops:
  0.6 21.5 %copy-start = (bf16[1,1,640,640]{3,2,1,0:T(8,128)(2,1)S(1)}, bf16[1,1,640,640]{3,2,1,0:T(8,128)(2,1)}, u32[]{:S(2)}) copy-start(bf16[1,1,640,640]{3,2,1,0:T(8,128)(2,1)} %param.11) | copy-start | bytes 2457604
  0.6 0.7 copy-start.28
  2.5 1.4 %copy-start.27 = (bf16[64,128]{1,0:T(8,128)(2,1)S(1)}, bf16[64,128]{1,0:T(8,128)(2,1)}, u32[]{:S(2)}) copy-start(bf16[64,128]{1,0:T(8,128)(2,1)} %param.13) | copy-start | bytes 49156
  3.9 0.7 copy-start.8
  3.9 1.4 %copy-start.26 = (f32[1,1,512,128]{3,2,1,0:T(8,128)S(1)}, f32[1,1,512,128]{3,2,1,0:T(8,128)}, u32[]{:S(2)}) copy-start(f32[1,1,512,128]{3,2,1,0:T(8,128)} %param.7) | copy-start | bytes 786436
  6.5 10.2 %all-to-all-start = ((bf16[4,128,128]{1,2,0:T(8,128)(2,1)}), bf16[4,128,128]{1,2,0:T(8,128)(2,1)S(1)}, u32[]{:S(2)}, u32[]{:S(2)}) async-start(bf16[4,128,128]{1,2,0:T(8,128)(2,1)} %pad_maximum_fusion.4), calls=%async_computation | async-start | bytes 262144 | tf_op jit(solution)/shard_map/all_to_all | solution.py:90
  16.7 14.5 %copy-start.5 = (bf16[1,128,128]{1,2,0:T(8,128)(2,1)}, bf16[1,128,128]{1,2,0:T(8,128)(2,1)S(1)}, u32[]{:S(2)}) copy-start(bf16[1,128,128]{1,2,0:T(8,128)(2,1)S(1)} %get-tuple-element.59) | copy-start | bytes 98308
  16.7 14.8 %copy-start.2 = (bf16[1,128,128]{1,2,0:T(8,128)(2,1)}, bf16[1,128,128]{1,2,0:T(8,128)(2,1)S(1)}, u32[]{:S(2)}) copy-start(bf16[1,128,128]{1,2,0:T(8,128)(2,1)S(1)} %get-tuple-element.58) | copy-start | bytes 98308
  16.8 5.3 %copy-start.15 = (f32[64,128]{0,1:T(8,128)}, f32[64,128]{0,1:T(8,128)S(1)}, u32[]{:S(2)}) copy-start(f32[64,128]{0,1:T(8,128)S(1)} %fusion.72) | copy-start | bytes 98308
  16.9 5.2 %copy-start.17 = (f32[64,128]{0,1:T(8,128)}, f32[64,128]{0,1:T(8,128)S(1)}, u32[]{:S(2)}) copy-start(f32[64,128]{0,1:T(8,128)S(1)} %fusion.71) | copy-start | bytes 98308
  17.8 12.5 %all-to-all-start.1 = ((bf16[32,16,128]{2,1,0:T(8,128)(2,1)}), bf16[32,16,128]{2,1,0:T(8,128)(2,1)S(1)}, u32[]{:S(2)}, u32[]{:S(2)}) async-start(bf16[32,16,128]{2,1,0:T(8,128)(2,1)} %broadcast_in_dim.293), calls=%async_computation.1 | async-start | bytes 262144 | tf_op jit(solution)/shard_map/all_to_all | solution.py:115
  22.9 8.4 %collective-permute-start.1 = (bf16[128,128]{0,1:T(8,128)(2,1)S(1)}, bf16[128,128]{0,1:T(8,128)(2,1)S(1)}, u32[]{:S(2)}, u32[]{:S(2)}) collective-permute-start(bf16[128,128]{0,1:T(8,128)(2,1)S(1)} %pad_maximum_fusion.9), channel_id=1, source_target_pairs={{1,0},{2,1},{3,2},{0,3},{5,4},{6,5},{7,6},{4,7},{9,8},{10,9},{11,1... | collective-permute-start | bytes 98312 | tf_op jit(solution)/shard_map/ppermute | solution.py:53
  25.7 5.8 %collective-permute-start = (bf16[128,128]{0,1:T(8,128)(2,1)S(1)}, bf16[128,128]{0,1:T(8,128)(2,1)S(1)}, u32[]{:S(2)}, u32[]{:S(2)}) collective-permute-start(bf16[128,128]{0,1:T(8,128)(2,1)S(1)} %pad_maximum_fusion.8), channel_id=1, source_target_pairs={{0,1},{1,2},{2,3},{3,0},{4,5},{5,6},{6,7},{7,4},{8,9},{9,10},{10,1... | collective-permute-start | bytes 98312 | tf_op jit(solution)/shard_map/ppermute | solution.py:52
  31.9 0.6 copy-start.11
  31.9 0.6 copy-start.13
  32.3 1.1 %copy-start.1 = (bf16[1,1,640,640]{3,2,1,0:T(8,128)(2,1)S(1)}, bf16[1,1,640,640]{3,2,1,0:T(8,128)(2,1)}, u32[]{:S(2)}) copy-start(bf16[1,1,640,640]{3,2,1,0:T(8,128)(2,1)} %param.10) | copy-start | bytes 2457604
  34.2 4.3 %collective-permute-start.3 = (bf16[128,128]{0,1:T(8,128)(2,1)S(1)}, bf16[128,128]{0,1:T(8,128)(2,1)S(1)}, u32[]{:S(2)}, u32[]{:S(2)}) collective-permute-start(bf16[128,128]{0,1:T(8,128)(2,1)S(1)} %pad_maximum_fusion.11), channel_id=1, source_target_pairs={{1,0},{2,1},{3,2},{0,3},{5,4},{6,5},{7,6},{4,7},{9,8},{10,9},{11,1... | collective-permute-start | bytes 98312 | tf_op jit(solution)/shard_map/ppermute | solution.py:53
  35.3 4.9 %collective-permute-start.2 = (bf16[128,128]{0,1:T(8,128)(2,1)S(1)}, bf16[128,128]{0,1:T(8,128)(2,1)S(1)}, u32[]{:S(2)}, u32[]{:S(2)}) collective-permute-start(bf16[128,128]{0,1:T(8,128)(2,1)S(1)} %pad_maximum_fusion.10), channel_id=1, source_target_pairs={{0,1},{1,2},{2,3},{3,0},{4,5},{5,6},{6,7},{7,4},{8,9},{9,10},{10,1... | collective-permute-start | bytes 98312 | tf_op jit(solution)/shard_map/ppermute | solution.py:52
  41.4 0.8 copy-start.16
  41.4 0.9 copy-start.18
  41.4 0.9 copy-start.19
  41.4 0.9 copy-start.20
  42.3 0.7 copy-start.9
  44.3 10.7 %all-to-all-start.2 = ((bf16[32,16,128]{2,1,0:T(8,128)(2,1)}), bf16[32,16,128]{2,1,0:T(8,128)(2,1)S(1)}, u32[]{:S(2)}, u32[]{:S(2)}) async-start(bf16[32,16,128]{2,1,0:T(8,128)(2,1)} %broadcast_in_dim.310), calls=%async_computation.2 | async-start | bytes 262144 | tf_op jit(solution)/shard_map/all_to_all | solution.py:115
  47.2 8.8 %collective-permute-start.5 = (bf16[128,128]{0,1:T(8,128)(2,1)S(1)}, bf16[128,128]{0,1:T(8,128)(2,1)S(1)}, u32[]{:S(2)}, u32[]{:S(2)}) collective-permute-start(bf16[128,128]{0,1:T(8,128)(2,1)S(1)} %pad_maximum_fusion.13), channel_id=1, source_target_pairs={{1,0},{2,1},{3,2},{0,3},{5,4},{6,5},{7,6},{4,7},{9,8},{10,9},{11,1... | collective-permute-start | bytes 98312 | tf_op jit(solution)/shard_map/ppermute | solution.py:53
  49.9 6.9 %collective-permute-start.4 = (bf16[128,128]{0,1:T(8,128)(2,1)S(1)}, bf16[128,128]{0,1:T(8,128)(2,1)S(1)}, u32[]{:S(2)}, u32[]{:S(2)}) collective-permute-start(bf16[128,128]{0,1:T(8,128)(2,1)S(1)} %pad_maximum_fusion.12), channel_id=1, source_target_pairs={{0,1},{1,2},{2,3},{3,0},{4,5},{5,6},{6,7},{7,4},{8,9},{9,10},{10,1... | collective-permute-start | bytes 98312 | tf_op jit(solution)/shard_map/ppermute | solution.py:52
  55.8 0.8 copy-start.6
  56.0 0.8 copy-start.3
  58.3 0.8 copy-start.12
  58.3 0.9 copy-start.14
  58.3 0.9 copy-start.21
  58.3 0.9 copy-start.22
  60.0 4.3 %collective-permute-start.7 = (bf16[128,128]{0,1:T(8,128)(2,1)S(1)}, bf16[128,128]{0,1:T(8,128)(2,1)S(1)}, u32[]{:S(2)}, u32[]{:S(2)}) collective-permute-start(bf16[128,128]{0,1:T(8,128)(2,1)S(1)} %pad_maximum_fusion.15), channel_id=1, source_target_pairs={{1,0},{2,1},{3,2},{0,3},{5,4},{6,5},{7,6},{4,7},{9,8},{10,9},{11,1... | collective-permute-start | bytes 98312 | tf_op jit(solution)/shard_map/ppermute | solution.py:53
  61.1 4.9 %collective-permute-start.6 = (bf16[128,128]{0,1:T(8,128)(2,1)S(1)}, bf16[128,128]{0,1:T(8,128)(2,1)S(1)}, u32[]{:S(2)}, u32[]{:S(2)}) collective-permute-start(bf16[128,128]{0,1:T(8,128)(2,1)S(1)} %pad_maximum_fusion.14), channel_id=1, source_target_pairs={{0,1},{1,2},{2,3},{3,0},{4,5},{5,6},{6,7},{7,4},{8,9},{9,10},{10,1... | collective-permute-start | bytes 98312 | tf_op jit(solution)/shard_map/ppermute | solution.py:52
  70.2 0.8 copy-start.23
  70.2 0.9 copy-start.24
  71.1 0.7 copy-start.10
  73.1 10.7 %all-to-all-start.3 = ((bf16[32,16,128]{2,1,0:T(8,128)(2,1)}), bf16[32,16,128]{2,1,0:T(8,128)(2,1)S(1)}, u32[]{:S(2)}, u32[]{:S(2)}) async-start(bf16[32,16,128]{2,1,0:T(8,128)(2,1)} %broadcast_in_dim.319), calls=%async_computation.3 | async-start | bytes 262144 | tf_op jit(solution)/shard_map/all_to_all | solution.py:115
  75.9 8.8 %collective-permute-start.9 = (bf16[128,128]{0,1:T(8,128)(2,1)S(1)}, bf16[128,128]{0,1:T(8,128)(2,1)S(1)}, u32[]{:S(2)}, u32[]{:S(2)}) collective-permute-start(bf16[128,128]{0,1:T(8,128)(2,1)S(1)} %pad_maximum_fusion.17), channel_id=1, source_target_pairs={{1,0},{2,1},{3,2},{0,3},{5,4},{6,5},{7,6},{4,7},{9,8},{10,9},{11,1... | collective-permute-start | bytes 98312 | tf_op jit(solution)/shard_map/ppermute | solution.py:53
  78.7 6.9 %collective-permute-start.8 = (bf16[128,128]{0,1:T(8,128)(2,1)S(1)}, bf16[128,128]{0,1:T(8,128)(2,1)S(1)}, u32[]{:S(2)}, u32[]{:S(2)}) collective-permute-start(bf16[128,128]{0,1:T(8,128)(2,1)S(1)} %pad_maximum_fusion.16), channel_id=1, source_target_pairs={{0,1},{1,2},{2,3},{3,0},{4,5},{5,6},{6,7},{7,4},{8,9},{9,10},{10,1... | collective-permute-start | bytes 98312 | tf_op jit(solution)/shard_map/ppermute | solution.py:52
  84.5 0.8 copy-start.7
  84.8 0.8 copy-start.4
  88.7 0.8 copy-start.25
  90.3 4.0 %collective-permute-start.11 = (bf16[128,128]{0,1:T(8,128)(2,1)S(1)}, bf16[128,128]{0,1:T(8,128)(2,1)S(1)}, u32[]{:S(2)}, u32[]{:S(2)}) collective-permute-start(bf16[128,128]{0,1:T(8,128)(2,1)S(1)} %pad_maximum_fusion.19), channel_id=1, source_target_pairs={{1,0},{2,1},{3,2},{0,3},{5,4},{6,5},{7,6},{4,7},{9,8},{10,9},{11,1... | collective-permute-start | bytes 98312 | tf_op jit(solution)/shard_map/ppermute | solution.py:53
  92.3 4.8 %collective-permute-start.10 = (bf16[128,128]{0,1:T(8,128)(2,1)S(1)}, bf16[128,128]{0,1:T(8,128)(2,1)S(1)}, u32[]{:S(2)}, u32[]{:S(2)}) collective-permute-start(bf16[128,128]{0,1:T(8,128)(2,1)S(1)} %pad_maximum_fusion.18), channel_id=1, source_target_pairs={{0,1},{1,2},{2,3},{3,0},{4,5},{5,6},{6,7},{7,4},{8,9},{9,10},{10,1... | collective-permute-start | bytes 98312 | tf_op jit(solution)/shard_map/ppermute | solution.py:52

commit v2 on v0

v2 whole, which is shorter than its diff:
```python
import functools

import jax
import jax.numpy as jnp
from jax import lax
from jax.experimental import pallas as pl
from jax.experimental.pallas import tpu as pltpu
from jax.sharding import PartitionSpec as P

ITERS = 3


STEP_SIZES = (0.8, 0.9, 1.0)
MOMENTUM = (0.0, 0.3, 0.3)

F32 = jnp.float32
BF16 = jnp.bfloat16


def mm(a, b):
    return jnp.dot(a, b, preferred_element_type=F32)


def tn(a, b):
    return lax.dot_general(a, b, (((0,), (0,)), ((), ())), preferred_element_type=F32)


def nt(a, b):
    return lax.dot_general(a, b, (((1,), (1,)), ((), ())), preferred_element_type=F32)


def run(kernel, name, outs, args, scalars=(), scratch=(), flops=1 << 22):
    nbytes = sum(x.size * x.dtype.itemsize for x in args) + sum(
        x.size * jnp.dtype(x.dtype).itemsize for x in outs
    )
    return pl.pallas_call(
        kernel,
        name=name,
        out_shape=outs,
        in_specs=[pl.BlockSpec(memory_space=pltpu.SMEM)] * len(scalars)
        + [pl.BlockSpec(memory_space=pltpu.VMEM)] * len(args),
        out_specs=[pl.BlockSpec(memory_space=pltpu.VMEM)] * len(outs),
        scratch_shapes=list(scratch),
        compiler_params=pltpu.CompilerParams(vmem_limit_bytes=24 << 20),
        cost_estimate=pl.CostEstimate(flops=flops, bytes_accessed=nbytes, transcendentals=0),
    )(*scalars, *args)


def shape(*dims, dtype=F32):
    return jax.ShapeDtypeStruct(dims, dtype)


class Sizes:
    def __init__(self, right_side, deflation, coarse_inverse):
        self.owned, self.loads = right_side.shape[-2:]
        self.order, self.modes = deflation.shape[-2:]
        self.blk = (self.order - self.owned) // 2
        self.subs = lax.axis_size("sub")
        self.groups = lax.axis_size("grp")
        self.near = min(self.subs, 5)
        self.chunks = coarse_inverse.shape[1] // self.loads
        self.window = self.near * self.modes
        self.wide = self.window * self.chunks

    def base(self, position):
        return jnp.clip(position - 2, 0, self.subs - self.near)


class Place:
    def __init__(self, z, margin, live):
        self.z = z
        self.position = lax.axis_index("sub")
        self.give_right = pl.multiple_of(margin[0, 0, 0] * z.blk, z.blk)
        self.give_left = pl.multiple_of(margin[0, 0, 1] * z.blk, z.blk)
        self.live = live[0, 0]
        self.has_left = self.position > 0
        self.has_right = self.position < z.subs - 1
        self.has_left2 = self.position > 1
        self.has_right2 = self.position < z.subs - 2

    def row_mask(self):
        z = self.z
        rows = lax.broadcasted_iota(jnp.int32, (z.owned, z.loads), 0)
        return rows < self.live

    def right_block(self, ref):
        return ref[pl.ds(self.give_right, self.z.blk), :]

    def left_block(self, ref):
        return ref[pl.ds(self.give_left, self.z.blk), :]

    def ahead(self, ref):
        z = self.z
        return jnp.concatenate([ref[z.owned + z.blk :, :], self.right_block(ref)], axis=0)

    def behind(self, ref):
        z = self.z
        return jnp.concatenate([ref[z.owned : z.owned + z.blk, :], self.left_block(ref)], axis=0)


def first_kernel(z, margin, live, source, vectors, panel, slots, own):
    at = Place(z, margin, live)
    own[...] = jnp.where(at.row_mask(), source[...], 0.0)
    side = 2 * z.blk
    eye = (
        lax.broadcasted_iota(jnp.int32, (side, side), 0)
        == lax.broadcasted_iota(jnp.int32, (side, side), 1)
    ).astype(BF16)
    ahead = jnp.concatenate(
        [tn(at.ahead(vectors), eye).astype(BF16), at.right_block(own).astype(BF16)], axis=0
    )
    behind = jnp.concatenate(
        [tn(at.behind(vectors), eye).astype(BF16), at.left_block(own).astype(BF16)], axis=0
    )
    for k in range(z.subs):
        first = min(max(k - 2, 0), z.subs - z.near) * z.modes
        for chunk in range(z.chunks):
            slots[k, chunk * z.window : (chunk + 1) * z.window, :] = panel[
                chunk, first : first + z.window, :
            ]
        slots[k, z.wide :, :] = jnp.where(k > at.position, ahead, behind)


def put_coarse(z, every_out, value):
    value = value.astype(BF16)

    def put(k, carry):
        every_out[k] = value
        return carry

    lax.fori_loop(0, z.subs * z.groups, put, 0, unroll=8)


def second_kernel(z, slots, own, vectors_t, resid, resid_low, every_out):
    position = lax.axis_index("sub")
    left = slots[jnp.maximum(position - 1, 0), z.wide + z.modes :, :]
    right = slots[jnp.minimum(position + 1, z.subs - 1), z.wide + z.modes :, :]
    value = jnp.concatenate(
        [
            own[...],
            jnp.where(position > 0, left.astype(F32), 0.0),
            jnp.where(position < z.subs - 1, right.astype(F32), 0.0),
        ],
        axis=0,
    )
    resid[...] = value
    low = value.astype(BF16)
    resid_low[...] = low
    put_coarse(z, every_out, mm(vectors_t[...], low))


def static_kernel(z, margin, live, operator, vectors_t, picked, ahead, behind):
    at = Place(z, margin, live)
    side = 2 * z.blk
    rows = jnp.concatenate([at.ahead(operator), at.behind(operator)], axis=0)
    picked[...] = rows
    row = lax.broadcasted_iota(jnp.int32, (z.order, side), 0)
    col = lax.broadcasted_iota(jnp.int32, (z.order, side), 1)
    on_left = jnp.where(col < z.blk, at.give_left + col, z.owned - z.blk + col)
    on_right = jnp.where(col < z.blk, at.give_right + col, z.owned + col)
    left_cols = mm(rows, (row == on_left).astype(BF16)).astype(BF16)
    right_cols = mm(rows, (row == on_right).astype(BF16)).astype(BF16)
    col = lax.broadcasted_iota(jnp.int32, (z.modes, z.order), 1)
    limit = jnp.where(at.has_left, z.owned + z.blk, z.owned)
    kept = (col < at.live) | ((col >= z.owned) & (col < limit))
    kept = kept | ((col >= z.owned + z.blk) & at.has_right)
    lifted = nt(jnp.where(kept, vectors_t[...].astype(F32), 0.0).astype(BF16), rows).astype(BF16)
    ahead[...] = jnp.concatenate([left_cols[:side], right_cols[:side], lifted[:, :side]], axis=0)
    behind[...] = jnp.concatenate([right_cols[side:], left_cols[side:], lifted[:, side:]], axis=0)


def window_kernel(z, turn, *refs):
    margin, live, resid_low, inverse, picked, *rest = refs
    old = rest.pop(0) if turn else None
    statics = None if turn else (rest.pop(0), rest.pop(0))
    fine, ahead, behind, *far = rest
    at = Place(z, margin, live)
    side = 2 * z.blk
    fine[...] = mm(inverse[...], resid_low[...])
    part = jnp.concatenate(
        [
            jnp.where(at.row_mask(), fine[: z.owned, :], 0.0),
            jnp.where(at.has_left, fine[z.owned : z.owned + z.blk, :], 0.0),
            jnp.where(at.has_right, fine[z.owned + z.blk :, :], 0.0),
        ],
        axis=0,
    )
    if turn:
        part = part + MOMENTUM[turn] * old[...]
    product = mm(picked[...], part.astype(BF16)).astype(BF16)
    to_right = at.ahead(fine).astype(BF16)
    to_left = at.behind(fine).astype(BF16)
    ahead[:side, :] = to_right
    ahead[side : 2 * side, :] = product[:side]
    behind[:side, :] = to_left
    behind[side : 2 * side, :] = product[side:]
    if statics:
        ahead[2 * side :, :] = statics[0][...]
        behind[2 * side :, :] = statics[1][...]
    if far:
        far[0][...] = jnp.where(at.has_right2, to_right, to_left)


def main_kernel(z, turn, *refs):
    last = turn == ITERS - 1
    margin, live, every, slots, vectors, operator, fine, *rest = refs
    left, right, far_left, far_right, left_static, right_static, resid_in, *rest = rest
    if turn:
        old, solution_in, *rest = rest
    if not last:
        vectors_t, *rest = rest
        direction, solution, resid, resid_low, every_out, error, coarse = rest
    else:
        solution, resid_out, direction, resid, error, coarse = rest
    at = Place(z, margin, live)
    owned, blk, side, modes = z.owned, z.blk, 2 * z.blk, z.modes
    cols = slice(None)

    total = jnp.zeros((z.window, z.loads), F32)
    for k in range(z.subs):
        for chunk in range(z.chunks):
            total = total + mm(
                slots[k, chunk * z.window : (chunk + 1) * z.window, :],
                every[k, chunk * z.loads : (chunk + 1) * z.loads, :],
            )
    coarse[...] = total.astype(BF16)

    def correction(offset):
        index = jnp.clip(at.position + offset - z.base(at.position), 0, z.near - 1)
        return coarse[pl.ds(pl.multiple_of(index * modes, modes), modes), :]

    def their_vectors(offset):
        index = jnp.clip(at.position + offset, 0, z.subs - 1)
        return slots[index, z.wide : z.wide + modes, :]

    def halo(have, piece, offset):
        value = piece.astype(F32) + tn(their_vectors(offset), correction(offset))
        return jnp.where(have, value, 0.0)

    error[...] = fine[...] + mm(vectors[...], correction(0))
    from_left = halo(at.has_left, left[:side, cols], -1)
    from_right = halo(at.has_right, right[:side, cols], 1)
    from_left2 = halo(at.has_left2, far_left[:side, cols], -2)
    from_right2 = halo(at.has_right2, far_right[:side, cols], 2)
    to_right = at.ahead(error).astype(BF16)
    to_left = at.behind(error).astype(BF16)

    mask = at.row_mask()

    def join(target, scale, before, rows, from_left, from_right):
        lower = slice(owned, owned + blk)
        upper = slice(owned + blk, owned + side)
        own = jnp.where(mask, rows[:owned, :], 0.0)
        low = jnp.where(at.has_left, rows[lower, :] + from_left[blk:], 0.0)
        high = jnp.where(at.has_right, rows[upper, :] + from_right[blk:], 0.0)
        parts = ((slice(0, owned), own), (lower, low), (upper, high))
        for span, part in parts:
            part = part if scale == 1.0 else scale * part
            target[span, :] = part if before is None else before(span) + part
        first, second = from_left[:blk], from_right[:blk]
        if scale != 1.0:
            first, second = scale * first, scale * second
        spot = pl.ds(at.give_left, blk)
        target[spot, :] = target[spot, :] + first
        spot = pl.ds(at.give_right, blk)
        target[spot, :] = target[spot, :] + second

    before = (lambda span: MOMENTUM[turn] * old[span, :]) if turn else None
    join(direction, 1.0, before, error, from_left, from_right)
    step = STEP_SIZES[turn] * direction[:owned, :]
    solution[...] = solution_in[...] + step if turn else step

    error[...] = mm(operator[...], direction[...].astype(BF16))

    def borrowed(have, piece, statics, far, near, offset):
        value = (
            piece[side : 2 * side, cols].astype(F32)
            + mm(statics[2 * side : 3 * side, cols], far.astype(BF16))
            + mm(statics[3 * side : 4 * side, cols], near)
            + tn(statics[4 * side :, cols], correction(offset))
        )
        return jnp.where(have, value, 0.0)

    from_left = borrowed(at.has_left, left, left_static, from_left2, to_left, -1)
    from_right = borrowed(at.has_right, right, right_static, from_right2, to_right, 1)
    join(resid, -STEP_SIZES[turn], lambda span: resid_in[span, :], error, from_left, from_right)
    if last:
        resid_out[...] = resid[:owned, :]
    else:
        low = resid[...].astype(BF16)
        resid_low[...] = low
        put_coarse(z, every_out, mm(vectors_t[...], low))


def body(
    right_side, live_rows, margin_blocks, local_operator, local_inverse, deflation, coarse_inverse
):
    z = Sizes(right_side, deflation, coarse_inverse)
    source = right_side[0, 0]
    operator = local_operator[0, 0]
    inverse = local_inverse[0, 0]
    vectors = deflation[0, 0]
    scalars = (margin_blocks, live_rows)
    owned, order, loads, modes = z.owned, z.order, z.loads, z.modes
    side = 2 * z.blk
    rim = 4 * side + modes
    devices = z.subs * z.groups

    def ring(offset):
        return [(i, (i + offset) % z.subs) for i in range(z.subs)]

    def part(function, *more):
        return functools.partial(function, z, *more)

    panel = coarse_inverse.reshape(-1, z.chunks, loads).swapaxes(0, 1)
    slots, own = run(
        part(first_kernel),
        "first",
        [shape(z.subs, z.wide + modes + z.blk, loads, dtype=BF16), shape(owned, loads)],
        [source, vectors, panel],
        scalars,
    )
    slots = lax.all_to_all(slots, "sub", 0, 0, tiled=True)
    vectors_t = vectors.T
    picked, ahead_static, behind_static = run(
        part(static_kernel),
        "static",
        [shape(2 * side, order, dtype=BF16)] + [shape(2 * side + modes, loads, dtype=BF16)] * 2,
        [operator, vectors_t],
        scalars,
    )
    every_shape = shape(devices, modes, loads, dtype=BF16)
    resid, resid_low, every = run(
        part(second_kernel),
        "second",
        [shape(order, loads), shape(order, loads, dtype=BF16), every_shape],
        [slots, own, vectors_t],
    )
    direction = solution = statics = None
    for turn in range(ITERS):
        last = turn == ITERS - 1
        every = lax.all_to_all(every, ("sub", "grp"), 0, 0, tiled=True)
        every = every.reshape(z.subs, z.groups * modes, loads)
        width = 2 * side if turn else rim
        sent = [shape(order, loads)] + [shape(width, loads, dtype=BF16)] * 2
        folded = z.subs == 4
        fine, ahead, behind, *far = run(
            part(window_kernel, turn),
            f"window{turn}",
            sent + [shape(side, loads, dtype=BF16)] * folded,
            [resid_low, inverse, picked]
            + ([direction] if turn else [ahead_static, behind_static]),
            scalars,
        )
        left = lax.ppermute(ahead, "sub", ring(1))
        right = lax.ppermute(behind, "sub", ring(-1))
        if folded:
            far_left = far_right = lax.ppermute(far[0], "sub", ring(2))
        else:
            far_left = lax.ppermute(ahead[:side], "sub", ring(2))
            far_right = lax.ppermute(behind[:side], "sub", ring(-2))
        if not turn:
            statics = (left, right)
        work = [pltpu.VMEM((order, loads), F32), pltpu.VMEM((z.window, loads), BF16)]
        args = [every, slots, vectors, operator, fine, left, right, far_left, far_right]
        args += [*statics, resid]
        if turn:
            args += [direction, solution]
        if last:
            solution, resid = run(
                part(main_kernel, turn),
                f"main{turn}",
                [shape(owned, loads)] * 2,
                args,
                scalars,
                [pltpu.VMEM((order, loads), F32)] * 2 + work,
            )
        else:
            direction, solution, resid, resid_low, every = run(
                part(main_kernel, turn),
                f"main{turn}",
                [
                    shape(order, loads),
                    shape(owned, loads),
                    shape(order, loads),
                    shape(order, loads, dtype=BF16),
                    every_shape,
                ],
                args + [vectors_t],
                scalars,
                work,
            )
    return (solution[None, None], resid[None, None])


def solution(mesh):
    return jax.shard_map(
        body,
        mesh=mesh,
        in_specs=(
            P("grp", "sub", None, None),
            P("grp", "sub"),
            P("grp", "sub", None),
            P("grp", "sub", None, None),
            P("grp", "sub", None, None),
            P("grp", "sub", None, None),
            P("grp", "sub"),
        ),
        out_specs=(P("grp", "sub", None, None), P("grp", "sub", None, None)),
        check_vma=False,
    )
```

time: 191 us -> 81.8 us (0.43)
  blocking collectives: 88.7 us -> 10.5 us
  waiting for transfers between devices: 30.3 us -> 9.86 us
  Pallas kernels: 0 us -> 12.2 us
  starting transfers between devices: 35.7 us -> 27.6 us
  other arithmetic: 7.52 us -> 0 us
  matrix products: 3.98 us -> 0 us
  between operations: 4.11 us -> 1.52 us
    unnamed x3 -> x0, blocking collectives: 45.9 us -> none
    all_gather x3 -> x0, blocking collectives: 42.8 us -> none  [body(): column = lax.all_gather(coarse_resid, 'grp', axis=0, tiled=True)]
    ppermute x14 -> x9, starting transfers between devices: 35.7 us -> 14.1 us  [the longest x3 5.3 us: body(): far_left = far_right = lax.ppermute(far[0], 'sub', ring(2))]
    ppermute x14 -> x9, waiting for transfers between devices: 30.3 us -> 9.85 us  [the longest x3 7.47 us: body(): far_left = far_right = lax.ppermute(far[0], 'sub', ring(2))]
    all_to_all x0 -> x3, starting transfers between devices: none -> 13.5 us  [body(): every = lax.all_to_all(every, ('sub', 'grp'), 0, 0, tiled=True)]
    unnamed x32 -> x57, local copies, waits for them, and re-layouts: 6.34 us -> 19.3 us
    pallas_call x0 -> x9, Pallas kernels: none -> 12.2 us  [run(): pl.pallas_call(kernel, name=name, out_shape=outs, in_specs=[pl.BlockSpec(...]
    all_to_all x0 -> x1, blocking collectives: none -> 10.5 us  [body(): slots = lax.all_to_all(slots, 'sub', 0, 0, tiled=True)]
  transfers between devices with their start and end apart: 14 -> 12, of which waited for: 12 -> 5; matrix products, arithmetic and copies ran while one was open for 1% -> 0% of each run, Pallas kernels for 0% -> 6%
where the time goes in v2:
time: 81.8 us; the launch traced here: 81 us
  starting transfers between devices  27.6 us (34%)
  local copies, waits for them, and re-layouts  19.3 us (24%)
  Pallas kernels  12.2 us (15%)
  blocking collectives  10.5 us (13%)
  waiting for transfers between devices  9.86 us (12%)
  between operations  1.52 us (2%)
    unnamed x57, local copies, waits for them, and re-layouts  19.3 us
    all_to_all x3, starting transfers between devices, body(): every = lax.all_to_all(every, ('sub', 'grp'), 0, 0, tiled=True)  13.5 us
    pallas_call x9, Pallas kernels, run(): pl.pallas_call(kernel, name=name, out_shape=outs, in_specs=[pl.BlockSpec(...  12.2 us
    all_to_all x1, blocking collectives, body(): slots = lax.all_to_all(slots, 'sub', 0, 0, tiled=True)  10.5 us
    ppermute x3, waiting for transfers between devices, body(): far_left = far_right = lax.ppermute(far[0], 'sub', ring(2))  7.47 us
    ppermute x3, starting transfers between devices, body(): far_left = far_right = lax.ppermute(far[0], 'sub', ring(2))  5.3 us
    ppermute x3, starting transfers between devices, body(): left = lax.ppermute(ahead, 'sub', ring(1))  5.3 us
    ppermute x3, starting transfers between devices, body(): right = lax.ppermute(behind, 'sub', ring(-1))  3.47 us
  transfers between devices with their start and end apart: 12, of which 5 were waited for; matrix products, arithmetic and copies ran while one was open for 0% of the time, Pallas kernels for 6%

profile of v2, /device:TPU:0, one launch (start us, length us, event | category | flops | bytes accessed | tf_op | source)
XLA Modules:
  0.0 81.0 jit_solution(14515434527176022174)
XLA Ops:
  1.4 0.9 %copy.9 = bf16[1,1,640,16]{3,2,1,0:T(8,128)(2,1)S(1)} copy(bf16[1,1,640,16]{2,3,1,0:T(8,128)(2,1)} %param.12) | data formatting | bytes 40960 | tf_op args[5]
  2.3 0.9 %copy-done.15 = f32[1,1,512,128]{3,2,1,0:T(8,128)S(1)} copy-done((f32[1,1,512,128]{3,2,1,0:T(8,128)S(1)}, f32[1,1,512,128]{3,2,1,0:T(8,128)}, u32[]{:S(2)}) %copy-start.15) | copy-done | bytes 262168
  3.2 0.7 copy-done.25
  3.9 0.7 copy-done.27
  4.6 0.7 first.1
  5.3 10.5 %all_to_all.20.slots.refs_3_ = bf16[4,144,128]{2,1,0:T(8,128)(2,1)S(1)} all-to-all(bf16[4,144,128]{2,1,0:T(8,128)(2,1)S(1)} %get-tuple-element.34), channel_id=1, replica_groups=mesh['grp'=8,'sub'=4] {'sub'}, dimensions={0} | all-to-all | bytes 294912 | tf_op jit(solution)/shard_map/all_to_all | solution.py:323
  15.9 0.8 %second.1 = (f32[640,128]{1,0:T(8,128)S(1)}, bf16[640,128]{1,0:T(8,128)(2,1)S(1)}, bf16[32,16,128]{2,1,0:T(8,128)(2,1)}) custom-call(bf16[4,144,128]{2,1,0:T(8,128)(2,1)S(1)} %all_to_all.20.slots.refs_3_, f32[512,128]{1,0:T(8,128)S(1)} %get-tuple-element.35.own, bf16[16,640]{1,0:T(8,128)(2,1)S(1)} %bitcast.26), custom_call_target="tpu_custom_call" | custom-call | flops 4194304 | bytes 1052672 | tf_op jit(solution)/shard_map/second/pallas_call | solution.py:36
  16.7 0.7 copy-done.3
  17.4 4.0 %all-to-all-start.1 = ((bf16[32,16,128]{2,1,0:T(8,128)(2,1)}), bf16[32,16,128]{2,1,0:T(8,128)(2,1)S(1)}, u32[]{:S(2)}, u32[]{:S(2)}) async-start(bf16[32,16,128]{2,1,0:T(8,128)(2,1)} %get-tuple-element.36), calls=%async_computation.1 | async-start | bytes 262144 | tf_op jit(solution)/shard_map/all_to_all | solution.py:342
  21.5 0.9 %static.1 = (bf16[256,640]{1,0:T(8,128)(2,1)S(1)}, bf16[272,128]{1,0:T(8,128)(2,1)S(1)}, bf16[272,128]{1,0:T(8,128)(2,1)S(1)}) custom-call(s32[1,1,2]{2,1,0:T(1,128)S(1)} %copy-done.26, s32[1,1]{1,0:T(1,128)S(6)} %copy.15.live.refs_1_, bf16[640,640]{1,0:T(8,128)(2,1)S(1)} %bitcast.12, bf16[16,640]{1,0:T(8,128)(2,1)S(1)} %bitcast.27), custom_call_target="tpu_custom_call" | custom-call | flops 4194304 | bytes 1306624 | tf_op jit(solution)/shard_map/static/pallas_call | solution.py:36
  22.4 1.2 %window0.1 = (f32[640,128]{1,0:T(8,128)S(1)}, bf16[528,128]{1,0:T(8,128)(2,1)S(1)}, bf16[528,128]{1,0:T(8,128)(2,1)S(1)}, bf16[128,128]{1,0:T(8,128)(2,1)S(1)}) custom-call(s32[1,1,2]{2,1,0:T(1,128)S(1)} %copy-done.26, s32[1,1]{1,0:T(1,128)S(6)} %copy.15.live.refs_1_, bf16[640,128]{1,0:T(8,128)(2,1)S(1)} %get-tuple-element.37.refs_2_, ...), custom_call_target="tpu_custom_call" | custom-call | flops 4194304 | bytes 2080768 | tf_op jit(solution)/shard_map/window0/pallas_call | solution.py:36
  23.6 0.7 copy-done.5
  24.3 1.8 %collective-permute-start = (bf16[528,128]{1,0:T(8,128)(2,1)S(1)}, bf16[528,128]{1,0:T(8,128)(2,1)S(1)}, u32[]{:S(2)}, u32[]{:S(2)}) collective-permute-start(bf16[528,128]{1,0:T(8,128)(2,1)S(1)} %get-tuple-element.42), channel_id=1, source_target_pairs={{0,1},{1,2},{2,3},{3,0},{4,5},{5,6},{6,7},{7,4},{8,9},{9,10},{10,1... | collective-permute-start | bytes 405512 | tf_op jit(solution)/shard_map/ppermute | solution.py:355
  26.1 1.2 %collective-permute-start.1 = (bf16[528,128]{1,0:T(8,128)(2,1)S(1)}, bf16[528,128]{1,0:T(8,128)(2,1)S(1)}, u32[]{:S(2)}, u32[]{:S(2)}) collective-permute-start(bf16[528,128]{1,0:T(8,128)(2,1)S(1)} %get-tuple-element.43), channel_id=1, source_target_pairs={{0,3},{1,0},{2,1},{3,2},{4,7},{5,4},{6,5},{7,6},{8,11},{9,8},{10,9... | collective-permute-start | bytes 405512 | tf_op jit(solution)/shard_map/ppermute | solution.py:356
  27.2 1.8 %collective-permute-start.2 = (bf16[128,128]{1,0:T(8,128)(2,1)S(1)}, bf16[128,128]{1,0:T(8,128)(2,1)S(1)}, u32[]{:S(2)}, u32[]{:S(2)}) collective-permute-start(bf16[128,128]{1,0:T(8,128)(2,1)S(1)} %get-tuple-element.44), channel_id=1, source_target_pairs={{0,2},{1,3},{2,0},{3,1},{4,6},{5,7},{6,4},{7,5},{8,10},{9,11},{10,... | collective-permute-start | bytes 98312 | tf_op jit(solution)/shard_map/ppermute | solution.py:358
  29.0 3.1 %collective-permute-done.2.refs_9_.refs_10_ = bf16[128,128]{1,0:T(8,128)(2,1)S(1)} collective-permute-done((bf16[128,128]{1,0:T(8,128)(2,1)S(1)}, bf16[128,128]{1,0:T(8,128)(2,1)S(1)}, u32[]{:S(2)}, u32[]{:S(2)}) %collective-permute-start.2) | collective-permute-done | bytes 32800 | tf_op jit(solution)/shard_map/ppermute | solution.py:358
  32.1 2.1 %collective-permute-done.1.refs_8_.refs_12_ = bf16[528,128]{1,0:T(8,128)(2,1)S(1)} collective-permute-done((bf16[528,128]{1,0:T(8,128)(2,1)S(1)}, bf16[528,128]{1,0:T(8,128)(2,1)S(1)}, u32[]{:S(2)}, u32[]{:S(2)}) %collective-permute-start.1) | collective-permute-done | bytes 135200 | tf_op jit(solution)/shard_map/ppermute | solution.py:356
  34.2 1.0 %copy-done.4 = f32[640,128]{1,0:T(8,128)S(1)} copy-done((f32[640,128]{1,0:T(8,128)S(1)}, f32[640,128]{1,0:T(8,128)}, u32[]{:S(2)}) %copy-start.4) | copy-done | bytes 327704
  35.2 1.0 %copy-done.6 = f32[640,128]{1,0:T(8,128)S(1)} copy-done((f32[640,128]{1,0:T(8,128)S(1)}, f32[640,128]{1,0:T(8,128)}, u32[]{:S(2)}) %copy-start.6) | copy-done | bytes 327704
  36.1 2.3 %main0.1 = (f32[640,128]{1,0:T(8,128)S(1)}, f32[512,128]{1,0:T(8,128)S(1)}, f32[640,128]{1,0:T(8,128)S(1)}, bf16[640,128]{1,0:T(8,128)(2,1)S(1)}, bf16[32,16,128]{2,1,0:T(8,128)(2,1)}) custom-call(s32[1,1,2]{2,1,0:T(1,128)S(1)} %copy-done.26, s32[1,1]{1,0:T(1,128)S(6)} %copy.15.live.refs_1_, bf16[4,128,128]{2,1,0:T(8,128)(2,1)S(1)} %bitcast.23, ...), custom_call_target="tpu_custom_call" | custom-call | flops 4194304 | bytes 3612672 | tf_op jit(solution)/shard_map/main0/pallas_call | solution.py:36
  38.4 0.7 copy-done.9
  39.2 0.7 copy-done.18
  39.9 4.5 %all-to-all-start.2 = ((bf16[32,16,128]{2,1,0:T(8,128)(2,1)}), bf16[32,16,128]{2,1,0:T(8,128)(2,1)S(1)}, u32[]{:S(2)}, u32[]{:S(2)}) async-start(bf16[32,16,128]{2,1,0:T(8,128)(2,1)} %get-tuple-element.46), calls=%async_computation.2 | async-start | bytes 262144 | tf_op jit(solution)/shard_map/all_to_all | solution.py:342
  44.3 1.2 %window1.1 = (f32[640,128]{1,0:T(8,128)S(1)}, bf16[256,128]{1,0:T(8,128)(2,1)S(1)}, bf16[256,128]{1,0:T(8,128)(2,1)S(1)}, bf16[128,128]{1,0:T(8,128)(2,1)S(1)}) custom-call(s32[1,1,2]{2,1,0:T(1,128)S(1)} %copy-done.26, s32[1,1]{1,0:T(1,128)S(6)} %copy.15.live.refs_1_, bf16[640,128]{1,0:T(8,128)(2,1)S(1)} %get-tuple-element.47.refs_2_, ...), custom_call_target="tpu_custom_call" | custom-call | flops 4194304 | bytes 2129920 | tf_op jit(solution)/shard_map/window1/pallas_call | solution.py:36
  45.6 0.7 copy-done.13
  46.3 1.8 %collective-permute-start.3 = (bf16[256,128]{1,0:T(8,128)(2,1)S(1)}, bf16[256,128]{1,0:T(8,128)(2,1)S(1)}, u32[]{:S(2)}, u32[]{:S(2)}) collective-permute-start(bf16[256,128]{1,0:T(8,128)(2,1)S(1)} %get-tuple-element.50), channel_id=1, source_target_pairs={{0,1},{1,2},{2,3},{3,0},{4,5},{5,6},{6,7},{7,4},{8,9},{9,10},{10,1... | collective-permute-start | bytes 196616 | tf_op jit(solution)/shard_map/ppermute | solution.py:355
  48.0 1.2 %collective-permute-start.4 = (bf16[256,128]{1,0:T(8,128)(2,1)S(1)}, bf16[256,128]{1,0:T(8,128)(2,1)S(1)}, u32[]{:S(2)}, u32[]{:S(2)}) collective-permute-start(bf16[256,128]{1,0:T(8,128)(2,1)S(1)} %get-tuple-element.51), channel_id=1, source_target_pairs={{0,3},{1,0},{2,1},{3,2},{4,7},{5,4},{6,5},{7,6},{8,11},{9,8},{10,9... | collective-permute-start | bytes 196616 | tf_op jit(solution)/shard_map/ppermute | solution.py:356
  49.2 1.8 %collective-permute-start.5 = (bf16[128,128]{1,0:T(8,128)(2,1)S(1)}, bf16[128,128]{1,0:T(8,128)(2,1)S(1)}, u32[]{:S(2)}, u32[]{:S(2)}) collective-permute-start(bf16[128,128]{1,0:T(8,128)(2,1)S(1)} %get-tuple-element.52), channel_id=1, source_target_pairs={{0,2},{1,3},{2,0},{3,1},{4,6},{5,7},{6,4},{7,5},{8,10},{9,11},{10,... | collective-permute-start | bytes 98312 | tf_op jit(solution)/shard_map/ppermute | solution.py:358
  51.0 2.2 %collective-permute-done.5.refs_9_.refs_10_ = bf16[128,128]{1,0:T(8,128)(2,1)S(1)} collective-permute-done((bf16[128,128]{1,0:T(8,128)(2,1)S(1)}, bf16[128,128]{1,0:T(8,128)(2,1)S(1)}, u32[]{:S(2)}, u32[]{:S(2)}) %collective-permute-start.5) | collective-permute-done | bytes 32800 | tf_op jit(solution)/shard_map/ppermute | solution.py:358
  54.4 1.0 %copy-done.10 = f32[640,128]{1,0:T(8,128)S(1)} copy-done((f32[640,128]{1,0:T(8,128)S(1)}, f32[640,128]{1,0:T(8,128)}, u32[]{:S(2)}) %copy-start.10) | copy-done | bytes 327704
  55.4 1.0 %copy-done.14 = f32[640,128]{1,0:T(8,128)S(1)} copy-done((f32[640,128]{1,0:T(8,128)S(1)}, f32[640,128]{1,0:T(8,128)}, u32[]{:S(2)}) %copy-start.14) | copy-done | bytes 327704
  56.3 0.9 %copy-done.19 = f32[512,128]{1,0:T(8,128)S(1)} copy-done((f32[512,128]{1,0:T(8,128)S(1)}, f32[512,128]{1,0:T(8,128)}, u32[]{:S(2)}) %copy-start.19) | copy-done | bytes 262168
  57.3 0.8 %copy-done.22 = bf16[256,128]{1,0:T(8,128)(2,1)S(1)} copy-done((bf16[256,128]{1,0:T(8,128)(2,1)S(1)}, bf16[256,128]{1,0:T(8,128)(2,1)}, u32[]{:S(2)}) %copy-start.22) | copy-done | bytes 65560
  58.1 0.8 %copy-done.24 = bf16[256,128]{1,0:T(8,128)(2,1)S(1)} copy-done((bf16[256,128]{1,0:T(8,128)(2,1)S(1)}, bf16[256,128]{1,0:T(8,128)(2,1)}, u32[]{:S(2)}) %copy-start.24) | copy-done | bytes 65560
  59.0 1.6 %main1.1 = (f32[640,128]{1,0:T(8,128)S(1)}, f32[512,128]{1,0:T(8,128)S(1)}, f32[640,128]{1,0:T(8,128)S(1)}, bf16[640,128]{1,0:T(8,128)(2,1)S(1)}, bf16[32,16,128]{2,1,0:T(8,128)(2,1)S(1)}) custom-call(s32[1,1,2]{2,1,0:T(1,128)S(1)} %copy-done.26, s32[1,1]{1,0:T(1,128)S(6)} %copy.15.live.refs_1_, bf16[4,128,128]{2,1,0:T(8,128)(2,1)S(1)} %bitcast.25, ...), custom_call_target="tpu_custom_call" | custom-call | flops 4194304 | bytes 4063232 | tf_op jit(solution)/shard_map/main1/pallas_call | solution.py:36
  60.6 0.7 copy-done.7
  61.4 0.7 copy-done.16
  62.1 0.7 copy-done.20
  62.7 5.1 %all-to-all-start.3 = ((bf16[32,16,128]{2,1,0:T(8,128)(2,1)}), bf16[32,16,128]{2,1,0:T(8,128)(2,1)S(1)}, u32[]{:S(2)}, u32[]{:S(2)}) async-start(bf16[32,16,128]{2,1,0:T(8,128)(2,1)} %copy-done.20), calls=%async_computation.3 | async-start | bytes 262144 | tf_op jit(solution)/shard_map/all_to_all | solution.py:342
  67.8 1.2 %window2.1 = (f32[640,128]{1,0:T(8,128)S(1)}, bf16[256,128]{1,0:T(8,128)(2,1)S(1)}, bf16[256,128]{1,0:T(8,128)(2,1)S(1)}, bf16[128,128]{1,0:T(8,128)(2,1)S(1)}) custom-call(s32[1,1,2]{2,1,0:T(1,128)S(1)} %copy-done.26, s32[1,1]{1,0:T(1,128)S(6)} %copy.15.live.refs_1_, bf16[640,128]{1,0:T(8,128)(2,1)S(1)} %get-tuple-element.56.refs_2_, ...), custom_call_target="tpu_custom_call" | custom-call | flops 4194304 | bytes 2129920 | tf_op jit(solution)/shard_map/window2/pallas_call | solution.py:36
  69.0 0.7 copy-done.11
  69.7 1.8 %collective-permute-start.6 = (bf16[256,128]{1,0:T(8,128)(2,1)S(1)}, bf16[256,128]{1,0:T(8,128)(2,1)S(1)}, u32[]{:S(2)}, u32[]{:S(2)}) collective-permute-start(bf16[256,128]{1,0:T(8,128)(2,1)S(1)} %get-tuple-element.59), channel_id=1, source_target_pairs={{0,1},{1,2},{2,3},{3,0},{4,5},{5,6},{6,7},{7,4},{8,9},{9,10},{10,1... | collective-permute-start | bytes 196616 | tf_op jit(solution)/shard_map/ppermute | solution.py:355
  71.5 1.2 %collective-permute-start.7 = (bf16[256,128]{1,0:T(8,128)(2,1)S(1)}, bf16[256,128]{1,0:T(8,128)(2,1)S(1)}, u32[]{:S(2)}, u32[]{:S(2)}) collective-permute-start(bf16[256,128]{1,0:T(8,128)(2,1)S(1)} %get-tuple-element.60), channel_id=1, source_target_pairs={{0,3},{1,0},{2,1},{3,2},{4,7},{5,4},{6,5},{7,6},{8,11},{9,8},{10,9... | collective-permute-start | bytes 196616 | tf_op jit(solution)/shard_map/ppermute | solution.py:356
  72.7 1.8 %collective-permute-start.8 = (bf16[128,128]{1,0:T(8,128)(2,1)S(1)}, bf16[128,128]{1,0:T(8,128)(2,1)S(1)}, u32[]{:S(2)}, u32[]{:S(2)}) collective-permute-start(bf16[128,128]{1,0:T(8,128)(2,1)S(1)} %get-tuple-element.61), channel_id=1, source_target_pairs={{0,2},{1,3},{2,0},{3,1},{4,6},{5,7},{6,4},{7,5},{8,10},{9,11},{10,... | collective-permute-start | bytes 98312 | tf_op jit(solution)/shard_map/ppermute | solution.py:358
  74.4 2.2 %collective-permute-done.8.refs_9_.refs_10_ = bf16[128,128]{1,0:T(8,128)(2,1)S(1)} collective-permute-done((bf16[128,128]{1,0:T(8,128)(2,1)S(1)}, bf16[128,128]{1,0:T(8,128)(2,1)S(1)}, u32[]{:S(2)}, u32[]{:S(2)}) %collective-permute-start.8) | collective-permute-done | bytes 32800 | tf_op jit(solution)/shard_map/ppermute | solution.py:358
  76.9 1.0 %copy-done.12 = f32[640,128]{1,0:T(8,128)S(1)} copy-done((f32[640,128]{1,0:T(8,128)S(1)}, f32[640,128]{1,0:T(8,128)}, u32[]{:S(2)}) %copy-start.12) | copy-done | bytes 327704
  77.9 0.9 %copy-done.17 = f32[512,128]{1,0:T(8,128)S(1)} copy-done((f32[512,128]{1,0:T(8,128)S(1)}, f32[512,128]{1,0:T(8,128)}, u32[]{:S(2)}) %copy-start.17) | copy-done | bytes 262168
  78.8 2.2 %main2.1 = (f32[512,128]{1,0:T(8,128)}, f32[512,128]{1,0:T(8,128)}) custom-call(s32[1,1,2]{2,1,0:T(1,128)S(1)} %copy-done.26, s32[1,1]{1,0:T(1,128)S(6)} %copy.15.live.refs_1_, bf16[4,128,128]{2,1,0:T(8,128)(2,1)S(1)} %bitcast.24, bf16[4,144,128]{2,1,0:T(8,128)(2,1)S(1)} %all_to_all.20.slots.refs_3_, bf16[640,16]{1,0:T(8,128)(2,1)S(1)} %bitcast.22, ...), custom_call_target="tpu_custom_call" | custom-call | flops 4194304 | bytes 3354624 | tf_op jit(solution)/shard_map/main2/pallas_call | solution.py:36
  (43 shorter events, 1.6 us)
Async XLA Ops:
  0.6 20.8 %copy-start = (bf16[1,1,640,640]{3,2,1,0:T(8,128)(2,1)S(1)}, bf16[1,1,640,640]{3,2,1,0:T(8,128)(2,1)}, u32[]{:S(2)}) copy-start(bf16[1,1,640,640]{3,2,1,0:T(8,128)(2,1)} %param.10) | copy-start | bytes 2457604
  2.3 1.0 %copy-start.15 = (f32[1,1,512,128]{3,2,1,0:T(8,128)S(1)}, f32[1,1,512,128]{3,2,1,0:T(8,128)}, u32[]{:S(2)}) copy-start(f32[1,1,512,128]{3,2,1,0:T(8,128)} %param.7) | copy-start | bytes 786436
  3.2 0.7 copy-start.25
  3.9 0.7 copy-start.27
  5.3 10.6 %copy-start.2 = (bf16[1,1,640,16]{2,3,1,0:T(8,128)(2,1)S(1)}, bf16[1,1,640,16]{2,3,1,0:T(8,128)(2,1)}, u32[]{:S(2)}) copy-start(bf16[1,1,640,16]{2,3,1,0:T(8,128)(2,1)} %param.12) | copy-start | bytes 61444
  5.3 16.2 %copy-start.26 = (s32[1,1,2]{2,1,0:T(1,128)S(1)}, s32[1,1,2]{2,1,0:T(1,128)}, u32[]{:S(2)}) copy-start(s32[1,1,2]{2,1,0:T(1,128)} %refs_0_.11) | copy-start | bytes 28
  15.8 6.5 %copy-start.1 = (bf16[1,1,640,640]{3,2,1,0:T(8,128)(2,1)S(1)}, bf16[1,1,640,640]{3,2,1,0:T(8,128)(2,1)}, u32[]{:S(2)}) copy-start(bf16[1,1,640,640]{3,2,1,0:T(8,128)(2,1)} %param.11) | copy-start | bytes 2457604
  16.7 0.7 copy-start.3
  17.4 16.8 %all-to-all-start.1 = ((bf16[32,16,128]{2,1,0:T(8,128)(2,1)}), bf16[32,16,128]{2,1,0:T(8,128)(2,1)S(1)}, u32[]{:S(2)}, u32[]{:S(2)}) async-start(bf16[32,16,128]{2,1,0:T(8,128)(2,1)} %get-tuple-element.36), calls=%async_computation.1 | async-start | bytes 262144 | tf_op jit(solution)/shard_map/all_to_all | solution.py:342
  23.6 0.7 copy-start.5
  24.3 7.8 %collective-permute-start = (bf16[528,128]{1,0:T(8,128)(2,1)S(1)}, bf16[528,128]{1,0:T(8,128)(2,1)S(1)}, u32[]{:S(2)}, u32[]{:S(2)}) collective-permute-start(bf16[528,128]{1,0:T(8,128)(2,1)S(1)} %get-tuple-element.42), channel_id=1, source_target_pairs={{0,1},{1,2},{2,3},{3,0},{4,5},{5,6},{6,7},{7,4},{8,9},{9,10},{10,1... | collective-permute-start | bytes 405512 | tf_op jit(solution)/shard_map/ppermute | solution.py:355
  26.1 8.1 %collective-permute-start.1 = (bf16[528,128]{1,0:T(8,128)(2,1)S(1)}, bf16[528,128]{1,0:T(8,128)(2,1)S(1)}, u32[]{:S(2)}, u32[]{:S(2)}) collective-permute-start(bf16[528,128]{1,0:T(8,128)(2,1)S(1)} %get-tuple-element.43), channel_id=1, source_target_pairs={{0,3},{1,0},{2,1},{3,2},{4,7},{5,4},{6,5},{7,6},{8,11},{9,8},{10,9... | collective-permute-start | bytes 405512 | tf_op jit(solution)/shard_map/ppermute | solution.py:356
  27.2 4.9 %collective-permute-start.2 = (bf16[128,128]{1,0:T(8,128)(2,1)S(1)}, bf16[128,128]{1,0:T(8,128)(2,1)S(1)}, u32[]{:S(2)}, u32[]{:S(2)}) collective-permute-start(bf16[128,128]{1,0:T(8,128)(2,1)S(1)} %get-tuple-element.44), channel_id=1, source_target_pairs={{0,2},{1,3},{2,0},{3,1},{4,6},{5,7},{6,4},{7,5},{8,10},{9,11},{10,... | collective-permute-start | bytes 98312 | tf_op jit(solution)/shard_map/ppermute | solution.py:358
  34.2 1.0 %copy-start.4 = (f32[640,128]{1,0:T(8,128)S(1)}, f32[640,128]{1,0:T(8,128)}, u32[]{:S(2)}) copy-start(f32[640,128]{1,0:T(8,128)} %copy-done.3) | copy-start | bytes 983044
  35.2 1.0 %copy-start.6 = (f32[640,128]{1,0:T(8,128)S(1)}, f32[640,128]{1,0:T(8,128)}, u32[]{:S(2)}) copy-start(f32[640,128]{1,0:T(8,128)} %copy-done.5) | copy-start | bytes 983044
  38.4 0.7 copy-start.9
  39.2 0.7 copy-start.18
  39.9 14.5 %all-to-all-start.2 = ((bf16[32,16,128]{2,1,0:T(8,128)(2,1)}), bf16[32,16,128]{2,1,0:T(8,128)(2,1)S(1)}, u32[]{:S(2)}, u32[]{:S(2)}) async-start(bf16[32,16,128]{2,1,0:T(8,128)(2,1)} %get-tuple-element.46), calls=%async_computation.2 | async-start | bytes 262144 | tf_op jit(solution)/shard_map/all_to_all | solution.py:342
  45.5 0.7 copy-start.13
  46.3 6.9 %collective-permute-start.3 = (bf16[256,128]{1,0:T(8,128)(2,1)S(1)}, bf16[256,128]{1,0:T(8,128)(2,1)S(1)}, u32[]{:S(2)}, u32[]{:S(2)}) collective-permute-start(bf16[256,128]{1,0:T(8,128)(2,1)S(1)} %get-tuple-element.50), channel_id=1, source_target_pairs={{0,1},{1,2},{2,3},{3,0},{4,5},{5,6},{6,7},{7,4},{8,9},{9,10},{10,1... | collective-permute-start | bytes 196616 | tf_op jit(solution)/shard_map/ppermute | solution.py:355
  48.0 5.7 %collective-permute-start.4 = (bf16[256,128]{1,0:T(8,128)(2,1)S(1)}, bf16[256,128]{1,0:T(8,128)(2,1)S(1)}, u32[]{:S(2)}, u32[]{:S(2)}) collective-permute-start(bf16[256,128]{1,0:T(8,128)(2,1)S(1)} %get-tuple-element.51), channel_id=1, source_target_pairs={{0,3},{1,0},{2,1},{3,2},{4,7},{5,4},{6,5},{7,6},{8,11},{9,8},{10,9... | collective-permute-start | bytes 196616 | tf_op jit(solution)/shard_map/ppermute | solution.py:356
  49.2 4.0 %collective-permute-start.5 = (bf16[128,128]{1,0:T(8,128)(2,1)S(1)}, bf16[128,128]{1,0:T(8,128)(2,1)S(1)}, u32[]{:S(2)}, u32[]{:S(2)}) collective-permute-start(bf16[128,128]{1,0:T(8,128)(2,1)S(1)} %get-tuple-element.52), channel_id=1, source_target_pairs={{0,2},{1,3},{2,0},{3,1},{4,6},{5,7},{6,4},{7,5},{8,10},{9,11},{10,... | collective-permute-start | bytes 98312 | tf_op jit(solution)/shard_map/ppermute | solution.py:358
  53.2 0.6 copy-start.21
  53.8 0.6 copy-start.23
  54.4 1.0 %copy-start.10 = (f32[640,128]{1,0:T(8,128)S(1)}, f32[640,128]{1,0:T(8,128)}, u32[]{:S(2)}) copy-start(f32[640,128]{1,0:T(8,128)} %copy-done.9) | copy-start | bytes 983044
  55.4 1.0 %copy-start.14 = (f32[640,128]{1,0:T(8,128)S(1)}, f32[640,128]{1,0:T(8,128)}, u32[]{:S(2)}) copy-start(f32[640,128]{1,0:T(8,128)} %copy-done.13) | copy-start | bytes 983044
  56.3 0.9 %copy-start.19 = (f32[512,128]{1,0:T(8,128)S(1)}, f32[512,128]{1,0:T(8,128)}, u32[]{:S(2)}) copy-start(f32[512,128]{1,0:T(8,128)} %copy-done.18) | copy-start | bytes 786436
  57.3 0.8 %copy-start.22 = (bf16[256,128]{1,0:T(8,128)(2,1)S(1)}, bf16[256,128]{1,0:T(8,128)(2,1)}, u32[]{:S(2)}) copy-start(bf16[256,128]{1,0:T(8,128)(2,1)} %copy-done.21) | copy-start | bytes 196612
  58.1 0.8 %copy-start.24 = (bf16[256,128]{1,0:T(8,128)(2,1)S(1)}, bf16[256,128]{1,0:T(8,128)(2,1)}, u32[]{:S(2)}) copy-start(bf16[256,128]{1,0:T(8,128)(2,1)} %copy-done.23) | copy-start | bytes 196612
  60.6 0.7 copy-start.7
  61.4 0.7 copy-start.16
  62.1 0.7 copy-start.20
  62.7 14.2 %all-to-all-start.3 = ((bf16[32,16,128]{2,1,0:T(8,128)(2,1)}), bf16[32,16,128]{2,1,0:T(8,128)(2,1)S(1)}, u32[]{:S(2)}, u32[]{:S(2)}) async-start(bf16[32,16,128]{2,1,0:T(8,128)(2,1)} %copy-done.20), calls=%async_computation.3 | async-start | bytes 262144 | tf_op jit(solution)/shard_map/all_to_all | solution.py:342
  67.8 9.1 %copy-start.8 = (f32[640,128]{1,0:T(8,128)S(1)}, f32[640,128]{1,0:T(8,128)}, u32[]{:S(2)}) copy-start(f32[640,128]{1,0:T(8,128)} %copy-done.7) | copy-start | bytes 983044
  69.0 0.7 copy-start.11
  69.7 6.9 %collective-permute-start.6 = (bf16[256,128]{1,0:T(8,128)(2,1)S(1)}, bf16[256,128]{1,0:T(8,128)(2,1)S(1)}, u32[]{:S(2)}, u32[]{:S(2)}) collective-permute-start(bf16[256,128]{1,0:T(8,128)(2,1)S(1)} %get-tuple-element.59), channel_id=1, source_target_pairs={{0,1},{1,2},{2,3},{3,0},{4,5},{5,6},{6,7},{7,4},{8,9},{9,10},{10,1... | collective-permute-start | bytes 196616 | tf_op jit(solution)/shard_map/ppermute | solution.py:355
  71.5 5.4 %collective-permute-start.7 = (bf16[256,128]{1,0:T(8,128)(2,1)S(1)}, bf16[256,128]{1,0:T(8,128)(2,1)S(1)}, u32[]{:S(2)}, u32[]{:S(2)}) collective-permute-start(bf16[256,128]{1,0:T(8,128)(2,1)S(1)} %get-tuple-element.60), channel_id=1, source_target_pairs={{0,3},{1,0},{2,1},{3,2},{4,7},{5,4},{6,5},{7,6},{8,11},{9,8},{10,9... | collective-permute-start | bytes 196616 | tf_op jit(solution)/shard_map/ppermute | solution.py:356
  72.7 4.0 %collective-permute-start.8 = (bf16[128,128]{1,0:T(8,128)(2,1)S(1)}, bf16[128,128]{1,0:T(8,128)(2,1)S(1)}, u32[]{:S(2)}, u32[]{:S(2)}) collective-permute-start(bf16[128,128]{1,0:T(8,128)(2,1)S(1)} %get-tuple-element.61), channel_id=1, source_target_pairs={{0,2},{1,3},{2,0},{3,1},{4,6},{5,7},{6,4},{7,5},{8,10},{9,11},{10,... | collective-permute-start | bytes 98312 | tf_op jit(solution)/shard_map/ppermute | solution.py:358
  76.9 1.0 %copy-start.12 = (f32[640,128]{1,0:T(8,128)S(1)}, f32[640,128]{1,0:T(8,128)}, u32[]{:S(2)}) copy-start(f32[640,128]{1,0:T(8,128)} %copy-done.11) | copy-start | bytes 983044
  77.9 0.9 %copy-start.17 = (f32[512,128]{1,0:T(8,128)S(1)}, f32[512,128]{1,0:T(8,128)}, u32[]{:S(2)}) copy-start(f32[512,128]{1,0:T(8,128)} %copy-done.16) | copy-start | bytes 786436

commit v3 on v2

v3 whole, which is shorter than its diff:
```python
import functools

import jax
import jax.numpy as jnp
from jax import lax
from jax.experimental import pallas as pl
from jax.experimental.pallas import tpu as pltpu
from jax.sharding import PartitionSpec as P

ITERS = 3


STEP_SIZES = (0.8, 0.9, 1.0)
MOMENTUM = (0.0, 0.3, 0.3)

F32 = jnp.float32
BF16 = jnp.bfloat16


def mm(a, b):
    return jnp.dot(a, b, preferred_element_type=F32)


def tn(a, b):
    return lax.dot_general(a, b, (((0,), (0,)), ((), ())), preferred_element_type=F32)


def nt(a, b):
    return lax.dot_general(a, b, (((1,), (1,)), ((), ())), preferred_element_type=F32)


def run(kernel, name, outs, args, scalars=(), scratch=(), flops=1 << 22):
    nbytes = sum(x.size * x.dtype.itemsize for x in map(bare, [*args, *outs]))
    return pl.pallas_call(
        kernel,
        name=name,
        out_shape=[held(x) for x in outs],
        in_specs=[pl.BlockSpec(memory_space=pltpu.SMEM)] * len(scalars) + [spec(x) for x in args],
        out_specs=[spec(x) for x in outs],
        scratch_shapes=list(scratch),
        compiler_params=pltpu.CompilerParams(vmem_limit_bytes=24 << 20),
        cost_estimate=pl.CostEstimate(flops=flops, bytes_accessed=nbytes, transcendentals=0),
    )(
        *scalars,
        *map(given, args),
    )


class Far:
    def __init__(self, array):
        self.array = array


def bare(x):
    return x.array if isinstance(x, Far) else x


def held(x):
    return pltpu.HBM(x.array.shape, x.array.dtype) if isinstance(x, Far) else x


def given(x):
    return pltpu.with_memory_space_constraint(x.array, pltpu.HBM) if isinstance(x, Far) else x


def spec(x):
    return pl.BlockSpec(memory_space=pltpu.HBM if isinstance(x, Far) else pltpu.VMEM)


def shape(*dims, dtype=F32):
    return jax.ShapeDtypeStruct(dims, dtype)


class Sizes:
    def __init__(self, right_side, deflation, coarse_inverse):
        self.owned, self.loads = right_side.shape[-2:]
        self.order, self.modes = deflation.shape[-2:]
        self.blk = (self.order - self.owned) // 2
        self.subs = lax.axis_size("sub")
        self.groups = lax.axis_size("grp")
        self.near = min(self.subs, 5)
        self.chunks = coarse_inverse.shape[1] // self.loads
        self.window = self.near * self.modes
        self.wide = self.window * self.chunks

    def base(self, position):
        return jnp.clip(position - 2, 0, self.subs - self.near)


class Place:
    def __init__(self, z, margin, live):
        self.z = z
        self.position = lax.axis_index("sub")
        self.give_right = pl.multiple_of(margin[0, 0] * z.blk, z.blk) if margin is not None else None
        self.give_left = pl.multiple_of(margin[0, 1] * z.blk, z.blk) if margin is not None else None
        self.live = live[0, 0]
        self.has_left = self.position > 0
        self.has_right = self.position < z.subs - 1
        self.has_left2 = self.position > 1
        self.has_right2 = self.position < z.subs - 2

    def row_mask(self):
        z = self.z
        rows = lax.broadcasted_iota(jnp.int32, (z.owned, z.loads), 0)
        return rows < self.live

    def kept(self, value):
        z = self.z
        low = value[z.owned : z.owned + z.blk]
        high = value[z.owned + z.blk :]
        return jnp.concatenate(
            [
                jnp.where(self.row_mask(), value[: z.owned], 0.0),
                jnp.where(self.has_left, low, 0.0),
                jnp.where(self.has_right, high, 0.0),
            ],
            axis=0,
        )

    def right_block(self, ref):
        return ref[pl.ds(self.give_right, self.z.blk), :]

    def left_block(self, ref):
        return ref[pl.ds(self.give_left, self.z.blk), :]

    def ahead(self, ref):
        z = self.z
        return jnp.concatenate([ref[z.owned + z.blk :, :], self.right_block(ref)], axis=0)

    def behind(self, ref):
        z = self.z
        return jnp.concatenate([ref[z.owned : z.owned + z.blk, :], self.left_block(ref)], axis=0)


def selection(z, block, rim):
    row = lax.broadcasted_iota(jnp.int32, (z.order, 2 * z.blk), 0)
    col = lax.broadcasted_iota(jnp.int32, (z.order, 2 * z.blk), 1)
    return (row == jnp.where(col < z.blk, block + col, rim - z.blk + col)).astype(BF16)


def swapped(z, block, rim):
    row = lax.broadcasted_iota(jnp.int32, (z.order, 2 * z.blk), 0)
    col = lax.broadcasted_iota(jnp.int32, (z.order, 2 * z.blk), 1)
    return (row == jnp.where(col < z.blk, rim + col, block - z.blk + col)).astype(BF16)


def first_kernel(z, live, source_far, vectors_far, panel_far, margin_far, slots, own, *scratch):
    source, vectors_t, panel, margin, sem = scratch
    loads = [
        pltpu.make_async_copy(far, near, sem.at[k])
        for k, (far, near) in enumerate(
            (
                (margin_far, margin),
                (vectors_far, vectors_t),
                (panel_far, panel),
                (source_far, source),
            )
        )
    ]
    for load in loads:
        load.start()
    loads[0].wait()
    at = Place(z, margin, live)
    right_rows = swapped(z, at.give_right, z.owned + z.blk)
    left_rows = swapped(z, at.give_left, z.owned)
    loads[1].wait()
    ahead_vectors = mm(vectors_t[...], right_rows).astype(BF16)
    behind_vectors = mm(vectors_t[...], left_rows).astype(BF16)
    loads[2].wait()
    loads[3].wait()
    own[...] = jnp.where(at.row_mask(), source[...], 0.0)
    ahead = jnp.concatenate([ahead_vectors, at.right_block(own).astype(BF16)], axis=0)
    behind = jnp.concatenate([behind_vectors, at.left_block(own).astype(BF16)], axis=0)
    for k in range(z.subs):
        first = min(max(k - 2, 0), z.subs - z.near) * z.modes
        for chunk in range(z.chunks):
            slots[k, chunk * z.window : (chunk + 1) * z.window, :] = panel[
                chunk, first : first + z.window, :
            ]
        slots[k, z.wide :, :] = jnp.where(k > at.position, ahead, behind)


def static_kernel(z, live, operator, vectors_t, margin_in, ahead, behind, margin, sem):
    load = pltpu.make_async_copy(margin_in, margin, sem)
    load.start()
    load.wait()
    at = Place(z, margin, live)
    side = 2 * z.blk
    rows = jnp.concatenate([at.ahead(operator), at.behind(operator)], axis=0)
    left_cols = mm(rows, selection(z, at.give_left, z.owned)).astype(BF16)
    right_cols = mm(rows, selection(z, at.give_right, z.owned + z.blk)).astype(BF16)
    col = lax.broadcasted_iota(jnp.int32, (z.modes, z.order), 1)
    limit = jnp.where(at.has_left, z.owned + z.blk, z.owned)
    kept = (col < at.live) | ((col >= z.owned) & (col < limit))
    kept = kept | ((col >= z.owned + z.blk) & at.has_right)
    lifted = nt(jnp.where(kept, vectors_t[...].astype(F32), 0.0).astype(BF16), rows).astype(BF16)
    ahead[...] = jnp.concatenate([left_cols[:side], right_cols[:side], lifted[:, :side]], axis=0)
    behind[...] = jnp.concatenate([right_cols[side:], left_cols[side:], lifted[:, side:]], axis=0)


def send_coarse(z, vectors_t, low, copies, every_out, sem):
    value = mm(vectors_t[...], low).astype(BF16)

    def put(k, carry):
        copies[k] = value
        return carry

    lax.fori_loop(0, z.subs * z.groups, put, 0, unroll=8)
    copy = pltpu.make_async_copy(copies, every_out, sem)
    copy.start()
    return copy


def lookahead(at, momentum, low, inverse, operator, part, ahead, behind, far):
    z = at.z
    side = 2 * z.blk
    part_value = mm(inverse[...], low)
    part[...] = part_value
    to_right = at.ahead(part).astype(BF16)
    to_left = at.behind(part).astype(BF16)
    value = at.kept(part_value)
    if momentum is not None:
        value = value + momentum
    part[...] = value
    rows = jnp.concatenate([at.ahead(operator), at.behind(operator)], axis=0)
    product = mm(rows, value.astype(BF16)).astype(BF16)
    ahead[:side, :] = to_right
    ahead[side : 2 * side, :] = product[:side]
    behind[:side, :] = to_left
    behind[side : 2 * side, :] = product[side:]
    if far:
        far[0][...] = jnp.where(at.has_right2, to_right, to_left)


def second_kernel(z, live, slots, own, vectors_t, inverse_far, operator, margin_in, *rest):
    ahead_static, behind_static, resid, every_out, part, ahead, behind, *rest = rest
    far, (inverse, copies, margin, sem) = rest[:-4], rest[-4:]
    load = pltpu.make_async_copy(inverse_far, inverse, sem.at[0])
    load.start()
    load_margin = pltpu.make_async_copy(margin_in, margin, sem.at[2])
    load_margin.start()
    at = Place(z, None, live)
    left = slots[jnp.maximum(at.position - 1, 0), z.wide + z.modes :, :]
    right = slots[jnp.minimum(at.position + 1, z.subs - 1), z.wide + z.modes :, :]
    value = jnp.concatenate(
        [
            own[...],
            jnp.where(at.has_left, left.astype(F32), 0.0),
            jnp.where(at.has_right, right.astype(F32), 0.0),
        ],
        axis=0,
    )
    resid[...] = value
    low = value.astype(BF16)
    store = send_coarse(z, vectors_t, low, copies, every_out, sem.at[1])
    load_margin.wait()
    at = Place(z, margin, live)
    load.wait()
    lookahead(at, None, low, inverse, operator, part, ahead, behind, far)
    ahead[4 * z.blk :, :] = ahead_static[...]
    behind[4 * z.blk :, :] = behind_static[...]
    store.wait()


def main_kernel(z, turn, *refs):
    last = turn == ITERS - 1
    live, every, slots, vectors_t, operator, margin_in, part_in, *rest = refs
    ahead_in, behind_in, left, right, far_left, far_right, *rest = rest
    left_static, right_static, resid_in, *rest = rest
    if turn:
        solution_far, *rest = rest
    if last:
        solution_out, resid_out, direction, resid, solution, error, coarse, margin, sem = rest
    else:
        inverse_far, *rest = rest
        solution_out, resid, every_out, part, ahead, behind, *rest = rest
        far = rest[:-8]
        direction, solution, error, coarse, inverse, copies, margin, sem = rest[-8:]
        load = pltpu.make_async_copy(inverse_far, inverse, sem.at[2])
        load.start()
    if turn:
        load_solution = pltpu.make_async_copy(solution_far, solution, sem.at[0])
        load_solution.start()
    load_margin = pltpu.make_async_copy(margin_in, margin, sem.at[4])
    load_margin.start()
    at = Place(z, None, live)
    owned, blk, side, modes = z.owned, z.blk, 2 * z.blk, z.modes
    cols = slice(None)

    total = jnp.zeros((z.window, z.loads), F32)
    for k in range(z.subs):
        for chunk in range(z.chunks):
            total = total + mm(
                slots[k, chunk * z.window : (chunk + 1) * z.window, :],
                every[k, chunk * z.loads : (chunk + 1) * z.loads, :],
            )
    coarse[...] = total.astype(BF16)

    def correction(offset):
        index = jnp.clip(at.position + offset - z.base(at.position), 0, z.near - 1)
        return coarse[pl.ds(pl.multiple_of(index * modes, modes), modes), :]

    def their_vectors(offset):
        index = jnp.clip(at.position + offset, 0, z.subs - 1)
        return slots[index, z.wide : z.wide + modes, :]

    def halo(have, piece, offset):
        value = piece.astype(F32) + tn(their_vectors(offset), correction(offset))
        return jnp.where(have, value, 0.0)

    lifted = tn(vectors_t[...], correction(0))
    error[...] = lifted
    from_left = halo(at.has_left, left[:side, cols], -1)
    from_right = halo(at.has_right, right[:side, cols], 1)
    from_left2 = halo(at.has_left2, far_left[:side, cols], -2)
    from_right2 = halo(at.has_right2, far_right[:side, cols], 2)
    load_margin.wait()
    at = Place(z, margin, live)
    to_right = (ahead_in[:side, cols].astype(F32) + at.ahead(error)).astype(BF16)
    to_left = (behind_in[:side, cols].astype(F32) + at.behind(error)).astype(BF16)

    def join(target, before, scale, rows, from_left, from_right):
        def scaled(value):
            return value if scale == 1.0 else scale * value

        low = jnp.where(at.has_left, scaled(from_left[blk:]), 0.0)
        high = jnp.where(at.has_right, scaled(from_right[blk:]), 0.0)
        target[...] = before + scaled(at.kept(rows))
        for spot, value in (
            (slice(owned, owned + blk), low),
            (slice(owned + blk, owned + side), high),
            (pl.ds(at.give_left, blk), scaled(from_left[:blk])),
            (pl.ds(at.give_right, blk), scaled(from_right[:blk])),
        ):
            target[spot, :] = target[spot, :] + value

    join(direction, part_in[...], 1.0, lifted, from_left, from_right)
    step = STEP_SIZES[turn] * direction[:owned, :]
    if turn:
        load_solution.wait()
        step = solution[...] + step
    solution[...] = step
    store_solution = pltpu.make_async_copy(solution, solution_out, sem.at[1])
    store_solution.start()

    def borrowed(have, piece, statics, far, near, offset):
        value = (
            piece[side : 2 * side, cols].astype(F32)
            + mm(statics[2 * side : 3 * side, cols], far.astype(BF16))
            + mm(statics[3 * side : 4 * side, cols], near)
            + tn(statics[4 * side :, cols], correction(offset))
        )
        return jnp.where(have, value, 0.0)

    from_left = borrowed(at.has_left, left, left_static, from_left2, to_left, -1)
    from_right = borrowed(at.has_right, right, right_static, from_right2, to_right, 1)
    applied = mm(operator[...], direction[...].astype(BF16))
    join(resid, resid_in[...], -STEP_SIZES[turn], applied, from_left, from_right)
    if last:
        store = pltpu.make_async_copy(resid.at[pl.ds(0, owned), :], resid_out, sem.at[0])
        store.start()
        store.wait()
    else:
        low = resid[...].astype(BF16)
        store = send_coarse(z, vectors_t, low, copies, every_out, sem.at[3])
        load.wait()
        momentum = MOMENTUM[turn + 1] * direction[...]
        lookahead(at, momentum, low, inverse, operator, part, ahead, behind, far)
        store.wait()
    store_solution.wait()


def body(
    right_side, live_rows, margin_blocks, local_operator, local_inverse, deflation, coarse_inverse
):
    z = Sizes(right_side, deflation, coarse_inverse)
    source = right_side[0, 0]
    operator = local_operator[0, 0]
    inverse = Far(local_inverse[0, 0])
    scalars = (live_rows,)
    margin = margin_blocks.reshape(1, -1)
    vectors_t = deflation[0, 0].T
    pick = pltpu.SMEM(margin.shape, jnp.int32)
    sems = pltpu.SemaphoreType.DMA
    owned, order, loads, modes = z.owned, z.order, z.loads, z.modes
    side = 2 * z.blk
    devices = z.subs * z.groups
    folded = z.subs == 4

    def ring(offset):
        return [(i, (i + offset) % z.subs) for i in range(z.subs)]

    def part(function, *more):
        return functools.partial(function, z, *more)

    panel = coarse_inverse.reshape(-1, z.chunks, loads).swapaxes(0, 1)
    slots, own = run(
        part(first_kernel),
        "first",
        [shape(z.subs, z.wide + modes + z.blk, loads, dtype=BF16), shape(owned, loads)],
        [Far(source), Far(vectors_t), Far(panel), Far(margin)],
        scalars,
        [
            pltpu.VMEM(source.shape, F32),
            pltpu.VMEM(vectors_t.shape, BF16),
            pltpu.VMEM(panel.shape, BF16),
            pick,
            sems((4,)),
        ],
    )
    slots = lax.all_to_all(slots, "sub", 0, 0, tiled=True)
    ahead_static, behind_static = run(
        part(static_kernel),
        "static",
        [shape(2 * side + modes, loads, dtype=BF16)] * 2,
        [operator, vectors_t, margin],
        scalars,
        [pick, sems(())],
    )
    full = shape(order, loads)
    next_outs = [full, Far(shape(devices, modes, loads, dtype=BF16)), full]
    next_outs += [shape(2 * side, loads, dtype=BF16)] * 2 + [shape(side, loads, dtype=BF16)] * folded
    next_work = [
        pltpu.VMEM((order, order), BF16),
        pltpu.VMEM((devices, modes, loads), BF16),
        pick,
        sems((5,)),
    ]
    resid, every, error, ahead, behind, *far = run(
        part(second_kernel),
        "second",
        next_outs[:3] + [shape(4 * side + modes, loads, dtype=BF16)] * 2 + next_outs[5:],
        [slots, own, vectors_t, inverse, operator, margin, ahead_static, behind_static],
        scalars,
        next_work,
    )
    solution = statics = None
    for turn in range(ITERS):
        last = turn == ITERS - 1
        every = lax.all_to_all(every, ("sub", "grp"), 0, 0, tiled=True)
        every = every.reshape(z.subs, z.groups * modes, loads)
        left = lax.ppermute(ahead, "sub", ring(1))
        right = lax.ppermute(behind, "sub", ring(-1))
        if folded:
            far_left = far_right = lax.ppermute(far[0], "sub", ring(2))
        else:
            far_left = lax.ppermute(ahead[:side], "sub", ring(2))
            far_right = lax.ppermute(behind[:side], "sub", ring(-2))
        if not turn:
            statics = (left, right)
        args = [every, slots, vectors_t, operator, margin, error, ahead, behind]
        args += [left, right, far_left, far_right, *statics, resid]
        if turn:
            args += [Far(solution)]
        work = [
            pltpu.VMEM((owned, loads), F32),
            pltpu.VMEM((order, loads), F32),
            pltpu.VMEM((z.window, loads), BF16),
        ]
        if last:
            solution, resid = run(
                part(main_kernel, turn),
                f"main{turn}",
                [Far(shape(owned, loads))] * 2,
                args,
                scalars,
                [pltpu.VMEM((order, loads), F32)] * 2 + work + [pick, sems((5,))],
            )
        else:
            solution, resid, every, error, ahead, behind, *far = run(
                part(main_kernel, turn),
                f"main{turn}",
                [Far(shape(owned, loads))] + next_outs,
                args + [inverse],
                scalars,
                [pltpu.VMEM((order, loads), F32)] + work + next_work,
            )
    return (solution[None, None], resid[None, None])


def solution(mesh):
    return jax.shard_map(
        body,
        mesh=mesh,
        in_specs=(
            P("grp", "sub", None, None),
            P("grp", "sub"),
            P("grp", "sub", None),
            P("grp", "sub", None, None),
            P("grp", "sub", None, None),
            P("grp", "sub", None, None),
            P("grp", "sub"),
        ),
        out_specs=(P("grp", "sub", None, None), P("grp", "sub", None, None)),
        check_vma=False,
    )
```

time: 81.8 us -> 62.7 us (0.77)
  local copies, waits for them, and re-layouts: 19.3 us -> 1.81 us
  blocking collectives: 10.5 us -> 0 us
  waiting for transfers between devices: 9.86 us -> 15.1 us
  starting transfers between devices: 27.6 us -> 31.9 us
    unnamed x57 -> x8, local copies, waits for them, and re-layouts: 19.3 us -> 1.81 us
    all_to_all x1 -> x0, blocking collectives: 10.5 us -> none  [body(): slots = lax.all_to_all(slots, 'sub', 0, 0, tiled=True)]
    all_to_all x0 -> x1, starting transfers between devices: none -> 5.2 us  [body(): slots = lax.all_to_all(slots, 'sub', 0, 0, tiled=True)]
    all_to_all x0 -> x1, waiting for transfers between devices: none -> 2.33 us  [body(): slots = lax.all_to_all(slots, 'sub', 0, 0, tiled=True)]
    ppermute x3, waiting for transfers between devices: 2.37 us -> 3.52 us  [body(): right = lax.ppermute(behind, 'sub', ring(-1))]
    all_to_all x3, starting transfers between devices: 13.5 us -> 12.4 us  [body(): every = lax.all_to_all(every, ('sub', 'grp'), 0, 0, tiled=True)]
    ppermute x3, waiting for transfers between devices: 7.47 us -> 8.38 us  [body(): far_left = far_right = lax.ppermute(far[0], 'sub', ring(2))]
    all_to_all x3, waiting for transfers between devices: 0.01 us -> 0.87 us  [body(): every = lax.all_to_all(every, ('sub', 'grp'), 0, 0, tiled=True)]
  transfers between devices with their start and end apart: 12 -> 13, of which waited for: 5 -> 9; matrix products, arithmetic and copies ran while one was open for 0% -> 0% of each run, Pallas kernels for 6% -> 1%
where the time goes in v3:
time: 62.7 us; the launch traced here: 62.1 us
  starting transfers between devices  31.9 us (51%)
  waiting for transfers between devices  15.1 us (24%)
  Pallas kernels  11.9 us (19%)
  local copies, waits for them, and re-layouts  1.81 us (3%)
  between operations  1.36 us (2%)
    all_to_all x3, starting transfers between devices, body(): every = lax.all_to_all(every, ('sub', 'grp'), 0, 0, tiled=True)  12.4 us
    pallas_call x6, Pallas kernels, run(): pl.pallas_call(kernel, name=name, out_shape=[held(x) for x in outs], in_s...  11.9 us
    ppermute x3, waiting for transfers between devices, body(): far_left = far_right = lax.ppermute(far[0], 'sub', ring(2))  8.38 us
    ppermute x3, starting transfers between devices, body(): left = lax.ppermute(ahead, 'sub', ring(1))  5.46 us
    ppermute x3, starting transfers between devices, body(): far_left = far_right = lax.ppermute(far[0], 'sub', ring(2))  5.31 us
    all_to_all x1, starting transfers between devices, body(): slots = lax.all_to_all(slots, 'sub', 0, 0, tiled=True)  5.2 us
    ppermute x3, waiting for transfers between devices, body(): right = lax.ppermute(behind, 'sub', ring(-1))  3.52 us
    ppermute x3, starting transfers between devices, body(): right = lax.ppermute(behind, 'sub', ring(-1))  3.47 us
  transfers between devices with their start and end apart: 13, of which 9 were waited for; matrix products, arithmetic and copies ran while one was open for 0% of the time, Pallas kernels for 1%

profile of v3, /device:TPU:0, one launch (start us, length us, event | category | flops | bytes accessed | tf_op | source)
XLA Modules:
  0.0 62.1 jit_solution(7574018078666540660)
XLA Ops:
  1.3 1.7 %first.1 = (bf16[4,144,128]{2,1,0:T(8,128)(2,1)}, f32[512,128]{1,0:T(8,128)S(1)}) custom-call(s32[1,1]{1,0:T(1,128)S(6)} %copy.9.live.refs_0_, f32[512,128]{1,0:T(8,128)} %bitcast.36, bf16[16,640]{1,0:T(8,128)(2,1)} %bitcast.18, bf16[1,64,128]{2,1,0:T(8,128)(2,1)} %bitcast.37, s32[1,2]{1,0:T(1,128)} %bitcast.27), custom_call_target="tpu_custom_call" | custom-call | flops 4194304 | bytes 708616 | tf_op jit(solution)/shard_map/first/pallas_call | solution.py:34
  3.0 0.0 copy-start.2
  3.0 5.2 %all-to-all-start = ((bf16[4,144,128]{2,1,0:T(8,128)(2,1)}), bf16[4,144,128]{2,1,0:T(8,128)(2,1)S(1)}, u32[]{:S(2)}, u32[]{:S(2)}) async-start(bf16[4,144,128]{2,1,0:T(8,128)(2,1)} %get-tuple-element.28), calls=%async_computation | async-start | bytes 294912 | tf_op jit(solution)/shard_map/all_to_all | solution.py:411
  8.2 0.0 copy-start.3
  8.2 0.0 copy-done.2
  8.2 0.7 %copy-done.3 = s32[1,1,2]{2,1,0:T(1,128)S(1)} copy-done((s32[1,1,2]{2,1,0:T(1,128)S(1)}, s32[1,1,2]{2,1,0:T(1,128)}, u32[]{:S(2)}) %copy-start.3) | copy-done | bytes 32
  8.9 0.0 copy-start
  8.9 1.1 %copy-done = bf16[1,1,640,640]{3,2,1,0:T(8,128)(2,1)S(1)} copy-done((bf16[1,1,640,640]{3,2,1,0:T(8,128)(2,1)S(1)}, bf16[1,1,640,640]{3,2,1,0:T(8,128)(2,1)}, u32[]{:S(2)}) %copy-start) | copy-done | bytes 819224
  10.0 0.0 copy-start.1
  10.0 0.9 %static.1 = (bf16[272,128]{1,0:T(8,128)(2,1)S(1)}, bf16[272,128]{1,0:T(8,128)(2,1)S(1)}) custom-call(s32[1,1]{1,0:T(1,128)S(6)} %copy.9.live.refs_0_, bf16[640,640]{1,0:T(8,128)(2,1)S(1)} %bitcast.13, bf16[16,640]{1,0:T(8,128)(2,1)S(1)} %bitcast.19, s32[1,2]{1,0:T(1,128)S(1)} %bitcast.28), custom_call_target="tpu_custom_call" | custom-call | flops 4194304 | bytes 978952 | tf_op jit(solution)/shard_map/static/pallas_call | solution.py:34
  11.0 2.3 %all-to-all-done.slots.refs_2_ = bf16[4,144,128]{2,1,0:T(8,128)(2,1)S(1)} async-done(((bf16[4,144,128]{2,1,0:T(8,128)(2,1)}), bf16[4,144,128]{2,1,0:T(8,128)(2,1)S(1)}, u32[]{:S(2)}, u32[]{:S(2)}) %all-to-all-start) | async-done | bytes 147488 | tf_op jit(solution)/shard_map/all_to_all | solution.py:411
  13.3 0.0 copy-done.1
  13.3 1.9 %second.1 = (f32[640,128]{1,0:T(8,128)S(1)}, bf16[32,16,128]{2,1,0:T(8,128)(2,1)}, f32[640,128]{1,0:T(8,128)S(1)}, bf16[528,128]{1,0:T(8,128)(2,1)S(1)}, bf16[52...) custom-call(s32[1,1]{1,0:T(1,128)S(6)} %copy.9.live.refs_0_, bf16[4,144,128]{2,1,0:T(8,128)(2,1)S(1)} %all-to-all-done.slots.refs_2_, ...), custom_call_target="tpu_custom_call" | custom-call | flops 4194304 | bytes 3297288 | tf_op jit(solution)/shard_map/second/pallas_call | solution.py:34
  15.2 4.4 %all-to-all-start.1 = ((bf16[32,16,128]{2,1,0:T(8,128)(2,1)}), bf16[32,16,128]{2,1,0:T(8,128)(2,1)S(1)}, u32[]{:S(2)}, u32[]{:S(2)}) async-start(bf16[32,16,128]{2,1,0:T(8,128)(2,1)} %get-tuple-element.32), calls=%async_computation.1 | async-start | bytes 262144 | tf_op jit(solution)/shard_map/all_to_all | solution.py:440
  19.6 1.8 %collective-permute-start = (bf16[528,128]{1,0:T(8,128)(2,1)S(1)}, bf16[528,128]{1,0:T(8,128)(2,1)S(1)}, u32[]{:S(2)}, u32[]{:S(2)}) collective-permute-start(bf16[528,128]{1,0:T(8,128)(2,1)S(1)} %get-tuple-element.34.refs_7_), channel_id=1, source_target_pairs={{0,1},{1,2},{2,3},{3,0},{4,5},{5,6},{6,7},{7,4},{8,9},{9,10},{10,1... | collective-permute-start | bytes 405512 | tf_op jit(solution)/shard_map/ppermute | solution.py:442
  21.4 1.2 %collective-permute-start.1 = (bf16[528,128]{1,0:T(8,128)(2,1)S(1)}, bf16[528,128]{1,0:T(8,128)(2,1)S(1)}, u32[]{:S(2)}, u32[]{:S(2)}) collective-permute-start(bf16[528,128]{1,0:T(8,128)(2,1)S(1)} %get-tuple-element.35.refs_8_), channel_id=1, source_target_pairs={{0,3},{1,0},{2,1},{3,2},{4,7},{5,4},{6,5},{7,6},{8,11},{9,8},{10,9... | collective-permute-start | bytes 405512 | tf_op jit(solution)/shard_map/ppermute | solution.py:443
  22.6 1.8 %collective-permute-start.2 = (bf16[128,128]{1,0:T(8,128)(2,1)S(1)}, bf16[128,128]{1,0:T(8,128)(2,1)S(1)}, u32[]{:S(2)}, u32[]{:S(2)}) collective-permute-start(bf16[128,128]{1,0:T(8,128)(2,1)S(1)} %get-tuple-element.36), channel_id=1, source_target_pairs={{0,2},{1,3},{2,0},{3,1},{4,6},{5,7},{6,4},{7,5},{8,10},{9,11},{10,... | collective-permute-start | bytes 98312 | tf_op jit(solution)/shard_map/ppermute | solution.py:445
  24.4 3.8 %collective-permute-done.2.refs_11_.refs_12_ = bf16[128,128]{1,0:T(8,128)(2,1)S(1)} collective-permute-done((bf16[128,128]{1,0:T(8,128)(2,1)S(1)}, bf16[128,128]{1,0:T(8,128)(2,1)S(1)}, u32[]{:S(2)}, u32[]{:S(2)}) %collective-permute-start.2) | collective-permute-done | bytes 32800 | tf_op jit(solution)/shard_map/ppermute | solution.py:445
  28.2 0.0 collective-permute-done.refs_9_.refs_13_
  28.2 2.1 %collective-permute-done.1.refs_10_.refs_14_ = bf16[528,128]{1,0:T(8,128)(2,1)S(1)} collective-permute-done((bf16[528,128]{1,0:T(8,128)(2,1)S(1)}, bf16[528,128]{1,0:T(8,128)(2,1)S(1)}, u32[]{:S(2)}, u32[]{:S(2)}) %collective-permute-start.1) | collective-permute-done | bytes 135200 | tf_op jit(solution)/shard_map/ppermute | solution.py:443
  30.3 0.0 all-to-all-done.1
  30.3 2.1 %main0.1 = (f32[512,128]{1,0:T(8,128)}, f32[640,128]{1,0:T(8,128)S(1)}, bf16[32,16,128]{2,1,0:T(8,128)(2,1)}, f32[640,128]{1,0:T(8,128)S(1)}, bf16[256,128]{1,0:...) custom-call(s32[1,1]{1,0:T(1,128)S(6)} %copy.9.live.refs_0_, ...), custom_call_target="tpu_custom_call" | custom-call | flops 4194304 | bytes 4681736 | tf_op jit(solution)/shard_map/main0/pallas_call | solution.py:34
  32.4 4.1 %all-to-all-start.2 = ((bf16[32,16,128]{2,1,0:T(8,128)(2,1)}), bf16[32,16,128]{2,1,0:T(8,128)(2,1)S(1)}, u32[]{:S(2)}, u32[]{:S(2)}) async-start(bf16[32,16,128]{2,1,0:T(8,128)(2,1)} %get-tuple-element.38), calls=%async_computation.2 | async-start | bytes 262144 | tf_op jit(solution)/shard_map/all_to_all | solution.py:440
  36.5 1.8 %collective-permute-start.3 = (bf16[256,128]{1,0:T(8,128)(2,1)S(1)}, bf16[256,128]{1,0:T(8,128)(2,1)S(1)}, u32[]{:S(2)}, u32[]{:S(2)}) collective-permute-start(bf16[256,128]{1,0:T(8,128)(2,1)S(1)} %get-tuple-element.40.refs_7_), channel_id=1, source_target_pairs={{0,1},{1,2},{2,3},{3,0},{4,5},{5,6},{6,7},{7,4},{8,9},{9,10},{10,1... | collective-permute-start | bytes 196616 | tf_op jit(solution)/shard_map/ppermute | solution.py:442
  38.3 1.2 %collective-permute-start.4 = (bf16[256,128]{1,0:T(8,128)(2,1)S(1)}, bf16[256,128]{1,0:T(8,128)(2,1)S(1)}, u32[]{:S(2)}, u32[]{:S(2)}) collective-permute-start(bf16[256,128]{1,0:T(8,128)(2,1)S(1)} %get-tuple-element.41.refs_8_), channel_id=1, source_target_pairs={{0,3},{1,0},{2,1},{3,2},{4,7},{5,4},{6,5},{7,6},{8,11},{9,8},{10,9... | collective-permute-start | bytes 196616 | tf_op jit(solution)/shard_map/ppermute | solution.py:443
  39.5 1.8 %collective-permute-start.5 = (bf16[128,128]{1,0:T(8,128)(2,1)S(1)}, bf16[128,128]{1,0:T(8,128)(2,1)S(1)}, u32[]{:S(2)}, u32[]{:S(2)}) collective-permute-start(bf16[128,128]{1,0:T(8,128)(2,1)S(1)} %get-tuple-element.42), channel_id=1, source_target_pairs={{0,2},{1,3},{2,0},{3,1},{4,6},{5,7},{6,4},{7,5},{8,10},{9,11},{10,... | collective-permute-start | bytes 98312 | tf_op jit(solution)/shard_map/ppermute | solution.py:445
  41.3 2.3 %collective-permute-done.5.refs_11_.refs_12_ = bf16[128,128]{1,0:T(8,128)(2,1)S(1)} collective-permute-done((bf16[128,128]{1,0:T(8,128)(2,1)S(1)}, bf16[128,128]{1,0:T(8,128)(2,1)S(1)}, u32[]{:S(2)}, u32[]{:S(2)}) %collective-permute-start.5) | collective-permute-done | bytes 32800 | tf_op jit(solution)/shard_map/ppermute | solution.py:445
  43.6 0.0 collective-permute-done.3.refs_9_
  43.6 0.7 %collective-permute-done.4.refs_10_ = bf16[256,128]{1,0:T(8,128)(2,1)S(1)} collective-permute-done((bf16[256,128]{1,0:T(8,128)(2,1)S(1)}, bf16[256,128]{1,0:T(8,128)(2,1)S(1)}, u32[]{:S(2)}, u32[]{:S(2)}) %collective-permute-start.4) | collective-permute-done | bytes 65568 | tf_op jit(solution)/shard_map/ppermute | solution.py:443
  44.2 0.4 all-to-all-done.2
  44.7 2.7 %main1.1 = (f32[512,128]{1,0:T(8,128)}, f32[640,128]{1,0:T(8,128)S(1)}, bf16[32,16,128]{2,1,0:T(8,128)(2,1)}, f32[640,128]{1,0:T(8,128)S(1)}, bf16[256,128]{1,0:...) custom-call(s32[1,1]{1,0:T(1,128)S(6)} %copy.9.live.refs_0_, ...), custom_call_target="tpu_custom_call" | custom-call | flops 4194304 | bytes 4665352 | tf_op jit(solution)/shard_map/main1/pallas_call | solution.py:34
  47.4 4.0 %all-to-all-start.3 = ((bf16[32,16,128]{2,1,0:T(8,128)(2,1)}), bf16[32,16,128]{2,1,0:T(8,128)(2,1)S(1)}, u32[]{:S(2)}, u32[]{:S(2)}) async-start(bf16[32,16,128]{2,1,0:T(8,128)(2,1)} %get-tuple-element.45), calls=%async_computation.3 | async-start | bytes 262144 | tf_op jit(solution)/shard_map/all_to_all | solution.py:440
  51.4 1.8 %collective-permute-start.6 = (bf16[256,128]{1,0:T(8,128)(2,1)S(1)}, bf16[256,128]{1,0:T(8,128)(2,1)S(1)}, u32[]{:S(2)}, u32[]{:S(2)}) collective-permute-start(bf16[256,128]{1,0:T(8,128)(2,1)S(1)} %get-tuple-element.47.refs_7_), channel_id=1, source_target_pairs={{0,1},{1,2},{2,3},{3,0},{4,5},{5,6},{6,7},{7,4},{8,9},{9,10},{10,1... | collective-permute-start | bytes 196616 | tf_op jit(solution)/shard_map/ppermute | solution.py:442
  53.2 1.2 %collective-permute-start.7 = (bf16[256,128]{1,0:T(8,128)(2,1)S(1)}, bf16[256,128]{1,0:T(8,128)(2,1)S(1)}, u32[]{:S(2)}, u32[]{:S(2)}) collective-permute-start(bf16[256,128]{1,0:T(8,128)(2,1)S(1)} %get-tuple-element.48.refs_8_), channel_id=1, source_target_pairs={{0,3},{1,0},{2,1},{3,2},{4,7},{5,4},{6,5},{7,6},{8,11},{9,8},{10,9... | collective-permute-start | bytes 196616 | tf_op jit(solution)/shard_map/ppermute | solution.py:443
  54.3 1.8 %collective-permute-start.8 = (bf16[128,128]{1,0:T(8,128)(2,1)S(1)}, bf16[128,128]{1,0:T(8,128)(2,1)S(1)}, u32[]{:S(2)}, u32[]{:S(2)}) collective-permute-start(bf16[128,128]{1,0:T(8,128)(2,1)S(1)} %get-tuple-element.49), channel_id=1, source_target_pairs={{0,2},{1,3},{2,0},{3,1},{4,6},{5,7},{6,4},{7,5},{8,10},{9,11},{10,... | collective-permute-start | bytes 98312 | tf_op jit(solution)/shard_map/ppermute | solution.py:445
  56.1 2.3 %collective-permute-done.8.refs_11_.refs_12_ = bf16[128,128]{1,0:T(8,128)(2,1)S(1)} collective-permute-done((bf16[128,128]{1,0:T(8,128)(2,1)S(1)}, bf16[128,128]{1,0:T(8,128)(2,1)S(1)}, u32[]{:S(2)}, u32[]{:S(2)}) %collective-permute-start.8) | collective-permute-done | bytes 32800 | tf_op jit(solution)/shard_map/ppermute | solution.py:445
  58.4 0.0 collective-permute-done.6.refs_9_
  58.4 0.7 %collective-permute-done.7.refs_10_ = bf16[256,128]{1,0:T(8,128)(2,1)S(1)} collective-permute-done((bf16[256,128]{1,0:T(8,128)(2,1)S(1)}, bf16[256,128]{1,0:T(8,128)(2,1)S(1)}, u32[]{:S(2)}, u32[]{:S(2)}) %collective-permute-start.7) | collective-permute-done | bytes 65568 | tf_op jit(solution)/shard_map/ppermute | solution.py:443
  59.1 0.4 all-to-all-done.3
  59.5 2.6 %main2.1 = (f32[512,128]{1,0:T(8,128)}, f32[512,128]{1,0:T(8,128)}) custom-call(s32[1,1]{1,0:T(1,128)S(6)} %copy.9.live.refs_0_, bf16[4,128,128]{2,1,0:T(8,128)(2,1)S(1)} %bitcast.26, bf16[4,144,128]{2,1,0:T(8,128)(2,1)S(1)} %all-to-all-done.slots.refs_2_, bf16[16,640]{1,0:T(8,128)(2,1)S(1)} %bitcast.23, bf16[640,640]{1,0:T(8,128)(2,1)S(1)} %bitcast.17, ...), custom_call_target="tpu_custom_call" | custom-call | flops 4194304 | bytes 3158024 | tf_op jit(solution)/shard_map/main2/pallas_call | solution.py:34
Async XLA Ops:
  3.0 5.2 %copy-start.2 = (bf16[1,1,640,16]{2,3,1,0:T(8,128)(2,1)S(1)}, bf16[1,1,640,16]{2,3,1,0:T(8,128)(2,1)}, u32[]{:S(2)}) copy-start(bf16[1,1,640,16]{2,3,1,0:T(8,128)(2,1)} %param.12) | copy-start | bytes 61444
  3.0 10.3 %all-to-all-start = ((bf16[4,144,128]{2,1,0:T(8,128)(2,1)}), bf16[4,144,128]{2,1,0:T(8,128)(2,1)S(1)}, u32[]{:S(2)}, u32[]{:S(2)}) async-start(bf16[4,144,128]{2,1,0:T(8,128)(2,1)} %get-tuple-element.28), calls=%async_computation | async-start | bytes 294912 | tf_op jit(solution)/shard_map/all_to_all | solution.py:411
  8.2 0.7 %copy-start.3 = (s32[1,1,2]{2,1,0:T(1,128)S(1)}, s32[1,1,2]{2,1,0:T(1,128)}, u32[]{:S(2)}) copy-start(s32[1,1,2]{2,1,0:T(1,128)} %param.9) | copy-start | bytes 28
  8.9 1.1 %copy-start = (bf16[1,1,640,640]{3,2,1,0:T(8,128)(2,1)S(1)}, bf16[1,1,640,640]{3,2,1,0:T(8,128)(2,1)}, u32[]{:S(2)}) copy-start(bf16[1,1,640,640]{3,2,1,0:T(8,128)(2,1)} %param.10) | copy-start | bytes 2457604
  10.0 3.3 %copy-start.1 = (bf16[1,1,640,640]{3,2,1,0:T(8,128)(2,1)S(1)}, bf16[1,1,640,640]{3,2,1,0:T(8,128)(2,1)}, u32[]{:S(2)}) copy-start(bf16[1,1,640,640]{3,2,1,0:T(8,128)(2,1)} %param.10) | copy-start | bytes 2457604
  15.2 15.1 %all-to-all-start.1 = ((bf16[32,16,128]{2,1,0:T(8,128)(2,1)}), bf16[32,16,128]{2,1,0:T(8,128)(2,1)S(1)}, u32[]{:S(2)}, u32[]{:S(2)}) async-start(bf16[32,16,128]{2,1,0:T(8,128)(2,1)} %get-tuple-element.32), calls=%async_computation.1 | async-start | bytes 262144 | tf_op jit(solution)/shard_map/all_to_all | solution.py:440
  19.6 8.6 %collective-permute-start = (bf16[528,128]{1,0:T(8,128)(2,1)S(1)}, bf16[528,128]{1,0:T(8,128)(2,1)S(1)}, u32[]{:S(2)}, u32[]{:S(2)}) collective-permute-start(bf16[528,128]{1,0:T(8,128)(2,1)S(1)} %get-tuple-element.34.refs_7_), channel_id=1, source_target_pairs={{0,1},{1,2},{2,3},{3,0},{4,5},{5,6},{6,7},{7,4},{8,9},{9,10},{10,1... | collective-permute-start | bytes 405512 | tf_op jit(solution)/shard_map/ppermute | solution.py:442
  21.4 8.9 %collective-permute-start.1 = (bf16[528,128]{1,0:T(8,128)(2,1)S(1)}, bf16[528,128]{1,0:T(8,128)(2,1)S(1)}, u32[]{:S(2)}, u32[]{:S(2)}) collective-permute-start(bf16[528,128]{1,0:T(8,128)(2,1)S(1)} %get-tuple-element.35.refs_8_), channel_id=1, source_target_pairs={{0,3},{1,0},{2,1},{3,2},{4,7},{5,4},{6,5},{7,6},{8,11},{9,8},{10,9... | collective-permute-start | bytes 405512 | tf_op jit(solution)/shard_map/ppermute | solution.py:443
  22.6 5.6 %collective-permute-start.2 = (bf16[128,128]{1,0:T(8,128)(2,1)S(1)}, bf16[128,128]{1,0:T(8,128)(2,1)S(1)}, u32[]{:S(2)}, u32[]{:S(2)}) collective-permute-start(bf16[128,128]{1,0:T(8,128)(2,1)S(1)} %get-tuple-element.36), channel_id=1, source_target_pairs={{0,2},{1,3},{2,0},{3,1},{4,6},{5,7},{6,4},{7,5},{8,10},{9,11},{10,... | collective-permute-start | bytes 98312 | tf_op jit(solution)/shard_map/ppermute | solution.py:445
  32.4 12.3 %all-to-all-start.2 = ((bf16[32,16,128]{2,1,0:T(8,128)(2,1)}), bf16[32,16,128]{2,1,0:T(8,128)(2,1)S(1)}, u32[]{:S(2)}, u32[]{:S(2)}) async-start(bf16[32,16,128]{2,1,0:T(8,128)(2,1)} %get-tuple-element.38), calls=%async_computation.2 | async-start | bytes 262144 | tf_op jit(solution)/shard_map/all_to_all | solution.py:440
  36.5 7.0 %collective-permute-start.3 = (bf16[256,128]{1,0:T(8,128)(2,1)S(1)}, bf16[256,128]{1,0:T(8,128)(2,1)S(1)}, u32[]{:S(2)}, u32[]{:S(2)}) collective-permute-start(bf16[256,128]{1,0:T(8,128)(2,1)S(1)} %get-tuple-element.40.refs_7_), channel_id=1, source_target_pairs={{0,1},{1,2},{2,3},{3,0},{4,5},{5,6},{6,7},{7,4},{8,9},{9,10},{10,1... | collective-permute-start | bytes 196616 | tf_op jit(solution)/shard_map/ppermute | solution.py:442
  38.3 5.9 %collective-permute-start.4 = (bf16[256,128]{1,0:T(8,128)(2,1)S(1)}, bf16[256,128]{1,0:T(8,128)(2,1)S(1)}, u32[]{:S(2)}, u32[]{:S(2)}) collective-permute-start(bf16[256,128]{1,0:T(8,128)(2,1)S(1)} %get-tuple-element.41.refs_8_), channel_id=1, source_target_pairs={{0,3},{1,0},{2,1},{3,2},{4,7},{5,4},{6,5},{7,6},{8,11},{9,8},{10,9... | collective-permute-start | bytes 196616 | tf_op jit(solution)/shard_map/ppermute | solution.py:443
  39.5 4.1 %collective-permute-start.5 = (bf16[128,128]{1,0:T(8,128)(2,1)S(1)}, bf16[128,128]{1,0:T(8,128)(2,1)S(1)}, u32[]{:S(2)}, u32[]{:S(2)}) collective-permute-start(bf16[128,128]{1,0:T(8,128)(2,1)S(1)} %get-tuple-element.42), channel_id=1, source_target_pairs={{0,2},{1,3},{2,0},{3,1},{4,6},{5,7},{6,4},{7,5},{8,10},{9,11},{10,... | collective-permute-start | bytes 98312 | tf_op jit(solution)/shard_map/ppermute | solution.py:445
  47.4 12.1 %all-to-all-start.3 = ((bf16[32,16,128]{2,1,0:T(8,128)(2,1)}), bf16[32,16,128]{2,1,0:T(8,128)(2,1)S(1)}, u32[]{:S(2)}, u32[]{:S(2)}) async-start(bf16[32,16,128]{2,1,0:T(8,128)(2,1)} %get-tuple-element.45), calls=%async_computation.3 | async-start | bytes 262144 | tf_op jit(solution)/shard_map/all_to_all | solution.py:440
  51.4 7.0 %collective-permute-start.6 = (bf16[256,128]{1,0:T(8,128)(2,1)S(1)}, bf16[256,128]{1,0:T(8,128)(2,1)S(1)}, u32[]{:S(2)}, u32[]{:S(2)}) collective-permute-start(bf16[256,128]{1,0:T(8,128)(2,1)S(1)} %get-tuple-element.47.refs_7_), channel_id=1, source_target_pairs={{0,1},{1,2},{2,3},{3,0},{4,5},{5,6},{6,7},{7,4},{8,9},{9,10},{10,1... | collective-permute-start | bytes 196616 | tf_op jit(solution)/shard_map/ppermute | solution.py:442
  53.2 5.9 %collective-permute-start.7 = (bf16[256,128]{1,0:T(8,128)(2,1)S(1)}, bf16[256,128]{1,0:T(8,128)(2,1)S(1)}, u32[]{:S(2)}, u32[]{:S(2)}) collective-permute-start(bf16[256,128]{1,0:T(8,128)(2,1)S(1)} %get-tuple-element.48.refs_8_), channel_id=1, source_target_pairs={{0,3},{1,0},{2,1},{3,2},{4,7},{5,4},{6,5},{7,6},{8,11},{9,8},{10,9... | collective-permute-start | bytes 196616 | tf_op jit(solution)/shard_map/ppermute | solution.py:443
  54.3 4.1 %collective-permute-start.8 = (bf16[128,128]{1,0:T(8,128)(2,1)S(1)}, bf16[128,128]{1,0:T(8,128)(2,1)S(1)}, u32[]{:S(2)}, u32[]{:S(2)}) collective-permute-start(bf16[128,128]{1,0:T(8,128)(2,1)S(1)} %get-tuple-element.49), channel_id=1, source_target_pairs={{0,2},{1,3},{2,0},{3,1},{4,6},{5,7},{6,4},{7,5},{8,10},{9,11},{10,... | collective-permute-start | bytes 98312 | tf_op jit(solution)/shard_map/ppermute | solution.py:445

commit v4 on v3

v4 whole, which is shorter than its diff:
```python
import functools

import jax
import jax.numpy as jnp
from jax import lax
from jax.experimental import pallas as pl
from jax.experimental.pallas import tpu as pltpu
from jax.sharding import PartitionSpec as P

ITERS = 3


STEP_SIZES = (0.8, 0.9, 1.0)
MOMENTUM = (0.0, 0.3, 0.3)

F32 = jnp.float32
BF16 = jnp.bfloat16


def mm(a, b):
    return jnp.dot(a, b, preferred_element_type=F32)


def tn(a, b):
    return lax.dot_general(a, b, (((0,), (0,)), ((), ())), preferred_element_type=F32)


def nt(a, b):
    return lax.dot_general(a, b, (((1,), (1,)), ((), ())), preferred_element_type=F32)


def run(kernel, name, outs, args, scalars=(), scratch=(), flops=1 << 22, aliases=None):
    nbytes = sum(x.size * x.dtype.itemsize for x in map(bare, [*args, *outs]))
    return pl.pallas_call(
        kernel,
        name=name,
        out_shape=[held(x) for x in outs],
        in_specs=[pl.BlockSpec(memory_space=pltpu.SMEM)] * len(scalars) + [spec(x) for x in args],
        out_specs=[spec(x) for x in outs],
        scratch_shapes=list(scratch),
        input_output_aliases=aliases or {},
        compiler_params=pltpu.CompilerParams(vmem_limit_bytes=24 << 20),
        cost_estimate=pl.CostEstimate(flops=flops, bytes_accessed=nbytes, transcendentals=0),
    )(
        *scalars,
        *map(given, args),
    )


class Far:
    def __init__(self, array):
        self.array = array


def bare(x):
    return x.array if isinstance(x, Far) else x


def held(x):
    return pltpu.HBM(x.array.shape, x.array.dtype) if isinstance(x, Far) else x


def given(x):
    return pltpu.with_memory_space_constraint(x.array, pltpu.HBM) if isinstance(x, Far) else x


def spec(x):
    return pl.BlockSpec(memory_space=pltpu.HBM if isinstance(x, Far) else pltpu.VMEM)


def shape(*dims, dtype=F32):
    return jax.ShapeDtypeStruct(dims, dtype)


class Sizes:
    def __init__(self, right_side, deflation, coarse_inverse):
        self.owned, self.loads = right_side.shape[-2:]
        self.order, self.modes = deflation.shape[-2:]
        self.blk = (self.order - self.owned) // 2
        self.side = 2 * self.blk
        self.subs = lax.axis_size("sub")
        self.groups = lax.axis_size("grp")
        self.near = min(self.subs, 5)
        self.chunks = coarse_inverse.shape[1] // self.loads
        self.window = self.near * self.modes
        self.wide = self.window * self.chunks
        self.picked = 2 * self.side
        self.stack = self.modes + 2 * self.picked
        self.folded = self.subs == 4
        self.segments = max(6, 2 + self.order // self.side)

    def base(self, position):
        return jnp.clip(position - 2, 0, self.subs - self.near)


class Place:
    def __init__(self, z, live, margin=None):
        self.z = z
        self.position = lax.axis_index("sub")
        self.even = self.position % 2 == 0
        self.live = live[0, 0]
        self.has_left = self.position > 0
        self.has_right = self.position < z.subs - 1
        self.has_left2 = self.position > 1
        self.has_right2 = self.position < z.subs - 2
        if margin is not None:
            self.lend(margin)

    def lend(self, margin):
        blk = self.z.blk
        self.give_right = pl.multiple_of(margin[0, 0] * blk, blk)
        self.give_left = pl.multiple_of(margin[0, 1] * blk, blk)

    def row_mask(self):
        z = self.z
        rows = lax.broadcasted_iota(jnp.int32, (z.owned, z.loads), 0)
        return rows < self.live

    def kept(self, value):
        z = self.z
        low = value[z.owned : z.owned + z.blk]
        high = value[z.owned + z.blk :]
        return jnp.concatenate(
            [
                jnp.where(self.row_mask(), value[: z.owned], 0.0),
                jnp.where(self.has_left, low, 0.0),
                jnp.where(self.has_right, high, 0.0),
            ],
            axis=0,
        )

    def right_block(self, ref):
        return ref[pl.ds(self.give_right, self.z.blk), :]

    def left_block(self, ref):
        return ref[pl.ds(self.give_left, self.z.blk), :]

    def ahead(self, ref):
        z = self.z
        return jnp.concatenate([ref[z.owned + z.blk :, :], self.right_block(ref)], axis=0)

    def behind(self, ref):
        z = self.z
        return jnp.concatenate([ref[z.owned : z.owned + z.blk, :], self.left_block(ref)], axis=0)

    def pair(self, ahead, behind):
        return jnp.where(self.even, ahead, behind), jnp.where(self.even, behind, ahead)

    def sides(self, first, second):
        return jnp.where(self.even, second, first), jnp.where(self.even, first, second)

    def add_lent(self, target, scale, from_left, from_right, source=None):
        z = self.z
        source = target if source is None else source
        for spot, value in (
            (slice(z.owned, z.owned + z.blk), from_left[z.blk :]),
            (slice(z.owned + z.blk, z.order), from_right[z.blk :]),
            (pl.ds(self.give_left, z.blk), from_left[: z.blk]),
            (pl.ds(self.give_right, z.blk), from_right[: z.blk]),
        ):
            target[spot, :] = source[spot, :] + (value if scale == 1.0 else scale * value)


def selection(z, first, second):
    row = lax.broadcasted_iota(jnp.int32, (z.order, z.side), 0)
    col = lax.broadcasted_iota(jnp.int32, (z.order, z.side), 1)
    return (row == jnp.where(col < z.blk, first + col, second - z.blk + col)).astype(BF16)


def start_all(sem, *pairs):
    copies = [
        pltpu.make_async_copy(source, target, sem.at[k])
        for k, (source, target) in enumerate(pairs)
    ]
    for copy in copies:
        copy.start()
    return copies


def first_kernel(
    z, live, source_far, vectors_far, panel_far, margin_far, slots, own, lent, *scratch
):
    source, vectors_t, panel, margin, sem = scratch
    loads = start_all(
        sem,
        (margin_far, margin),
        (vectors_far, vectors_t),
        (panel_far, panel),
        (source_far, source),
    )
    loads[0].wait()
    at = Place(z, live, margin)
    loads[1].wait()
    rows = selection(z, z.owned + z.blk, at.give_right)
    ahead_vectors = mm(vectors_t[...], rows).astype(BF16)
    rows = selection(z, z.owned, at.give_left)
    behind_vectors = mm(vectors_t[...], rows).astype(BF16)
    lent[...] = jnp.concatenate([ahead_vectors, behind_vectors], axis=0)
    loads[2].wait()
    loads[3].wait()
    own[...] = jnp.where(at.row_mask(), source[...], 0.0)
    ahead = jnp.concatenate([ahead_vectors, at.right_block(own).astype(BF16)], axis=0)
    behind = jnp.concatenate([behind_vectors, at.left_block(own).astype(BF16)], axis=0)
    for k in range(z.subs):
        first = min(max(k - 2, 0), z.subs - z.near) * z.modes
        for chunk in range(z.chunks):
            slots[k, chunk * z.window : (chunk + 1) * z.window, :] = panel[
                chunk, first : first + z.window, :
            ]
        slots[k, z.wide :, :] = jnp.where(k > at.position, ahead, behind)


def static_kernel(z, live, operator_far, inverse_far, margin_far, vectors_t, *refs):
    stack, columns, lifted, first, second, operator, inverse, margin, sem = refs
    loads = start_all(
        sem, (margin_far, margin), (operator_far, operator), (inverse_far, inverse)
    )
    loads[0].wait()
    at = Place(z, live, margin)
    side, modes, picked = z.side, z.modes, z.picked
    from_left = selection(z, at.give_left, z.owned)
    from_right = selection(z, at.give_right, z.owned + z.blk)
    col = lax.broadcasted_iota(jnp.int32, (modes, z.order), 1)
    limit = jnp.where(at.has_left, z.owned + z.blk, z.owned)
    kept = (col < at.live) | ((col >= z.owned) & (col < limit))
    kept = jnp.where(kept | ((col >= z.owned + z.blk) & at.has_right), 1.0, 0.0)
    stack[:modes, :] = vectors_t[...]
    masked = (vectors_t[...].astype(F32) * kept).astype(BF16)
    loads[1].wait()
    rows = jnp.concatenate([at.ahead(operator), at.behind(operator)], axis=0)
    columns[:, :side] = mm(operator[...], from_left).astype(BF16)
    columns[:, side:] = mm(operator[...], from_right).astype(BF16)
    up = nt(masked, rows).astype(BF16)
    ahead = at.ahead(columns)
    behind = at.behind(columns)
    ahead = jnp.concatenate([ahead[:, :side], ahead[:, side:], up[:, :side]], axis=0)
    behind = jnp.concatenate([behind[:, side:], behind[:, :side], up[:, side:]], axis=0)
    first[...], second[...] = at.pair(ahead, behind)
    lifted[...] = nt(masked, operator[...]).astype(BF16)
    loads[2].wait()
    stack[modes : modes + picked, :] = jnp.concatenate(
        [at.ahead(inverse), at.behind(inverse)], axis=0
    )
    rows = (rows.astype(F32) * kept[:1]).astype(BF16)
    stack[modes + picked :, :] = mm(rows, inverse[...]).astype(BF16)


def send(z, at, value, momentum, copies, every_out, sem, first, second, far):
    side, modes = z.side, z.modes
    mine = value[:modes].astype(BF16)

    def put(k, carry):
        copies[k] = mine
        return carry

    lax.fori_loop(0, z.subs * z.groups, put, 0, unroll=8)
    copy = pltpu.make_async_copy(copies, every_out, sem)
    copy.start()
    pieces = [value[modes + k * side : modes + (k + 1) * side] for k in range(4)]
    if momentum is not None:
        pieces[2] = pieces[2] + momentum[0]
        pieces[3] = pieces[3] + momentum[1]
    pieces = [piece.astype(BF16) for piece in pieces]
    first[:side, :], second[:side, :] = at.pair(pieces[0], pieces[1])
    first[side:, :], second[side:, :] = at.pair(pieces[2], pieces[3])
    if z.folded:
        far[0][...] = jnp.where(at.has_right2, pieces[0], pieces[1])
    else:
        far[0][...], far[1][...] = pieces[0], pieces[1]
    return copy


def second_kernel(z, live, slots, own, stack, resid, every_out, first, second, *rest):
    far, (copies, sem) = rest[:-2], rest[-2:]
    at = Place(z, live)
    left = slots[jnp.maximum(at.position - 1, 0), z.wide + z.modes :, :]
    right = slots[jnp.minimum(at.position + 1, z.subs - 1), z.wide + z.modes :, :]
    value = jnp.concatenate(
        [
            own[...],
            jnp.where(at.has_left, left.astype(F32), 0.0),
            jnp.where(at.has_right, right.astype(F32), 0.0),
        ],
        axis=0,
    )
    resid[...] = value
    value = mm(stack[...], value.astype(BF16))
    send(z, at, value, None, copies, every_out, sem, first, second, far).wait()


def window_kernel(z, turn, live, resid, inverse_far, operator_far, *refs):
    if turn:
        part_in, coarse, stack, *refs = refs
        if turn > 1:
            solution_far, *refs = refs
        part, product, solution_out, *refs = refs
        inverse, operator, direction, solution, sem = refs
        more = [(solution_far, solution)] if turn > 1 else []
    else:
        slots, lent, lifted, first_static, second_static, *refs = refs
        part, product, spread, panels, inverse, operator, sem = refs
        more = []
    loads = start_all(sem, (inverse_far, inverse), (operator_far, operator), *more)
    at = Place(z, live)
    if turn:
        index = at.position - z.base(at.position)
        own = coarse[pl.ds(pl.multiple_of(index * z.modes, z.modes), z.modes), :]
        direction[...] = part_in[...] + at.kept(tn(stack[: z.modes, :], own))
        step = STEP_SIZES[turn - 1] * direction[: z.owned, :]
        if turn > 1:
            loads[2].wait()
            step = solution[...] + step
        solution[...] = step
        store = pltpu.make_async_copy(solution, solution_out, sem.at[3])
        store.start()
    else:
        for k in range(z.subs):
            for chunk in range(z.chunks):
                start = (k * z.chunks + chunk) * z.loads
                panels[:, start : start + z.loads] = slots[
                    k, chunk * z.window : (chunk + 1) * z.window, :
                ]
        spread_corrections(z, at, slots, lent, lifted, first_static, second_static, spread)
    loads[0].wait()
    value = at.kept(mm(inverse[...], resid[...].astype(BF16)))
    if turn:
        value = value + MOMENTUM[turn] * direction[...]
    part[...] = value
    loads[1].wait()
    product[...] = mm(operator[...], value.astype(BF16))
    if turn:
        store.wait()


def spread_corrections(z, at, slots, lent, lifted, first_static, second_static, spread):
    side, modes = z.side, z.modes
    row = lax.broadcasted_iota(jnp.int32, (modes, 2 * z.window), 0)
    col = lax.broadcasted_iota(jnp.int32, (modes, 2 * z.window), 1)
    base = z.base(at.position)

    def theirs(offset):
        index = jnp.clip(at.position + offset, 0, z.subs - 1)
        return slots[index, z.wide : z.wide + modes, :]

    left, right = at.sides(first_static[2 * side :, :], second_static[2 * side :, :])
    halves = (
        [
            (theirs(-1), -1, at.has_left),
            (theirs(1), 1, at.has_right),
            (theirs(-2), -2, at.has_left2),
            (theirs(2), 2, at.has_right2),
            (lent[:modes, :], 0, True),
            (lent[modes:, :], 0, True),
        ],
        [(left, -1, at.has_left), (right, 1, at.has_right)]
        + [(lifted[:, k : k + side], 0, True) for k in range(0, z.order, side)],
    )
    for segment in range(z.segments):
        total = jnp.zeros((side, 2 * z.window), F32)
        for half, entries in enumerate(halves):
            if segment < len(entries):
                transposed, offset, have = entries[segment]
                first = half * z.window + (at.position + offset - base) * modes
                place = jnp.where(have, 1.0, 0.0) * jnp.where(col == first + row, 1.0, 0.0)
                total = total + tn(transposed, place.astype(BF16))
        spread[segment * side : (segment + 1) * side, :] = total.astype(BF16)


def main_kernel(z, turn, live, *refs):
    last = turn == ITERS - 1
    every, panels, spread, columns, margin_far, product, resid_in, *refs = refs
    first_in, second_in, first_got, second_got, *refs = refs
    far_left, far_right, first_static, second_static, *refs = refs
    if last:
        part, stack, solution_far, solution_out, resid_out, *refs = refs
        margin, error, resid, direction, solution, sem = refs
        loads = start_all(sem, (margin_far, margin), (solution_far, solution))
    else:
        part, stack, resid, every_out, first, second, *refs = refs
        far, (coarse_out, part_out, margin, error, copies, sem) = refs[:-6], refs[-6:]
        loads = start_all(sem, (margin_far, margin))
    at = Place(z, live)
    side, owned, modes = z.side, z.owned, z.modes

    coarse = jnp.zeros((z.window, z.loads), F32)
    for start in range(0, panels.shape[1], 4 * z.loads):
        stop = min(start + 4 * z.loads, panels.shape[1])
        coarse = coarse + mm(panels[:, start:stop], every[start:stop, :])
    coarse = coarse.astype(BF16)
    nothing = jnp.zeros_like(coarse)
    twice = jnp.concatenate(
        [jnp.concatenate([coarse, nothing], axis=1), jnp.concatenate([nothing, coarse], axis=1)],
        axis=0,
    )
    taken = mm(spread[...], twice)

    def term(segment):
        return taken[segment * side : (segment + 1) * side, : z.loads]

    def other_term(start, rows):
        return taken[start : start + rows, z.loads :]

    left_got, right_got = at.sides(first_got[...], second_got[...])
    ahead_in, behind_in = at.pair(first_in[:side, :], second_in[:side, :])
    left_static, right_static = at.sides(first_static[: 2 * side, :], second_static[: 2 * side, :])

    def masked(have, value):
        return jnp.where(have, value.astype(F32), 0.0)

    from_left = masked(at.has_left, left_got[:side]) + term(0)
    from_right = masked(at.has_right, right_got[:side]) + term(1)
    halo = jnp.concatenate([from_left, from_right], axis=0)
    from_left2 = masked(at.has_left2, far_left[...]) + term(2)
    from_right2 = masked(at.has_right2, far_right[...]) + term(3)
    loads[0].wait()
    at.lend(margin)
    to_right = (ahead_in.astype(F32) + term(4)).astype(BF16)
    to_left = (behind_in.astype(F32) + term(5)).astype(BF16)
    if last:
        index = at.position - z.base(at.position)
        error[: z.window, :] = coarse.astype(F32)
        own = error[pl.ds(pl.multiple_of(index * modes, modes), modes), :].astype(BF16)
        direction[...] = part[...] + at.kept(tn(stack[:modes, :], own))
        at.add_lent(direction, 1.0, from_left, from_right)
        loads[1].wait()
        solution[...] = solution[...] + STEP_SIZES[turn] * direction[:owned, :]
        store_solution = pltpu.make_async_copy(solution, solution_out, sem.at[2])
        store_solution.start()

    def borrowed(have, got, statics, far, near, start):
        rows = jnp.concatenate([statics[:side], statics[side:]], axis=1)
        value = mm(rows, jnp.concatenate([far.astype(BF16), near], axis=0))
        return masked(have, value + got[side:].astype(F32)) + other_term(start, side)

    applied = product[...] + other_term(2 * side, z.order) + mm(columns[...], halo.astype(BF16))
    left = borrowed(at.has_left, left_got, left_static, from_left2, to_left, 0)
    right = borrowed(at.has_right, right_got, right_static, from_right2, to_right, side)
    error[...] = applied
    resid[...] = resid_in[...] - STEP_SIZES[turn] * at.kept(applied)
    at.add_lent(resid, -STEP_SIZES[turn], left, right)
    if last:
        store = pltpu.make_async_copy(resid.at[pl.ds(0, owned), :], resid_out, sem.at[3])
        store.start()
        store.wait()
        store_solution.wait()
    else:
        value = mm(stack[...], resid[...].astype(BF16))
        beta = MOMENTUM[turn + 1]
        momentum = beta * at.ahead(error), beta * at.behind(error)
        store = send(z, at, value, momentum, copies, every_out, sem.at[2], first, second, far)
        coarse_out[...] = coarse
        at.add_lent(part_out, 1.0, from_left, from_right, part)
        store.wait()


def body(
    right_side, live_rows, margin_blocks, local_operator, local_inverse, deflation, coarse_inverse
):
    z = Sizes(right_side, deflation, coarse_inverse)
    source = right_side[0, 0]
    operator = Far(local_operator[0, 0])
    inverse = Far(local_inverse[0, 0])
    vectors_t = deflation[0, 0].T
    margin = Far(margin_blocks.reshape(1, -1))
    scalars = (live_rows,)
    owned, order, loads, modes, side = z.owned, z.order, z.loads, z.modes, z.side
    devices = z.subs * z.groups

    pick = pltpu.SMEM((1, margin_blocks.shape[-1]), jnp.int32)
    sems = pltpu.SemaphoreType.DMA
    square = pltpu.VMEM((order, order), BF16)

    def part(function, *more):
        return functools.partial(function, z, *more)

    def low(*dims):
        return shape(*dims, dtype=BF16)

    def pairs(first):
        partner = list(range(z.subs))
        for k in range(first, z.subs - 1, 2):
            partner[k], partner[k + 1] = k + 1, k
        return list(enumerate(partner))

    def exchange(first, second):
        return lax.ppermute(second, "sub", pairs(1)), lax.ppermute(first, "sub", pairs(0))

    def ring(offset):
        return [(i, (i + offset) % z.subs) for i in range(z.subs)]

    panel = coarse_inverse.reshape(-1, z.chunks, loads).swapaxes(0, 1)
    slots, own, lent = run(
        part(first_kernel),
        "first",
        [
            low(z.subs, z.wide + modes + z.blk, loads),
            shape(owned, loads),
            low(2 * modes, side),
        ],
        [Far(source), Far(vectors_t), Far(panel), margin],
        scalars,
        [
            pltpu.VMEM(source.shape, F32),
            pltpu.VMEM(vectors_t.shape, BF16),
            pltpu.VMEM(panel.shape, BF16),
            pick,
            sems((4,)),
        ],
    )
    slots = lax.all_to_all(slots, "sub", 0, 0, tiled=True)
    stack, columns, lifted, first, second = run(
        part(static_kernel),
        "static",
        [low(z.stack, order), low(order, 2 * side), low(modes, order)]
        + [low(2 * side + modes, loads)] * 2,
        [operator, inverse, margin, vectors_t],
        scalars,
        [square, square, pick, sems((3,))],
    )
    second_static, first_static = exchange(first, second)
    sent = [shape(order, loads), Far(low(devices, modes, loads))]
    sent += [low(2 * side, loads)] * 2 + [low(side, loads)] * (1 if z.folded else 2)
    copies = pltpu.VMEM((devices, modes, loads), BF16)
    resid, every, first, second, *far = run(
        part(second_kernel),
        "second",
        sent,
        [slots, own, stack],
        scalars,
        [copies, sems(())],
    )
    full = shape(order, loads)
    floor = pltpu.VMEM((order, loads), F32)
    solution = None
    for turn in range(ITERS):
        last = turn == ITERS - 1
        every = lax.all_to_all(every, ("sub", "grp"), 0, 0, tiled=True)
        every = every.reshape(devices * modes, loads)
        second_got, first_got = exchange(first, second)
        if z.folded:
            far_left = far_right = lax.ppermute(far[0], "sub", ring(2))
        else:
            far_left = lax.ppermute(far[0], "sub", ring(2))
            far_right = lax.ppermute(far[1], "sub", ring(-2))
        args = [resid, inverse, operator]
        if turn:
            args += [error, coarse, stack]
            args += [solution] if turn > 1 else []
            outs = [full, full, Far(shape(owned, loads))]
            work = [square, square, floor, pltpu.VMEM((owned, loads), F32), sems((4,))]
        else:
            args += [slots, lent, lifted, first_static, second_static]
            outs = [full, full, low(z.segments * side, 2 * z.window)]
            outs += [low(z.window, z.subs * z.chunks * loads)]
            work = [square, square, sems((2,))]
        error, product, *more = run(
            part(window_kernel, turn),
            f"window{turn}",
            outs,
            args,
            scalars,
            work,
            aliases={len(scalars) + 3: 0} if turn else None,
        )
        if turn:
            solution = Far(more[0])
        else:
            spread, panels = more
        args = [every, panels, spread, columns, margin, product, resid]
        args += [first, second, first_got, second_got, far_left, far_right]
        args += [first_static, second_static]
        if last:
            solution, resid = run(
                part(main_kernel, turn),
                f"main{turn}",
                [Far(shape(owned, loads))] * 2,
                args + [error, stack, solution],
                scalars,
                [pick, floor, floor, floor, pltpu.VMEM((owned, loads), F32), sems((4,))],
            )
        else:
            outs = sent + [low(z.window, loads), full]
            resid, every, first, second, *far, coarse, error = run(
                part(main_kernel, turn),
                f"main{turn}",
                outs,
                args + [error, stack],
                scalars,
                [pick, floor, copies, sems((3,))],
                aliases={len(scalars) + len(args): len(outs) - 1},
            )
    return (solution[None, None], resid[None, None])


def solution(mesh):
    return jax.shard_map(
        body,
        mesh=mesh,
        in_specs=(
            P("grp", "sub", None, None),
            P("grp", "sub"),
            P("grp", "sub", None),
            P("grp", "sub", None, None),
            P("grp", "sub", None, None),
            P("grp", "sub", None, None),
            P("grp", "sub"),
        ),
        out_specs=(P("grp", "sub", None, None), P("grp", "sub", None, None)),
        check_vma=False,
    )
```

time: 62.7 us -> 66 us (1.053)
  waiting for transfers between devices: 15.1 us -> 3.08 us
  starting transfers between devices: 31.9 us -> 41.3 us
  Pallas kernels: 11.9 us -> 19.4 us
  local copies, waits for them, and re-layouts: 1.81 us -> 0.01 us
    ppermute x3, waiting for transfers between devices: 8.38 us -> 0.01 us  [body(): far_left = far_right = lax.ppermute(far[0], 'sub', ring(2))]
    pallas_call x6 -> x9, Pallas kernels: 11.9 us -> 19.4 us  [run(): pl.pallas_call(kernel, name=name, out_shape=[held(x) for x in outs], in_s...]
    ppermute x3, starting transfers between devices: 5.31 us -> 8.86 us  [body(): far_left = far_right = lax.ppermute(far[0], 'sub', ring(2))]
    ppermute x6 -> x8, waiting for transfers between devices: 3.53 us -> 0.02 us  [the longest x4 0.01 us: exchange(): lax.ppermute(second, 'sub', pairs(1))]
    ppermute x6 -> x8, starting transfers between devices: 8.93 us -> 12.3 us  [the longest x4 9.73 us: exchange(): lax.ppermute(first, 'sub', pairs(0))]
    all_to_all x3, starting transfers between devices: 12.4 us -> 14.9 us  [body(): every = lax.all_to_all(every, ('sub', 'grp'), 0, 0, tiled=True)]
    unnamed x8 -> x2, local copies, waits for them, and re-layouts: 1.81 us -> 0.01 us
  transfers between devices with their start and end apart: 13 -> 15, of which waited for: 9 -> 3; matrix products, arithmetic and copies ran while one was open for 0% -> 0% of each run, Pallas kernels for 1% -> 14%
where the time goes in v4:
time: 66 us; the launch traced here: 65.3 us
  starting transfers between devices  41.3 us (63%)
  Pallas kernels  19.4 us (29%)
  waiting for transfers between devices  3.08 us (5%)
  between operations  1.49 us (2%)
    pallas_call x9, Pallas kernels, run(): pl.pallas_call(kernel, name=name, out_shape=[held(x) for x in outs], in_s...  19.4 us
    all_to_all x3, starting transfers between devices, body(): every = lax.all_to_all(every, ('sub', 'grp'), 0, 0, tiled=True)  14.9 us
    ppermute x4, starting transfers between devices, exchange(): lax.ppermute(first, 'sub', pairs(0))  9.73 us
    ppermute x3, starting transfers between devices, body(): far_left = far_right = lax.ppermute(far[0], 'sub', ring(2))  8.86 us
    all_to_all x1, starting transfers between devices, body(): slots = lax.all_to_all(slots, 'sub', 0, 0, tiled=True)  5.2 us
    ppermute x4, starting transfers between devices, exchange(): lax.ppermute(second, 'sub', pairs(1))  2.61 us
    all_to_all x1, waiting for transfers between devices, body(): slots = lax.all_to_all(slots, 'sub', 0, 0, tiled=True)  2.53 us
  transfers between devices with their start and end apart: 15, of which 3 were waited for; matrix products, arithmetic and copies ran while one was open for 0% of the time, Pallas kernels for 14%

profile of v4, /device:TPU:0, one launch (start us, length us, event | category | flops | bytes accessed | tf_op | source)
XLA Modules:
  0.0 65.3 jit_solution(15278873741131150084)
XLA Ops:
  1.3 1.7 %first.1 = (bf16[4,144,128]{2,1,0:T(8,128)(2,1)}, f32[512,128]{1,0:T(8,128)S(1)}, bf16[32,128]{1,0:T(8,128)(2,1)S(1)}) custom-call(s32[1,1]{1,0:T(1,128)S(6)} %copy.17.live, f32[512,128]{1,0:T(8,128)} %bitcast.26, bf16[16,640]{1,0:T(8,128)(2,1)} %bitcast.16, bf16[1,64,128]{2,1,0:T(8,128)(2,1)} %bitcast.27, s32[1,2]{1,0:T(1,128)} %bitcast.28), custom_call_target="tpu_custom_call" | custom-call | flops 4194304 | bytes 716808 | tf_op jit(solution)/shard_map/first/pallas_call | solution.py:34
  3.0 0.0 copy-start
  3.0 5.2 %all-to-all-start = ((bf16[4,144,128]{2,1,0:T(8,128)(2,1)}), bf16[4,144,128]{2,1,0:T(8,128)(2,1)S(1)}, u32[]{:S(2)}, u32[]{:S(2)}) async-start(bf16[4,144,128]{2,1,0:T(8,128)(2,1)} %get-tuple-element.41), calls=%async_computation | async-start | bytes 294912 | tf_op jit(solution)/shard_map/all_to_all | solution.py:510
  8.2 0.0 copy-done
  8.2 2.5 %static.1 = (bf16[528,640]{1,0:T(8,128)(2,1)S(1)}, bf16[640,256]{1,0:T(8,128)(2,1)S(1)}, bf16[16,640]{1,0:T(8,128)(2,1)S(1)}, bf16[272,128]{1,0:T(8,128)(2,1)S(1)}, bf16[272,128]{1,0:T(8,128)(2,1)S(1)}) custom-call(s32[1,1]{1,0:T(1,128)S(6)} %copy.17.live, bf16[640,640]{1,0:T(8,128)(2,1)} %bitcast.18, bf16[640,640]{1,0:T(8,128)(2,1)} %bitcast.22, ...), custom_call_target="tpu_custom_call" | custom-call | flops 4194304 | bytes 2822152 | tf_op jit(solution)/shard_map/static/pallas_call | solution.py:34
  10.8 2.5 %all-to-all-done.slots.refs_0_ = bf16[4,144,128]{2,1,0:T(8,128)(2,1)S(1)} async-done(((bf16[4,144,128]{2,1,0:T(8,128)(2,1)}), bf16[4,144,128]{2,1,0:T(8,128)(2,1)S(1)}, u32[]{:S(2)}, u32[]{:S(2)}) %all-to-all-start) | async-done | bytes 147488 | tf_op jit(solution)/shard_map/all_to_all | solution.py:510
  13.3 1.1 %second.1 = (f32[640,128]{1,0:T(8,128)S(1)}, bf16[32,16,128]{2,1,0:T(8,128)(2,1)}, bf16[256,128]{1,0:T(8,128)(2,1)S(1)}, bf16[256,128]{1,0:T(8,128)(2,1)S(1)}, bf16[128,128]{1,0:T(8,128)(2,1)S(1)}) custom-call(s32[1,1]{1,0:T(1,128)S(6)} %copy.17.live, bf16[4,144,128]{2,1,0:T(8,128)(2,1)S(1)} %all-to-all-done.slots.refs_0_, ...), custom_call_target="tpu_custom_call" | custom-call | flops 4194304 | bytes 1708032 | tf_op jit(solution)/shard_map/second/pallas_call | solution.py:34
  14.4 4.4 %all-to-all-start.1 = ((bf16[32,16,128]{2,1,0:T(8,128)(2,1)}), bf16[32,16,128]{2,1,0:T(8,128)(2,1)S(1)}, u32[]{:S(2)}, u32[]{:S(2)}) async-start(bf16[32,16,128]{2,1,0:T(8,128)(2,1)} %get-tuple-element.44), calls=%async_computation.1 | async-start | bytes 262144 | tf_op jit(solution)/shard_map/all_to_all | solution.py:537
  18.8 1.8 %collective-permute-start = (bf16[272,128]{1,0:T(8,128)(2,1)S(1)}, bf16[272,128]{1,0:T(8,128)(2,1)S(1)}, u32[]{:S(2)}, u32[]{:S(2)}) collective-permute-start(bf16[272,128]{1,0:T(8,128)(2,1)S(1)} %get-tuple-element.48), channel_id=1, source_target_pairs={{0,1},{1,0},{2,3},{3,2},{4,5},{5,4},{6,7},{7,6},{8,9},{9,8},{10,11... | collective-permute-start | bytes 208904 | tf_op jit(solution)/shard_map/ppermute | solution.py:486
  20.6 0.7 collective-permute-start.1
  21.2 4.2 %collective-permute-start.2 = (bf16[256,128]{1,0:T(8,128)(2,1)S(1)}, bf16[256,128]{1,0:T(8,128)(2,1)S(1)}, u32[]{:S(2)}, u32[]{:S(2)}) collective-permute-start(bf16[256,128]{1,0:T(8,128)(2,1)S(1)} %get-tuple-element.54.refs_7_), channel_id=1, source_target_pairs={{0,1},{1,0},{2,3},{3,2},{4,5},{5,4},{6,7},{7,6},{8,9},{9,8},{10,11... | collective-permute-start | bytes 196616 | tf_op jit(solution)/shard_map/ppermute | solution.py:486
  25.5 0.7 collective-permute-start.3
  26.1 2.8 %collective-permute-start.4 = (bf16[128,128]{1,0:T(8,128)(2,1)S(1)}, bf16[128,128]{1,0:T(8,128)(2,1)S(1)}, u32[]{:S(2)}, u32[]{:S(2)}) collective-permute-start(bf16[128,128]{1,0:T(8,128)(2,1)S(1)} %get-tuple-element.56), channel_id=1, source_target_pairs={{0,2},{1,3},{2,0},{3,1},{4,6},{5,7},{6,4},{7,5},{8,10},{9,11},{10,... | collective-permute-start | bytes 98312 | tf_op jit(solution)/shard_map/ppermute | solution.py:541
  28.9 0.0 collective-permute-done.refs_3_.refs_13_
  28.9 0.0 collective-permute-done.1.refs_4_.refs_14_
  28.9 2.2 %window0.1 = (f32[640,128]{1,0:T(8,128)S(1)}, f32[640,128]{1,0:T(8,128)S(1)}, bf16[896,128]{1,0:T(8,128)(2,1)S(1)}, bf16[64,512]{1,0:T(8,128)(2,1)S(1)}) custom-call(s32[1,1]{1,0:T(1,128)S(6)} %copy.17.live, f32[640,128]{1,0:T(8,128)S(1)} %get-tuple-element.45.resid.refs_6_, bf16[640,640]{1,0:T(8,128)(2,1)} %bitcast.23, bf16[640,640]{1,0:T(8,128)(2,1)} %bitcast.19, ...), custom_call_target="tpu_custom_call" | custom-call | flops 4194304 | bytes 3231744 | tf_op jit(solution)/shard_map/window0/pallas_call | solution.py:34
  31.1 0.0 collective-permute-done.4.refs_11_.refs_12_
  31.1 0.0 collective-permute-done.2.refs_9_
  31.1 0.0 collective-permute-done.3.refs_10_
  31.2 0.0 all-to-all-done.1
  31.2 2.4 %main0.1 = (f32[640,128]{1,0:T(8,128)S(1)}, bf16[32,16,128]{2,1,0:T(8,128)(2,1)}, bf16[256,128]{1,0:T(8,128)(2,1)S(1)}, bf16[256,128]{1,0:T(8,128)(2,1)S(1)}, bf...) custom-call(s32[1,1]{1,0:T(1,128)S(6)} %copy.17.live, ...), custom_call_target="tpu_custom_call", output_to_operand_aliasing={{6}: (16, {})} | custom-call | flops 4194304 | bytes 3846152 | tf_op jit(solution)/shard_map/main0/pallas_call | solution.py:34
  33.6 4.9 %all-to-all-start.2 = ((bf16[32,16,128]{2,1,0:T(8,128)(2,1)}), bf16[32,16,128]{2,1,0:T(8,128)(2,1)S(1)}, u32[]{:S(2)}, u32[]{:S(2)}) async-start(bf16[32,16,128]{2,1,0:T(8,128)(2,1)} %get-tuple-element.58), calls=%async_computation.2 | async-start | bytes 262144 | tf_op jit(solution)/shard_map/all_to_all | solution.py:537
  38.4 1.8 %collective-permute-start.5 = (bf16[256,128]{1,0:T(8,128)(2,1)S(1)}, bf16[256,128]{1,0:T(8,128)(2,1)S(1)}, u32[]{:S(2)}, u32[]{:S(2)}) collective-permute-start(bf16[256,128]{1,0:T(8,128)(2,1)S(1)} %get-tuple-element.63.refs_7_), channel_id=1, source_target_pairs={{0,1},{1,0},{2,3},{3,2},{4,5},{5,4},{6,7},{7,6},{8,9},{9,8},{10,11... | collective-permute-start | bytes 196616 | tf_op jit(solution)/shard_map/ppermute | solution.py:486
  40.3 0.7 collective-permute-start.6
  40.9 3.0 %collective-permute-start.7 = (bf16[128,128]{1,0:T(8,128)(2,1)S(1)}, bf16[128,128]{1,0:T(8,128)(2,1)S(1)}, u32[]{:S(2)}, u32[]{:S(2)}) collective-permute-start(bf16[128,128]{1,0:T(8,128)(2,1)S(1)} %get-tuple-element.65), channel_id=1, source_target_pairs={{0,2},{1,3},{2,0},{3,1},{4,6},{5,7},{6,4},{7,5},{8,10},{9,11},{10,... | collective-permute-start | bytes 98312 | tf_op jit(solution)/shard_map/ppermute | solution.py:541
  44.0 2.2 %window1.1 = (f32[640,128]{1,0:T(8,128)S(1)}, f32[640,128]{1,0:T(8,128)S(1)}, f32[512,128]{1,0:T(8,128)}) custom-call(s32[1,1]{1,0:T(1,128)S(6)} %copy.17.live, f32[640,128]{1,0:T(8,128)S(1)} %get-tuple-element.59.resid.refs_6_, bf16[640,640]{1,0:T(8,128)(2,1)} %bitcast.24, bf16[640,640]{1,0:T(8,128)(2,1)} %bitcast.20, ...), custom_call_target="tpu_custom_call", output_to_operand_aliasing={{0}: (4, {})} | custom-call | flops 4194304 | bytes 3903488 | tf_op jit(solution)/shard_map/window1/pallas_call | solution.py:34
  46.1 0.0 collective-permute-done.7.refs_11_.refs_12_
  46.2 0.0 collective-permute-done.5.refs_9_
  46.2 0.0 collective-permute-done.6.refs_10_
  46.2 0.4 all-to-all-done.2
  46.6 2.4 %main1.1 = (f32[640,128]{1,0:T(8,128)S(1)}, bf16[32,16,128]{2,1,0:T(8,128)(2,1)}, bf16[256,128]{1,0:T(8,128)(2,1)S(1)}, bf16[256,128]{1,0:T(8,128)(2,1)S(1)}, bf...) custom-call(s32[1,1]{1,0:T(1,128)S(6)} %copy.17.live, ...), custom_call_target="tpu_custom_call", output_to_operand_aliasing={{6}: (16, {})} | custom-call | flops 4194304 | bytes 3846152 | tf_op jit(solution)/shard_map/main1/pallas_call | solution.py:34
  49.0 5.7 %all-to-all-start.3 = ((bf16[32,16,128]{2,1,0:T(8,128)(2,1)}), bf16[32,16,128]{2,1,0:T(8,128)(2,1)S(1)}, u32[]{:S(2)}, u32[]{:S(2)}) async-start(bf16[32,16,128]{2,1,0:T(8,128)(2,1)} %get-tuple-element.67), calls=%async_computation.3 | async-start | bytes 262144 | tf_op jit(solution)/shard_map/all_to_all | solution.py:537
  54.7 1.8 %collective-permute-start.8 = (bf16[256,128]{1,0:T(8,128)(2,1)S(1)}, bf16[256,128]{1,0:T(8,128)(2,1)S(1)}, u32[]{:S(2)}, u32[]{:S(2)}) collective-permute-start(bf16[256,128]{1,0:T(8,128)(2,1)S(1)} %get-tuple-element.73.refs_7_), channel_id=1, source_target_pairs={{0,1},{1,0},{2,3},{3,2},{4,5},{5,4},{6,7},{7,6},{8,9},{9,8},{10,11... | collective-permute-start | bytes 196616 | tf_op jit(solution)/shard_map/ppermute | solution.py:486
  56.5 0.7 collective-permute-start.9
  57.2 3.0 %collective-permute-start.10 = (bf16[128,128]{1,0:T(8,128)(2,1)S(1)}, bf16[128,128]{1,0:T(8,128)(2,1)S(1)}, u32[]{:S(2)}, u32[]{:S(2)}) collective-permute-start(bf16[128,128]{1,0:T(8,128)(2,1)S(1)} %get-tuple-element.75), channel_id=1, source_target_pairs={{0,2},{1,3},{2,0},{3,1},{4,6},{5,7},{6,4},{7,5},{8,10},{9,11},{10,... | collective-permute-start | bytes 98312 | tf_op jit(solution)/shard_map/ppermute | solution.py:541
  60.2 2.5 %window2.1 = (f32[640,128]{1,0:T(8,128)S(1)}, f32[640,128]{1,0:T(8,128)S(1)}, f32[512,128]{1,0:T(8,128)}) custom-call(s32[1,1]{1,0:T(1,128)S(6)} %copy.17.live, f32[640,128]{1,0:T(8,128)S(1)} %get-tuple-element.68.resid.refs_6_, bf16[640,640]{1,0:T(8,128)(2,1)} %bitcast.25, bf16[640,640]{1,0:T(8,128)(2,1)} %bitcast.21, ...), custom_call_target="tpu_custom_call", output_to_operand_aliasing={{0}: (4, {})} | custom-call | flops 4194304 | bytes 4165632 | tf_op jit(solution)/shard_map/window2/pallas_call | solution.py:34
  62.7 0.0 collective-permute-done.10.refs_11_.refs_12_
  62.7 0.0 collective-permute-done.8.refs_9_
  62.7 0.0 collective-permute-done.9.refs_10_
  62.7 0.1 all-to-all-done.3
  62.8 2.5 %main2.1 = (f32[512,128]{1,0:T(8,128)}, f32[512,128]{1,0:T(8,128)}) custom-call(s32[1,1]{1,0:T(1,128)S(6)} %copy.17.live, bf16[512,128]{1,0:T(8,128)(2,1)S(1)} %bitcast.13, bf16[64,512]{1,0:T(8,128)(2,1)S(1)} %get-tuple-element.50.refs_1_, bf16[896,128]{1,0:T(8,128)(2,1)S(1)} %get-tuple-element.51.refs_2_, bf16[640,256]{1,0:T(8,128)(2,1)S(1)} %get-tuple-element.52.refs_3_, ...), custom_call_target="tpu_custom_call" | custom-call | flops 4194304 | bytes 3665928 | tf_op jit(solution)/shard_map/main2/pallas_call | solution.py:34
Async XLA Ops:
  3.0 5.2 %copy-start = (bf16[1,1,640,16]{2,3,1,0:T(8,128)(2,1)S(1)}, bf16[1,1,640,16]{2,3,1,0:T(8,128)(2,1)}, u32[]{:S(2)}) copy-start(bf16[1,1,640,16]{2,3,1,0:T(8,128)(2,1)} %param.12) | copy-start | bytes 61444
  3.0 10.3 %all-to-all-start = ((bf16[4,144,128]{2,1,0:T(8,128)(2,1)}), bf16[4,144,128]{2,1,0:T(8,128)(2,1)S(1)}, u32[]{:S(2)}, u32[]{:S(2)}) async-start(bf16[4,144,128]{2,1,0:T(8,128)(2,1)} %get-tuple-element.41), calls=%async_computation | async-start | bytes 294912 | tf_op jit(solution)/shard_map/all_to_all | solution.py:510
  14.4 16.8 %all-to-all-start.1 = ((bf16[32,16,128]{2,1,0:T(8,128)(2,1)}), bf16[32,16,128]{2,1,0:T(8,128)(2,1)S(1)}, u32[]{:S(2)}, u32[]{:S(2)}) async-start(bf16[32,16,128]{2,1,0:T(8,128)(2,1)} %get-tuple-element.44), calls=%async_computation.1 | async-start | bytes 262144 | tf_op jit(solution)/shard_map/all_to_all | solution.py:537
  18.8 10.2 %collective-permute-start = (bf16[272,128]{1,0:T(8,128)(2,1)S(1)}, bf16[272,128]{1,0:T(8,128)(2,1)S(1)}, u32[]{:S(2)}, u32[]{:S(2)}) collective-permute-start(bf16[272,128]{1,0:T(8,128)(2,1)S(1)} %get-tuple-element.48), channel_id=1, source_target_pairs={{0,1},{1,0},{2,3},{3,2},{4,5},{5,4},{6,7},{7,6},{8,9},{9,8},{10,11... | collective-permute-start | bytes 208904 | tf_op jit(solution)/shard_map/ppermute | solution.py:486
  20.6 8.4 %collective-permute-start.1 = (bf16[272,128]{1,0:T(8,128)(2,1)S(1)}, bf16[272,128]{1,0:T(8,128)(2,1)S(1)}, u32[]{:S(2)}, u32[]{:S(2)}) collective-permute-start(bf16[272,128]{1,0:T(8,128)(2,1)S(1)} %get-tuple-element.49), channel_id=1, source_target_pairs={{0,0},{1,2},{2,1},{3,3},{4,4},{5,6},{6,5},{7,7},{8,8},{9,10},{10,9... | collective-permute-start | bytes 208904 | tf_op jit(solution)/shard_map/ppermute | solution.py:486
  21.2 9.9 %collective-permute-start.2 = (bf16[256,128]{1,0:T(8,128)(2,1)S(1)}, bf16[256,128]{1,0:T(8,128)(2,1)S(1)}, u32[]{:S(2)}, u32[]{:S(2)}) collective-permute-start(bf16[256,128]{1,0:T(8,128)(2,1)S(1)} %get-tuple-element.54.refs_7_), channel_id=1, source_target_pairs={{0,1},{1,0},{2,3},{3,2},{4,5},{5,4},{6,7},{7,6},{8,9},{9,8},{10,11... | collective-permute-start | bytes 196616 | tf_op jit(solution)/shard_map/ppermute | solution.py:486
  25.5 5.7 %collective-permute-start.3 = (bf16[256,128]{1,0:T(8,128)(2,1)S(1)}, bf16[256,128]{1,0:T(8,128)(2,1)S(1)}, u32[]{:S(2)}, u32[]{:S(2)}) collective-permute-start(bf16[256,128]{1,0:T(8,128)(2,1)S(1)} %get-tuple-element.55.refs_8_), channel_id=1, source_target_pairs={{0,0},{1,2},{2,1},{3,3},{4,4},{5,6},{6,5},{7,7},{8,8},{9,10},{10,9... | collective-permute-start | bytes 196616 | tf_op jit(solution)/shard_map/ppermute | solution.py:486
  26.1 5.0 %collective-permute-start.4 = (bf16[128,128]{1,0:T(8,128)(2,1)S(1)}, bf16[128,128]{1,0:T(8,128)(2,1)S(1)}, u32[]{:S(2)}, u32[]{:S(2)}) collective-permute-start(bf16[128,128]{1,0:T(8,128)(2,1)S(1)} %get-tuple-element.56), channel_id=1, source_target_pairs={{0,2},{1,3},{2,0},{3,1},{4,6},{5,7},{6,4},{7,5},{8,10},{9,11},{10,... | collective-permute-start | bytes 98312 | tf_op jit(solution)/shard_map/ppermute | solution.py:541
  33.6 13.0 %all-to-all-start.2 = ((bf16[32,16,128]{2,1,0:T(8,128)(2,1)}), bf16[32,16,128]{2,1,0:T(8,128)(2,1)S(1)}, u32[]{:S(2)}, u32[]{:S(2)}) async-start(bf16[32,16,128]{2,1,0:T(8,128)(2,1)} %get-tuple-element.58), calls=%async_computation.2 | async-start | bytes 262144 | tf_op jit(solution)/shard_map/all_to_all | solution.py:537
  38.4 7.7 %collective-permute-start.5 = (bf16[256,128]{1,0:T(8,128)(2,1)S(1)}, bf16[256,128]{1,0:T(8,128)(2,1)S(1)}, u32[]{:S(2)}, u32[]{:S(2)}) collective-permute-start(bf16[256,128]{1,0:T(8,128)(2,1)S(1)} %get-tuple-element.63.refs_7_), channel_id=1, source_target_pairs={{0,1},{1,0},{2,3},{3,2},{4,5},{5,4},{6,7},{7,6},{8,9},{9,8},{10,11... | collective-permute-start | bytes 196616 | tf_op jit(solution)/shard_map/ppermute | solution.py:486
  40.3 5.9 %collective-permute-start.6 = (bf16[256,128]{1,0:T(8,128)(2,1)S(1)}, bf16[256,128]{1,0:T(8,128)(2,1)S(1)}, u32[]{:S(2)}, u32[]{:S(2)}) collective-permute-start(bf16[256,128]{1,0:T(8,128)(2,1)S(1)} %get-tuple-element.64.refs_8_), channel_id=1, source_target_pairs={{0,0},{1,2},{2,1},{3,3},{4,4},{5,6},{6,5},{7,7},{8,8},{9,10},{10,9... | collective-permute-start | bytes 196616 | tf_op jit(solution)/shard_map/ppermute | solution.py:486
  40.9 5.2 %collective-permute-start.7 = (bf16[128,128]{1,0:T(8,128)(2,1)S(1)}, bf16[128,128]{1,0:T(8,128)(2,1)S(1)}, u32[]{:S(2)}, u32[]{:S(2)}) collective-permute-start(bf16[128,128]{1,0:T(8,128)(2,1)S(1)} %get-tuple-element.65), channel_id=1, source_target_pairs={{0,2},{1,3},{2,0},{3,1},{4,6},{5,7},{6,4},{7,5},{8,10},{9,11},{10,... | collective-permute-start | bytes 98312 | tf_op jit(solution)/shard_map/ppermute | solution.py:541
  49.0 13.9 %all-to-all-start.3 = ((bf16[32,16,128]{2,1,0:T(8,128)(2,1)}), bf16[32,16,128]{2,1,0:T(8,128)(2,1)S(1)}, u32[]{:S(2)}, u32[]{:S(2)}) async-start(bf16[32,16,128]{2,1,0:T(8,128)(2,1)} %get-tuple-element.67), calls=%async_computation.3 | async-start | bytes 262144 | tf_op jit(solution)/shard_map/all_to_all | solution.py:537
  54.7 8.0 %collective-permute-start.8 = (bf16[256,128]{1,0:T(8,128)(2,1)S(1)}, bf16[256,128]{1,0:T(8,128)(2,1)S(1)}, u32[]{:S(2)}, u32[]{:S(2)}) collective-permute-start(bf16[256,128]{1,0:T(8,128)(2,1)S(1)} %get-tuple-element.73.refs_7_), channel_id=1, source_target_pairs={{0,1},{1,0},{2,3},{3,2},{4,5},{5,4},{6,7},{7,6},{8,9},{9,8},{10,11... | collective-permute-start | bytes 196616 | tf_op jit(solution)/shard_map/ppermute | solution.py:486
  56.5 6.2 %collective-permute-start.9 = (bf16[256,128]{1,0:T(8,128)(2,1)S(1)}, bf16[256,128]{1,0:T(8,128)(2,1)S(1)}, u32[]{:S(2)}, u32[]{:S(2)}) collective-permute-start(bf16[256,128]{1,0:T(8,128)(2,1)S(1)} %get-tuple-element.74.refs_8_), channel_id=1, source_target_pairs={{0,0},{1,2},{2,1},{3,3},{4,4},{5,6},{6,5},{7,7},{8,8},{9,10},{10,9... | collective-permute-start | bytes 196616 | tf_op jit(solution)/shard_map/ppermute | solution.py:486
  57.2 5.5 %collective-permute-start.10 = (bf16[128,128]{1,0:T(8,128)(2,1)S(1)}, bf16[128,128]{1,0:T(8,128)(2,1)S(1)}, u32[]{:S(2)}, u32[]{:S(2)}) collective-permute-start(bf16[128,128]{1,0:T(8,128)(2,1)S(1)} %get-tuple-element.75), channel_id=1, source_target_pairs={{0,2},{1,3},{2,0},{3,1},{4,6},{5,7},{6,4},{7,5},{8,10},{9,11},{10,... | collective-permute-start | bytes 98312 | tf_op jit(solution)/shard_map/ppermute | solution.py:541

commit v5 on v4

--- a/solution.py
+++ b/solution.py
@@ -29,11 +29,10 @@
     return lax.dot_general(a, b, (((1,), (1,)), ((), ())), preferred_element_type=F32)
 
 
-def run(kernel, name, outs, args, scalars=(), scratch=(), flops=1 << 22, aliases=None):
+def run(kernel, outs, args, scalars=(), scratch=(), flops=1 << 22, aliases=None):
     nbytes = sum(x.size * x.dtype.itemsize for x in map(bare, [*args, *outs]))
     return pl.pallas_call(
         kernel,
-        name=name,
         out_shape=[held(x) for x in outs],
         in_specs=[pl.BlockSpec(memory_space=pltpu.SMEM)] * len(scalars) + [spec(x) for x in args],
         out_specs=[spec(x) for x in outs],
@@ -97,7 +96,6 @@
     def __init__(self, z, live, margin=None):
         self.z = z
         self.position = lax.axis_index("sub")
-        self.even = self.position % 2 == 0
         self.live = live[0, 0]
         self.has_left = self.position > 0
         self.has_right = self.position < z.subs - 1
@@ -142,12 +140,6 @@
     def behind(self, ref):
         z = self.z
         return jnp.concatenate([ref[z.owned : z.owned + z.blk, :], self.left_block(ref)], axis=0)
-
-    def pair(self, ahead, behind):
-        return jnp.where(self.even, ahead, behind), jnp.where(self.even, behind, ahead)
-
-    def sides(self, first, second):
-        return jnp.where(self.even, second, first), jnp.where(self.even, first, second)
 
     def add_lent(self, target, scale, from_left, from_right, source=None):
         z = self.z
@@ -235,7 +227,7 @@
     behind = at.behind(columns)
     ahead = jnp.concatenate([ahead[:, :side], ahead[:, side:], up[:, :side]], axis=0)
     behind = jnp.concatenate([behind[:, side:], behind[:, :side], up[:, side:]], axis=0)
-    first[...], second[...] = at.pair(ahead, behind)
+    first[...], second[...] = ahead, behind
     lifted[...] = nt(masked, operator[...]).astype(BF16)
     loads[2].wait()
     stack[modes : modes + picked, :] = jnp.concatenate(
@@ -261,8 +253,8 @@
         pieces[2] = pieces[2] + momentum[0]
         pieces[3] = pieces[3] + momentum[1]
     pieces = [piece.astype(BF16) for piece in pieces]
-    first[:side, :], second[:side, :] = at.pair(pieces[0], pieces[1])
-    first[side:, :], second[side:, :] = at.pair(pieces[2], pieces[3])
+    first[:side, :], second[:side, :] = pieces[0], pieces[1]
+    first[side:, :], second[side:, :] = pieces[2], pieces[3]
     if z.folded:
         far[0][...] = jnp.where(at.has_right2, pieces[0], pieces[1])
     else:
@@ -297,7 +289,7 @@
         inverse, operator, direction, solution, sem = refs
         more = [(solution_far, solution)] if turn > 1 else []
     else:
-        slots, lent, lifted, first_static, second_static, *refs = refs
+        slots, lent, lifted, left_static, right_static, *refs = refs
         part, product, spread, panels, inverse, operator, sem = refs
         more = []
     loads = start_all(sem, (inverse_far, inverse), (operator_far, operator), *more)
@@ -320,7 +312,7 @@
                 panels[:, start : start + z.loads] = slots[
                     k, chunk * z.window : (chunk + 1) * z.window, :
                 ]
-        spread_corrections(z, at, slots, lent, lifted, first_static, second_static, spread)
+        spread_corrections(z, at, slots, lent, lifted, left_static, right_static, spread)
     loads[0].wait()
     value = at.kept(mm(inverse[...], resid[...].astype(BF16)))
     if turn:
@@ -332,7 +324,7 @@
         store.wait()
 
 
-def spread_corrections(z, at, slots, lent, lifted, first_static, second_static, spread):
+def spread_corrections(z, at, slots, lent, lifted, left_static, right_static, spread):
     side, modes = z.side, z.modes
     row = lax.broadcasted_iota(jnp.int32, (modes, 2 * z.window), 0)
     col = lax.broadcasted_iota(jnp.int32, (modes, 2 * z.window), 1)
@@ -342,7 +334,7 @@
         index = jnp.clip(at.position + offset, 0, z.subs - 1)
         return slots[index, z.wide : z.wide + modes, :]
 
-    left, right = at.sides(first_static[2 * side :, :], second_static[2 * side :, :])
+    left, right = left_static[2 * side :, :], right_static[2 * side :, :]
     halves = (
         [
             (theirs(-1), -1, at.has_left),
@@ -369,8 +361,8 @@
 def main_kernel(z, turn, live, *refs):
     last = turn == ITERS - 1
     every, panels, spread, columns, margin_far, product, resid_in, *refs = refs
-    first_in, second_in, first_got, second_got, *refs = refs
-    far_left, far_right, first_static, second_static, *refs = refs
+    ahead_in, behind_in, left_got, right_got, *refs = refs
+    far_left, far_right, left_static, right_static, *refs = refs
     if last:
         part, stack, solution_far, solution_out, resid_out, *refs = refs
         margin, error, resid, direction, solution, sem = refs
@@ -400,22 +392,19 @@
     def other_term(start, rows):
         return taken[start : start + rows, z.loads :]
 
-    left_got, right_got = at.sides(first_got[...], second_got[...])
-    ahead_in, behind_in = at.pair(first_in[:side, :], second_in[:side, :])
-    left_static, right_static = at.sides(first_static[: 2 * side, :], second_static[: 2 * side, :])
 
     def masked(have, value):
         return jnp.where(have, value.astype(F32), 0.0)
 
-    from_left = masked(at.has_left, left_got[:side]) + term(0)
-    from_right = masked(at.has_right, right_got[:side]) + term(1)
+    from_left = masked(at.has_left, left_got[:side, :]) + term(0)
+    from_right = masked(at.has_right, right_got[:side, :]) + term(1)
     halo = jnp.concatenate([from_left, from_right], axis=0)
     from_left2 = masked(at.has_left2, far_left[...]) + term(2)
     from_right2 = masked(at.has_right2, far_right[...]) + term(3)
     loads[0].wait()
     at.lend(margin)
-    to_right = (ahead_in.astype(F32) + term(4)).astype(BF16)
-    to_left = (behind_in.astype(F32) + term(5)).astype(BF16)
+    to_right = (ahead_in[:side, :].astype(F32) + term(4)).astype(BF16)
+    to_left = (behind_in[:side, :].astype(F32) + term(5)).astype(BF16)
     if last:
         index = at.position - z.base(at.position)
         error[: z.window, :] = coarse.astype(F32)
@@ -428,9 +417,9 @@
         store_solution.start()
 
     def borrowed(have, got, statics, far, near, start):
-        rows = jnp.concatenate([statics[:side], statics[side:]], axis=1)
+        rows = jnp.concatenate([statics[:side, :], statics[side : 2 * side, :]], axis=1)
         value = mm(rows, jnp.concatenate([far.astype(BF16), near], axis=0))
-        return masked(have, value + got[side:].astype(F32)) + other_term(start, side)
+        return masked(have, value + got[side:, :].astype(F32)) + other_term(start, side)
 
     applied = product[...] + other_term(2 * side, z.order) + mm(columns[...], halo.astype(BF16))
     left = borrowed(at.has_left, left_got, left_static, from_left2, to_left, 0)
@@ -476,14 +465,8 @@
     def low(*dims):
         return shape(*dims, dtype=BF16)
 
-    def pairs(first):
-        partner = list(range(z.subs))
-        for k in range(first, z.subs - 1, 2):
-            partner[k], partner[k + 1] = k + 1, k
-        return list(enumerate(partner))
-
     def exchange(first, second):
-        return lax.ppermute(second, "sub", pairs(1)), lax.ppermute(first, "sub", pairs(0))
+        return lax.ppermute(first, "sub", ring(1)), lax.ppermute(second, "sub", ring(-1))
 
     def ring(offset):
         return [(i, (i + offset) % z.subs) for i in range(z.subs)]
@@ -491,7 +474,6 @@
     panel = coarse_inverse.reshape(-1, z.chunks, loads).swapaxes(0, 1)
     slots, own, lent = run(
         part(first_kernel),
-        "first",
         [
             low(z.subs, z.wide + modes + z.blk, loads),
             shape(owned, loads),
@@ -510,24 +492,18 @@
     slots = lax.all_to_all(slots, "sub", 0, 0, tiled=True)
     stack, columns, lifted, first, second = run(
         part(static_kernel),
-        "static",
         [low(z.stack, order), low(order, 2 * side), low(modes, order)]
         + [low(2 * side + modes, loads)] * 2,
         [operator, inverse, margin, vectors_t],
         scalars,
         [square, square, pick, sems((3,))],
     )
-    second_static, first_static = exchange(first, second)
+    left_static, right_static = exchange(first, second)
     sent = [shape(order, loads), Far(low(devices, modes, loads))]
     sent += [low(2 * side, loads)] * 2 + [low(side, loads)] * (1 if z.folded else 2)
     copies = pltpu.VMEM((devices, modes, loads), BF16)
     resid, every, first, second, *far = run(
-        part(second_kernel),
-        "second",
-        sent,
-        [slots, own, stack],
-        scalars,
-        [copies, sems(())],
+        part(second_kernel), sent, [slots, own, stack], scalars, [copies, sems(())]
     )
     full = shape(order, loads)
     floor = pltpu.VMEM((order, loads), F32)
@@ -536,7 +512,7 @@
         last = turn == ITERS - 1
         every = lax.all_to_all(every, ("sub", "grp"), 0, 0, tiled=True)
         every = every.reshape(devices * modes, loads)
-        second_got, first_got = exchange(first, second)
+        left_got, right_got = exchange(first, second)
         if z.folded:
             far_left = far_right = lax.ppermute(far[0], "sub", ring(2))
         else:
@@ -549,13 +525,12 @@
             outs = [full, full, Far(shape(owned, loads))]
             work = [square, square, floor, pltpu.VMEM((owned, loads), F32), sems((4,))]
         else:
-            args += [slots, lent, lifted, first_static, second_static]
+            args += [slots, lent, lifted, left_static, right_static]
             outs = [full, full, low(z.segments * side, 2 * z.window)]
             outs += [low(z.window, z.subs * z.chunks * loads)]
             work = [square, square, sems((2,))]
         error, product, *more = run(
             part(window_kernel, turn),
-            f"window{turn}",
             outs,
             args,
             scalars,
@@ -567,12 +542,11 @@
         else:
             spread, panels = more
         args = [every, panels, spread, columns, margin, product, resid]
-        args += [first, second, first_got, second_got, far_left, far_right]
-        args += [first_static, second_static]
+        args += [first, second, left_got, right_got, far_left, far_right]
+        args += [left_static, right_static]
         if last:
             solution, resid = run(
                 part(main_kernel, turn),
-                f"main{turn}",
                 [Far(shape(owned, loads))] * 2,
                 args + [error, stack, solution],
                 scalars,
@@ -582,7 +556,6 @@
             outs = sent + [low(z.window, loads), full]
             resid, every, first, second, *far, coarse, error = run(
                 part(main_kernel, turn),
-                f"main{turn}",
                 outs,
                 args + [error, stack],
                 scalars,

time: 66 us -> 62.4 us (0.945)
  starting transfers between devices: 41.3 us -> 34.9 us
  waiting for transfers between devices: 3.08 us -> 5.49 us
    ppermute x3, starting transfers between devices: 8.86 us -> 5.31 us  [body(): far_left = far_right = lax.ppermute(far[0], 'sub', ring(2))]
    all_to_all x3, starting transfers between devices: 14.9 us -> 12.6 us  [body(): every = lax.all_to_all(every, ('sub', 'grp'), 0, 0, tiled=True)]
    ppermute x8, waiting for transfers between devices: 0.02 us -> 1.97 us  [the longest x4 1.96 us: exchange(): lax.ppermute(second, 'sub', ring(-1))]
  transfers between devices with their start and end apart: 15 -> 15, of which waited for: 3 -> 7; matrix products, arithmetic and copies ran while one was open for 0% -> 0% of each run, Pallas kernels for 14% -> 15%
where the time goes in v5:
time: 62.4 us; the launch traced here: 61.8 us
  starting transfers between devices  34.9 us (56%)
  Pallas kernels  19.9 us (32%)
  waiting for transfers between devices  5.49 us (9%)
  between operations  1.42 us (2%)
    pallas_call x9, Pallas kernels, run(): pl.pallas_call(kernel, out_shape=[held(x) for x in outs], in_specs=[pl.Bl...  19.9 us
    all_to_all x3, starting transfers between devices, body(): every = lax.all_to_all(every, ('sub', 'grp'), 0, 0, tiled=True)  12.6 us
    ppermute x4, starting transfers between devices, exchange(): lax.ppermute(first, 'sub', ring(1))  6.33 us
    ppermute x4, starting transfers between devices, exchange(): lax.ppermute(second, 'sub', ring(-1))  5.53 us
    ppermute x3, starting transfers between devices, body(): far_left = far_right = lax.ppermute(far[0], 'sub', ring(2))  5.31 us
    all_to_all x1, starting transfers between devices, body(): slots = lax.all_to_all(slots, 'sub', 0, 0, tiled=True)  5.2 us
    all_to_all x1, waiting for transfers between devices, body(): slots = lax.all_to_all(slots, 'sub', 0, 0, tiled=True)  2.53 us
    ppermute x4, waiting for transfers between devices, exchange(): lax.ppermute(second, 'sub', ring(-1))  1.96 us
  transfers between devices with their start and end apart: 15, of which 7 were waited for; matrix products, arithmetic and copies ran while one was open for 0% of the time, Pallas kernels for 15%

profile of v5, /device:TPU:0, one launch (start us, length us, event | category | flops | bytes accessed | tf_op | source)
XLA Modules:
  0.0 61.8 jit_solution(14164118448693572289)
XLA Ops:
  1.3 1.7 %shard_map.86 = (bf16[4,144,128]{2,1,0:T(8,128)(2,1)}, f32[512,128]{1,0:T(8,128)S(1)}, bf16[32,128]{1,0:T(8,128)(2,1)S(1)}) custom-call(s32[1,1]{1,0:T(1,128)S(6)} %copy.17.live, f32[512,128]{1,0:T(8,128)} %bitcast.26, bf16[16,640]{1,0:T(8,128)(2,1)} %bitcast.16, bf16[1,64,128]{2,1,0:T(8,128)(2,1)} %bitcast.27, s32[1,2]{1,0:T(1,128)} %bitcast.28), custom_call_target="tpu_custom_call" | custom-call | flops 4194304 | bytes 716808 | tf_op jit(solution)/shard_map/pallas_call | solution.py:34
  3.0 0.0 copy-start
  3.0 5.2 %all-to-all-start = ((bf16[4,144,128]{2,1,0:T(8,128)(2,1)}), bf16[4,144,128]{2,1,0:T(8,128)(2,1)S(1)}, u32[]{:S(2)}, u32[]{:S(2)}) async-start(bf16[4,144,128]{2,1,0:T(8,128)(2,1)} %get-tuple-element.41), calls=%async_computation | async-start | bytes 294912 | tf_op jit(solution)/shard_map/all_to_all | solution.py:492
  8.2 0.0 copy-done
  8.2 2.5 %shard_map.87 = (bf16[528,640]{1,0:T(8,128)(2,1)S(1)}, bf16[640,256]{1,0:T(8,128)(2,1)S(1)}, bf16[16,640]{1,0:T(8,128)(2,1)S(1)}, bf16[272,128]{1,0:T(8,128)(2,1)S(1)}, bf16[272,128]{1,0:T(8,128)(2,1)S(1)}) custom-call(s32[1,1]{1,0:T(1,128)S(6)} %copy.17.live, bf16[640,640]{1,0:T(8,128)(2,1)} %bitcast.18, bf16[640,640]{1,0:T(8,128)(2,1)} %bitcast.22, ...), custom_call_target="tpu_custom_call" | custom-call | flops 4194304 | bytes 2822152 | tf_op jit(solution)/shard_map/pallas_call | solution.py:34
  10.8 2.5 %all-to-all-done.slots.refs_0_ = bf16[4,144,128]{2,1,0:T(8,128)(2,1)S(1)} async-done(((bf16[4,144,128]{2,1,0:T(8,128)(2,1)}), bf16[4,144,128]{2,1,0:T(8,128)(2,1)S(1)}, u32[]{:S(2)}, u32[]{:S(2)}) %all-to-all-start) | async-done | bytes 147488 | tf_op jit(solution)/shard_map/all_to_all | solution.py:492
  13.3 1.1 %shard_map.88 = (f32[640,128]{1,0:T(8,128)S(1)}, bf16[32,16,128]{2,1,0:T(8,128)(2,1)}, bf16[256,128]{1,0:T(8,128)(2,1)S(1)}, bf16[256,128]{1,0:T(8,128)(2,1)S(1)}, bf16[128,128]{1,0:T(8,128)(2,1)S(1)}) custom-call(s32[1,1]{1,0:T(1,128)S(6)} %copy.17.live, bf16[4,144,128]{2,1,0:T(8,128)(2,1)S(1)} %all-to-all-done.slots.refs_0_, ...), custom_call_target="tpu_custom_call" | custom-call | flops 4194304 | bytes 1708032 | tf_op jit(solution)/shard_map/pallas_call | solution.py:34
  14.4 4.4 %all-to-all-start.1 = ((bf16[32,16,128]{2,1,0:T(8,128)(2,1)}), bf16[32,16,128]{2,1,0:T(8,128)(2,1)S(1)}, u32[]{:S(2)}, u32[]{:S(2)}) async-start(bf16[32,16,128]{2,1,0:T(8,128)(2,1)} %get-tuple-element.44), calls=%async_computation.1 | async-start | bytes 262144 | tf_op jit(solution)/shard_map/all_to_all | solution.py:513
  18.8 1.8 %collective-permute-start = (bf16[272,128]{1,0:T(8,128)(2,1)S(1)}, bf16[272,128]{1,0:T(8,128)(2,1)S(1)}, u32[]{:S(2)}, u32[]{:S(2)}) collective-permute-start(bf16[272,128]{1,0:T(8,128)(2,1)S(1)} %get-tuple-element.48), channel_id=1, source_target_pairs={{0,1},{1,2},{2,3},{3,0},{4,5},{5,6},{6,7},{7,4},{8,9},{9,10},{10,1... | collective-permute-start | bytes 208904 | tf_op jit(solution)/shard_map/ppermute | solution.py:469
  20.6 1.2 %collective-permute-start.1 = (bf16[272,128]{1,0:T(8,128)(2,1)S(1)}, bf16[272,128]{1,0:T(8,128)(2,1)S(1)}, u32[]{:S(2)}, u32[]{:S(2)}) collective-permute-start(bf16[272,128]{1,0:T(8,128)(2,1)S(1)} %get-tuple-element.49), channel_id=1, source_target_pairs={{0,3},{1,0},{2,1},{3,2},{4,7},{5,4},{6,5},{7,6},{8,11},{9,8},{10,9... | collective-permute-start | bytes 208904 | tf_op jit(solution)/shard_map/ppermute | solution.py:469
  21.7 0.9 %collective-permute-start.2 = (bf16[256,128]{1,0:T(8,128)(2,1)S(1)}, bf16[256,128]{1,0:T(8,128)(2,1)S(1)}, u32[]{:S(2)}, u32[]{:S(2)}) collective-permute-start(bf16[256,128]{1,0:T(8,128)(2,1)S(1)} %get-tuple-element.54.refs_7_), channel_id=1, source_target_pairs={{0,1},{1,2},{2,3},{3,0},{4,5},{5,6},{6,7},{7,4},{8,9},{9,10},{10,1... | collective-permute-start | bytes 196616 | tf_op jit(solution)/shard_map/ppermute | solution.py:469
  22.6 2.1 %collective-permute-start.3 = (bf16[256,128]{1,0:T(8,128)(2,1)S(1)}, bf16[256,128]{1,0:T(8,128)(2,1)S(1)}, u32[]{:S(2)}, u32[]{:S(2)}) collective-permute-start(bf16[256,128]{1,0:T(8,128)(2,1)S(1)} %get-tuple-element.55.refs_8_), channel_id=1, source_target_pairs={{0,3},{1,0},{2,1},{3,2},{4,7},{5,4},{6,5},{7,6},{8,11},{9,8},{10,9... | collective-permute-start | bytes 196616 | tf_op jit(solution)/shard_map/ppermute | solution.py:469
  24.7 1.8 %collective-permute-start.4 = (bf16[128,128]{1,0:T(8,128)(2,1)S(1)}, bf16[128,128]{1,0:T(8,128)(2,1)S(1)}, u32[]{:S(2)}, u32[]{:S(2)}) collective-permute-start(bf16[128,128]{1,0:T(8,128)(2,1)S(1)} %get-tuple-element.56), channel_id=1, source_target_pairs={{0,2},{1,3},{2,0},{3,1},{4,6},{5,7},{6,4},{7,5},{8,10},{9,11},{10,... | collective-permute-start | bytes 98312 | tf_op jit(solution)/shard_map/ppermute | solution.py:517
  26.4 0.0 collective-permute-done.refs_3_.refs_13_
  26.4 0.8 %collective-permute-done.1.refs_4_.refs_14_ = bf16[272,128]{1,0:T(8,128)(2,1)S(1)} collective-permute-done((bf16[272,128]{1,0:T(8,128)(2,1)S(1)}, bf16[272,128]{1,0:T(8,128)(2,1)S(1)}, u32[]{:S(2)}, u32[]{:S(2)}) %collective-permute-start.1) | collective-permute-done | bytes 69664 | tf_op jit(solution)/shard_map/ppermute | solution.py:469
  27.2 2.2 %shard_map.89 = (f32[640,128]{1,0:T(8,128)S(1)}, f32[640,128]{1,0:T(8,128)S(1)}, bf16[896,128]{1,0:T(8,128)(2,1)S(1)}, bf16[64,512]{1,0:T(8,128)(2,1)S(1)}) custom-call(s32[1,1]{1,0:T(1,128)S(6)} %copy.17.live, f32[640,128]{1,0:T(8,128)S(1)} %get-tuple-element.45.resid.refs_6_, bf16[640,640]{1,0:T(8,128)(2,1)} %bitcast.23, bf16[640,640]{1,0:T(8,128)(2,1)} %bitcast.19, ...), custom_call_target="tpu_custom_call" | custom-call | flops 4194304 | bytes 3231744 | tf_op jit(solution)/shard_map/pallas_call | solution.py:34
  29.4 0.0 collective-permute-done.4.refs_11_.refs_12_
  29.4 0.0 collective-permute-done.2.refs_9_
  29.4 0.0 collective-permute-done.3.refs_10_
  29.5 0.0 all-to-all-done.1
  29.5 2.6 %shard_map.90 = (f32[640,128]{1,0:T(8,128)S(1)}, bf16[32,16,128]{2,1,0:T(8,128)(2,1)}, bf16[256,128]{1,0:T(8,128)(2,1)S(1)}, bf16[256,128]{1,0:T(8,128)(2,1)S(1)...) custom-call(s32[1,1]{1,0:T(1,128)S(6)} %copy.17.live, ...), custom_call_target="tpu_custom_call", output_to_operand_aliasing={{6}: (16, {})} | custom-call | flops 4194304 | bytes 3846152 | tf_op jit(solution)/shard_map/pallas_call | solution.py:34
  32.1 4.2 %all-to-all-start.2 = ((bf16[32,16,128]{2,1,0:T(8,128)(2,1)}), bf16[32,16,128]{2,1,0:T(8,128)(2,1)S(1)}, u32[]{:S(2)}, u32[]{:S(2)}) async-start(bf16[32,16,128]{2,1,0:T(8,128)(2,1)} %get-tuple-element.58), calls=%async_computation.2 | async-start | bytes 262144 | tf_op jit(solution)/shard_map/all_to_all | solution.py:513
  36.3 1.8 %collective-permute-start.5 = (bf16[256,128]{1,0:T(8,128)(2,1)S(1)}, bf16[256,128]{1,0:T(8,128)(2,1)S(1)}, u32[]{:S(2)}, u32[]{:S(2)}) collective-permute-start(bf16[256,128]{1,0:T(8,128)(2,1)S(1)} %get-tuple-element.63.refs_7_), channel_id=1, source_target_pairs={{0,1},{1,2},{2,3},{3,0},{4,5},{5,6},{6,7},{7,4},{8,9},{9,10},{10,1... | collective-permute-start | bytes 196616 | tf_op jit(solution)/shard_map/ppermute | solution.py:469
  38.1 1.2 %collective-permute-start.6 = (bf16[256,128]{1,0:T(8,128)(2,1)S(1)}, bf16[256,128]{1,0:T(8,128)(2,1)S(1)}, u32[]{:S(2)}, u32[]{:S(2)}) collective-permute-start(bf16[256,128]{1,0:T(8,128)(2,1)S(1)} %get-tuple-element.64.refs_8_), channel_id=1, source_target_pairs={{0,3},{1,0},{2,1},{3,2},{4,7},{5,4},{6,5},{7,6},{8,11},{9,8},{10,9... | collective-permute-start | bytes 196616 | tf_op jit(solution)/shard_map/ppermute | solution.py:469
  39.3 1.8 %collective-permute-start.7 = (bf16[128,128]{1,0:T(8,128)(2,1)S(1)}, bf16[128,128]{1,0:T(8,128)(2,1)S(1)}, u32[]{:S(2)}, u32[]{:S(2)}) collective-permute-start(bf16[128,128]{1,0:T(8,128)(2,1)S(1)} %get-tuple-element.65), channel_id=1, source_target_pairs={{0,2},{1,3},{2,0},{3,1},{4,6},{5,7},{6,4},{7,5},{8,10},{9,11},{10,... | collective-permute-start | bytes 98312 | tf_op jit(solution)/shard_map/ppermute | solution.py:517
  41.1 2.2 %shard_map.91 = (f32[640,128]{1,0:T(8,128)S(1)}, f32[640,128]{1,0:T(8,128)S(1)}, f32[512,128]{1,0:T(8,128)}) custom-call(s32[1,1]{1,0:T(1,128)S(6)} %copy.17.live, f32[640,128]{1,0:T(8,128)S(1)} %get-tuple-element.59.resid.refs_6_, bf16[640,640]{1,0:T(8,128)(2,1)} %bitcast.24, bf16[640,640]{1,0:T(8,128)(2,1)} %bitcast.20, ...), custom_call_target="tpu_custom_call", output_to_operand_aliasing={{0}: (4, {})} | custom-call | flops 4194304 | bytes 3903488 | tf_op jit(solution)/shard_map/pallas_call | solution.py:34
  43.2 0.1 collective-permute-done.7.refs_11_.refs_12_
  43.4 0.0 collective-permute-done.5.refs_9_
  43.4 0.7 %collective-permute-done.6.refs_10_ = bf16[256,128]{1,0:T(8,128)(2,1)S(1)} collective-permute-done((bf16[256,128]{1,0:T(8,128)(2,1)S(1)}, bf16[256,128]{1,0:T(8,128)(2,1)S(1)}, u32[]{:S(2)}, u32[]{:S(2)}) %collective-permute-start.6) | collective-permute-done | bytes 65568 | tf_op jit(solution)/shard_map/ppermute | solution.py:469
  44.0 0.4 all-to-all-done.2
  44.5 2.6 %shard_map.92 = (f32[640,128]{1,0:T(8,128)S(1)}, bf16[32,16,128]{2,1,0:T(8,128)(2,1)}, bf16[256,128]{1,0:T(8,128)(2,1)S(1)}, bf16[256,128]{1,0:T(8,128)(2,1)S(1)...) custom-call(s32[1,1]{1,0:T(1,128)S(6)} %copy.17.live, ...), custom_call_target="tpu_custom_call", output_to_operand_aliasing={{6}: (16, {})} | custom-call | flops 4194304 | bytes 3846152 | tf_op jit(solution)/shard_map/pallas_call | solution.py:34
  47.1 4.0 %all-to-all-start.3 = ((bf16[32,16,128]{2,1,0:T(8,128)(2,1)}), bf16[32,16,128]{2,1,0:T(8,128)(2,1)S(1)}, u32[]{:S(2)}, u32[]{:S(2)}) async-start(bf16[32,16,128]{2,1,0:T(8,128)(2,1)} %get-tuple-element.67), calls=%async_computation.3 | async-start | bytes 262144 | tf_op jit(solution)/shard_map/all_to_all | solution.py:513
  51.1 1.8 %collective-permute-start.8 = (bf16[256,128]{1,0:T(8,128)(2,1)S(1)}, bf16[256,128]{1,0:T(8,128)(2,1)S(1)}, u32[]{:S(2)}, u32[]{:S(2)}) collective-permute-start(bf16[256,128]{1,0:T(8,128)(2,1)S(1)} %get-tuple-element.73.refs_7_), channel_id=1, source_target_pairs={{0,1},{1,2},{2,3},{3,0},{4,5},{5,6},{6,7},{7,4},{8,9},{9,10},{10,1... | collective-permute-start | bytes 196616 | tf_op jit(solution)/shard_map/ppermute | solution.py:469
  52.9 1.2 %collective-permute-start.9 = (bf16[256,128]{1,0:T(8,128)(2,1)S(1)}, bf16[256,128]{1,0:T(8,128)(2,1)S(1)}, u32[]{:S(2)}, u32[]{:S(2)}) collective-permute-start(bf16[256,128]{1,0:T(8,128)(2,1)S(1)} %get-tuple-element.74.refs_8_), channel_id=1, source_target_pairs={{0,3},{1,0},{2,1},{3,2},{4,7},{5,4},{6,5},{7,6},{8,11},{9,8},{10,9... | collective-permute-start | bytes 196616 | tf_op jit(solution)/shard_map/ppermute | solution.py:469
  54.1 1.8 %collective-permute-start.10 = (bf16[128,128]{1,0:T(8,128)(2,1)S(1)}, bf16[128,128]{1,0:T(8,128)(2,1)S(1)}, u32[]{:S(2)}, u32[]{:S(2)}) collective-permute-start(bf16[128,128]{1,0:T(8,128)(2,1)S(1)} %get-tuple-element.75), channel_id=1, source_target_pairs={{0,2},{1,3},{2,0},{3,1},{4,6},{5,7},{6,4},{7,5},{8,10},{9,11},{10,... | collective-permute-start | bytes 98312 | tf_op jit(solution)/shard_map/ppermute | solution.py:517
  55.9 2.5 %shard_map.93 = (f32[640,128]{1,0:T(8,128)S(1)}, f32[640,128]{1,0:T(8,128)S(1)}, f32[512,128]{1,0:T(8,128)}) custom-call(s32[1,1]{1,0:T(1,128)S(6)} %copy.17.live, f32[640,128]{1,0:T(8,128)S(1)} %get-tuple-element.68.resid.refs_6_, bf16[640,640]{1,0:T(8,128)(2,1)} %bitcast.25, bf16[640,640]{1,0:T(8,128)(2,1)} %bitcast.21, ...), custom_call_target="tpu_custom_call", output_to_operand_aliasing={{0}: (4, {})} | custom-call | flops 4194304 | bytes 4165632 | tf_op jit(solution)/shard_map/pallas_call | solution.py:34
  58.4 0.0 collective-permute-done.10.refs_11_.refs_12_
  58.4 0.0 collective-permute-done.8.refs_9_
  58.4 0.4 collective-permute-done.9.refs_10_
  58.8 0.4 all-to-all-done.3
  59.3 2.5 %shard_map.94 = (f32[512,128]{1,0:T(8,128)}, f32[512,128]{1,0:T(8,128)}) custom-call(s32[1,1]{1,0:T(1,128)S(6)} %copy.17.live, bf16[512,128]{1,0:T(8,128)(2,1)S(1)} %bitcast.13, bf16[64,512]{1,0:T(8,128)(2,1)S(1)} %get-tuple-element.50.refs_1_, bf16[896,128]{1,0:T(8,128)(2,1)S(1)} %get-tuple-element.51.refs_2_, ...), custom_call_target="tpu_custom_call" | custom-call | flops 4194304 | bytes 3665928 | tf_op jit(solution)/shard_map/pallas_call | solution.py:34
Async XLA Ops:
  3.0 5.2 %copy-start = (bf16[1,1,640,16]{2,3,1,0:T(8,128)(2,1)S(1)}, bf16[1,1,640,16]{2,3,1,0:T(8,128)(2,1)}, u32[]{:S(2)}) copy-start(bf16[1,1,640,16]{2,3,1,0:T(8,128)(2,1)} %param.12) | copy-start | bytes 61444
  3.0 10.3 %all-to-all-start = ((bf16[4,144,128]{2,1,0:T(8,128)(2,1)}), bf16[4,144,128]{2,1,0:T(8,128)(2,1)S(1)}, u32[]{:S(2)}, u32[]{:S(2)}) async-start(bf16[4,144,128]{2,1,0:T(8,128)(2,1)} %get-tuple-element.41), calls=%async_computation | async-start | bytes 294912 | tf_op jit(solution)/shard_map/all_to_all | solution.py:492
  14.4 15.1 %all-to-all-start.1 = ((bf16[32,16,128]{2,1,0:T(8,128)(2,1)}), bf16[32,16,128]{2,1,0:T(8,128)(2,1)S(1)}, u32[]{:S(2)}, u32[]{:S(2)}) async-start(bf16[32,16,128]{2,1,0:T(8,128)(2,1)} %get-tuple-element.44), calls=%async_computation.1 | async-start | bytes 262144 | tf_op jit(solution)/shard_map/all_to_all | solution.py:513
  18.8 7.7 %collective-permute-start = (bf16[272,128]{1,0:T(8,128)(2,1)S(1)}, bf16[272,128]{1,0:T(8,128)(2,1)S(1)}, u32[]{:S(2)}, u32[]{:S(2)}) collective-permute-start(bf16[272,128]{1,0:T(8,128)(2,1)S(1)} %get-tuple-element.48), channel_id=1, source_target_pairs={{0,1},{1,2},{2,3},{3,0},{4,5},{5,6},{6,7},{7,4},{8,9},{9,10},{10,1... | collective-permute-start | bytes 208904 | tf_op jit(solution)/shard_map/ppermute | solution.py:469
  20.6 6.6 %collective-permute-start.1 = (bf16[272,128]{1,0:T(8,128)(2,1)S(1)}, bf16[272,128]{1,0:T(8,128)(2,1)S(1)}, u32[]{:S(2)}, u32[]{:S(2)}) collective-permute-start(bf16[272,128]{1,0:T(8,128)(2,1)S(1)} %get-tuple-element.49), channel_id=1, source_target_pairs={{0,3},{1,0},{2,1},{3,2},{4,7},{5,4},{6,5},{7,6},{8,11},{9,8},{10,9... | collective-permute-start | bytes 208904 | tf_op jit(solution)/shard_map/ppermute | solution.py:469
  21.7 7.7 %collective-permute-start.2 = (bf16[256,128]{1,0:T(8,128)(2,1)S(1)}, bf16[256,128]{1,0:T(8,128)(2,1)S(1)}, u32[]{:S(2)}, u32[]{:S(2)}) collective-permute-start(bf16[256,128]{1,0:T(8,128)(2,1)S(1)} %get-tuple-element.54.refs_7_), channel_id=1, source_target_pairs={{0,1},{1,2},{2,3},{3,0},{4,5},{5,6},{6,7},{7,4},{8,9},{9,10},{10,1... | collective-permute-start | bytes 196616 | tf_op jit(solution)/shard_map/ppermute | solution.py:469
  22.6 6.9 %collective-permute-start.3 = (bf16[256,128]{1,0:T(8,128)(2,1)S(1)}, bf16[256,128]{1,0:T(8,128)(2,1)S(1)}, u32[]{:S(2)}, u32[]{:S(2)}) collective-permute-start(bf16[256,128]{1,0:T(8,128)(2,1)S(1)} %get-tuple-element.55.refs_8_), channel_id=1, source_target_pairs={{0,3},{1,0},{2,1},{3,2},{4,7},{5,4},{6,5},{7,6},{8,11},{9,8},{10,9... | collective-permute-start | bytes 196616 | tf_op jit(solution)/shard_map/ppermute | solution.py:469
  24.7 4.7 %collective-permute-start.4 = (bf16[128,128]{1,0:T(8,128)(2,1)S(1)}, bf16[128,128]{1,0:T(8,128)(2,1)S(1)}, u32[]{:S(2)}, u32[]{:S(2)}) collective-permute-start(bf16[128,128]{1,0:T(8,128)(2,1)S(1)} %get-tuple-element.56), channel_id=1, source_target_pairs={{0,2},{1,3},{2,0},{3,1},{4,6},{5,7},{6,4},{7,5},{8,10},{9,11},{10,... | collective-permute-start | bytes 98312 | tf_op jit(solution)/shard_map/ppermute | solution.py:517
  32.1 12.4 %all-to-all-start.2 = ((bf16[32,16,128]{2,1,0:T(8,128)(2,1)}), bf16[32,16,128]{2,1,0:T(8,128)(2,1)S(1)}, u32[]{:S(2)}, u32[]{:S(2)}) async-start(bf16[32,16,128]{2,1,0:T(8,128)(2,1)} %get-tuple-element.58), calls=%async_computation.2 | async-start | bytes 262144 | tf_op jit(solution)/shard_map/all_to_all | solution.py:513
  36.3 7.0 %collective-permute-start.5 = (bf16[256,128]{1,0:T(8,128)(2,1)S(1)}, bf16[256,128]{1,0:T(8,128)(2,1)S(1)}, u32[]{:S(2)}, u32[]{:S(2)}) collective-permute-start(bf16[256,128]{1,0:T(8,128)(2,1)S(1)} %get-tuple-element.63.refs_7_), channel_id=1, source_target_pairs={{0,1},{1,2},{2,3},{3,0},{4,5},{5,6},{6,7},{7,4},{8,9},{9,10},{10,1... | collective-permute-start | bytes 196616 | tf_op jit(solution)/shard_map/ppermute | solution.py:469
  38.1 5.9 %collective-permute-start.6 = (bf16[256,128]{1,0:T(8,128)(2,1)S(1)}, bf16[256,128]{1,0:T(8,128)(2,1)S(1)}, u32[]{:S(2)}, u32[]{:S(2)}) collective-permute-start(bf16[256,128]{1,0:T(8,128)(2,1)S(1)} %get-tuple-element.64.refs_8_), channel_id=1, source_target_pairs={{0,3},{1,0},{2,1},{3,2},{4,7},{5,4},{6,5},{7,6},{8,11},{9,8},{10,9... | collective-permute-start | bytes 196616 | tf_op jit(solution)/shard_map/ppermute | solution.py:469
  39.3 4.1 %collective-permute-start.7 = (bf16[128,128]{1,0:T(8,128)(2,1)S(1)}, bf16[128,128]{1,0:T(8,128)(2,1)S(1)}, u32[]{:S(2)}, u32[]{:S(2)}) collective-permute-start(bf16[128,128]{1,0:T(8,128)(2,1)S(1)} %get-tuple-element.65), channel_id=1, source_target_pairs={{0,2},{1,3},{2,0},{3,1},{4,6},{5,7},{6,4},{7,5},{8,10},{9,11},{10,... | collective-permute-start | bytes 98312 | tf_op jit(solution)/shard_map/ppermute | solution.py:517
  47.1 12.2 %all-to-all-start.3 = ((bf16[32,16,128]{2,1,0:T(8,128)(2,1)}), bf16[32,16,128]{2,1,0:T(8,128)(2,1)S(1)}, u32[]{:S(2)}, u32[]{:S(2)}) async-start(bf16[32,16,128]{2,1,0:T(8,128)(2,1)} %get-tuple-element.67), calls=%async_computation.3 | async-start | bytes 262144 | tf_op jit(solution)/shard_map/all_to_all | solution.py:513
  51.1 7.3 %collective-permute-start.8 = (bf16[256,128]{1,0:T(8,128)(2,1)S(1)}, bf16[256,128]{1,0:T(8,128)(2,1)S(1)}, u32[]{:S(2)}, u32[]{:S(2)}) collective-permute-start(bf16[256,128]{1,0:T(8,128)(2,1)S(1)} %get-tuple-element.73.refs_7_), channel_id=1, source_target_pairs={{0,1},{1,2},{2,3},{3,0},{4,5},{5,6},{6,7},{7,4},{8,9},{9,10},{10,1... | collective-permute-start | bytes 196616 | tf_op jit(solution)/shard_map/ppermute | solution.py:469
  52.9 5.9 %collective-permute-start.9 = (bf16[256,128]{1,0:T(8,128)(2,1)S(1)}, bf16[256,128]{1,0:T(8,128)(2,1)S(1)}, u32[]{:S(2)}, u32[]{:S(2)}) collective-permute-start(bf16[256,128]{1,0:T(8,128)(2,1)S(1)} %get-tuple-element.74.refs_8_), channel_id=1, source_target_pairs={{0,3},{1,0},{2,1},{3,2},{4,7},{5,4},{6,5},{7,6},{8,11},{9,8},{10,9... | collective-permute-start | bytes 196616 | tf_op jit(solution)/shard_map/ppermute | solution.py:469
  54.1 4.3 %collective-permute-start.10 = (bf16[128,128]{1,0:T(8,128)(2,1)S(1)}, bf16[128,128]{1,0:T(8,128)(2,1)S(1)}, u32[]{:S(2)}, u32[]{:S(2)}) collective-permute-start(bf16[128,128]{1,0:T(8,128)(2,1)S(1)} %get-tuple-element.75), channel_id=1, source_target_pairs={{0,2},{1,3},{2,0},{3,1},{4,6},{5,7},{6,4},{7,5},{8,10},{9,11},{10,... | collective-permute-start | bytes 98312 | tf_op jit(solution)/shard_map/ppermute | solution.py:517

commit v6 on v5

--- a/solution.py
+++ b/solution.py
@@ -96,18 +96,18 @@
     def __init__(self, z, live, margin=None):
         self.z = z
         self.position = lax.axis_index("sub")
-        self.live = live[0, 0]
+        self.live = None if live is None else live[0, 0]
         self.has_left = self.position > 0
         self.has_right = self.position < z.subs - 1
         self.has_left2 = self.position > 1
         self.has_right2 = self.position < z.subs - 2
         if margin is not None:
-            self.lend(margin)
-
-    def lend(self, margin):
+            self.lend(margin[0, 0], margin[0, 1])
+
+    def lend(self, right, left):
         blk = self.z.blk
-        self.give_right = pl.multiple_of(margin[0, 0] * blk, blk)
-        self.give_left = pl.multiple_of(margin[0, 1] * blk, blk)
+        self.give_right = pl.multiple_of(right * blk, blk)
+        self.give_left = pl.multiple_of(left * blk, blk)
 
     def row_mask(self):
         z = self.z
@@ -127,6 +127,23 @@
             axis=0,
         )
 
+    def kept_columns(self):
+        z = self.z
+        col = lax.broadcasted_iota(jnp.int32, (z.modes, z.order), 1)
+        limit = jnp.where(self.has_left, z.owned + z.blk, z.owned)
+        kept = (col < self.live) | ((col >= z.owned) & (col < limit))
+        return jnp.where(kept | ((col >= z.owned + z.blk) & self.has_right), 1.0, 0.0)
+
+    def lent_columns(self):
+        z = self.z
+        return jnp.concatenate(
+            [
+                selection(z, self.give_left, z.owned),
+                selection(z, self.give_right, z.owned + z.blk),
+            ],
+            axis=1,
+        )
+
     def right_block(self, ref):
         return ref[pl.ds(self.give_right, self.z.blk), :]
 
@@ -170,8 +187,9 @@
 
 
 def first_kernel(
-    z, live, source_far, vectors_far, panel_far, margin_far, slots, own, lent, *scratch
+    z, source_far, vectors_far, panel_far, margin_far, operator_far, inverse_far, *refs
 ):
+    slots_far, lent, spot, operator, inverse, slots, *scratch = refs
     source, vectors_t, panel, margin, sem = scratch
     loads = start_all(
         sem,
@@ -179,9 +197,12 @@
         (vectors_far, vectors_t),
         (panel_far, panel),
         (source_far, source),
+        (margin_far, spot),
+        (operator_far, operator),
+        (inverse_far, inverse),
     )
     loads[0].wait()
-    at = Place(z, live, margin)
+    at = Place(z, None, margin)
     loads[1].wait()
     rows = selection(z, z.owned + z.blk, at.give_right)
     ahead_vectors = mm(vectors_t[...], rows).astype(BF16)
@@ -189,10 +210,10 @@
     behind_vectors = mm(vectors_t[...], rows).astype(BF16)
     lent[...] = jnp.concatenate([ahead_vectors, behind_vectors], axis=0)
     loads[2].wait()
+    loads[4].wait()
     loads[3].wait()
-    own[...] = jnp.where(at.row_mask(), source[...], 0.0)
-    ahead = jnp.concatenate([ahead_vectors, at.right_block(own).astype(BF16)], axis=0)
-    behind = jnp.concatenate([behind_vectors, at.left_block(own).astype(BF16)], axis=0)
+    ahead = jnp.concatenate([ahead_vectors, at.right_block(source).astype(BF16)], axis=0)
+    behind = jnp.concatenate([behind_vectors, at.left_block(source).astype(BF16)], axis=0)
     for k in range(z.subs):
         first = min(max(k - 2, 0), z.subs - z.near) * z.modes
         for chunk in range(z.chunks):
@@ -200,55 +221,53 @@
                 chunk, first : first + z.window, :
             ]
         slots[k, z.wide :, :] = jnp.where(k > at.position, ahead, behind)
-
-
-def static_kernel(z, live, operator_far, inverse_far, margin_far, vectors_t, *refs):
-    stack, columns, lifted, first, second, operator, inverse, margin, sem = refs
-    loads = start_all(
-        sem, (margin_far, margin), (operator_far, operator), (inverse_far, inverse)
-    )
-    loads[0].wait()
+    store = pltpu.make_async_copy(slots, slots_far, sem.at[7])
+    store.start()
+    loads[5].wait()
+    loads[6].wait()
+    store.wait()
+
+
+def static_kernel(z, live, operator, inverse, margin_in, vectors_t, *refs):
+    stack, first, second, margin, sem = refs
+    side, modes, picked = z.side, z.modes, z.picked
+    load = pltpu.make_async_copy(margin_in, margin, sem)
+    load.start()
+    load.wait()
     at = Place(z, live, margin)
-    side, modes, picked = z.side, z.modes, z.picked
-    from_left = selection(z, at.give_left, z.owned)
-    from_right = selection(z, at.give_right, z.owned + z.blk)
-    col = lax.broadcasted_iota(jnp.int32, (modes, z.order), 1)
-    limit = jnp.where(at.has_left, z.owned + z.blk, z.owned)
-    kept = (col < at.live) | ((col >= z.owned) & (col < limit))
-    kept = jnp.where(kept | ((col >= z.owned + z.blk) & at.has_right), 1.0, 0.0)
+    rows = jnp.concatenate([at.ahead(operator), at.behind(operator)], axis=0)
+    kept = at.kept_columns()
     stack[:modes, :] = vectors_t[...]
     masked = (vectors_t[...].astype(F32) * kept).astype(BF16)
-    loads[1].wait()
-    rows = jnp.concatenate([at.ahead(operator), at.behind(operator)], axis=0)
-    columns[:, :side] = mm(operator[...], from_left).astype(BF16)
-    columns[:, side:] = mm(operator[...], from_right).astype(BF16)
+    picks = at.lent_columns()
+    columns = mm(rows, picks).astype(BF16)
     up = nt(masked, rows).astype(BF16)
-    ahead = at.ahead(columns)
-    behind = at.behind(columns)
-    ahead = jnp.concatenate([ahead[:, :side], ahead[:, side:], up[:, :side]], axis=0)
-    behind = jnp.concatenate([behind[:, side:], behind[:, :side], up[:, side:]], axis=0)
-    first[...], second[...] = ahead, behind
-    lifted[...] = nt(masked, operator[...]).astype(BF16)
-    loads[2].wait()
+    first[...] = jnp.concatenate(
+        [columns[:side, :side], columns[:side, side:], up[:, :side]], axis=0
+    )
+    second[...] = jnp.concatenate(
+        [columns[side:, side:], columns[side:, :side], up[:, side:]], axis=0
+    )
     stack[modes : modes + picked, :] = jnp.concatenate(
         [at.ahead(inverse), at.behind(inverse)], axis=0
     )
-    rows = (rows.astype(F32) * kept[:1]).astype(BF16)
-    stack[modes + picked :, :] = mm(rows, inverse[...]).astype(BF16)
-
-
-def send(z, at, value, momentum, copies, every_out, sem, first, second, far):
+    value = (rows.astype(F32) * kept[:1]).astype(BF16)
+    stack[modes + picked :, :] = mm(value, inverse[...]).astype(BF16)
+
+
+def send(z, at, stack, low, momentum, copies, every_out, sem, first, second, far):
     side, modes = z.side, z.modes
-    mine = value[:modes].astype(BF16)
+    mine = mm(stack[:modes, :], low).astype(BF16)
 
     def put(k, carry):
         copies[k] = mine
         return carry
 
-    lax.fori_loop(0, z.subs * z.groups, put, 0, unroll=8)
+    lax.fori_loop(0, z.subs * z.groups, put, 0, unroll=min(32, z.subs * z.groups))
     copy = pltpu.make_async_copy(copies, every_out, sem)
     copy.start()
-    pieces = [value[modes + k * side : modes + (k + 1) * side] for k in range(4)]
+    value = mm(stack[modes:, :], low)
+    pieces = [value[k * side : (k + 1) * side] for k in range(4)]
     if momentum is not None:
         pieces[2] = pieces[2] + momentum[0]
         pieces[3] = pieces[3] + momentum[1]
@@ -262,22 +281,22 @@
     return copy
 
 
-def second_kernel(z, live, slots, own, stack, resid, every_out, first, second, *rest):
+def second_kernel(z, live, slots, source, stack, resid, every_out, first, second, *rest):
     far, (copies, sem) = rest[:-2], rest[-2:]
     at = Place(z, live)
     left = slots[jnp.maximum(at.position - 1, 0), z.wide + z.modes :, :]
     right = slots[jnp.minimum(at.position + 1, z.subs - 1), z.wide + z.modes :, :]
     value = jnp.concatenate(
         [
-            own[...],
+            jnp.where(at.row_mask(), source[...], 0.0),
             jnp.where(at.has_left, left.astype(F32), 0.0),
             jnp.where(at.has_right, right.astype(F32), 0.0),
         ],
         axis=0,
     )
     resid[...] = value
-    value = mm(stack[...], value.astype(BF16))
-    send(z, at, value, None, copies, every_out, sem, first, second, far).wait()
+    low = value.astype(BF16)
+    send(z, at, stack, low, None, copies, every_out, sem, first, second, far).wait()
 
 
 def window_kernel(z, turn, live, resid, inverse_far, operator_far, *refs):
@@ -289,9 +308,9 @@
         inverse, operator, direction, solution, sem = refs
         more = [(solution_far, solution)] if turn > 1 else []
     else:
-        slots, lent, lifted, left_static, right_static, *refs = refs
-        part, product, spread, panels, inverse, operator, sem = refs
-        more = []
+        slots, lent, stack, margin_in, left_static, right_static, *refs = refs
+        part, product, spread, panels, columns, inverse, operator, margin, sem = refs
+        more = [(margin_in, margin)]
     loads = start_all(sem, (inverse_far, inverse), (operator_far, operator), *more)
     at = Place(z, live)
     if turn:
@@ -312,13 +331,20 @@
                 panels[:, start : start + z.loads] = slots[
                     k, chunk * z.window : (chunk + 1) * z.window, :
                 ]
+        loads[2].wait()
+        picks = Place(z, live, margin).lent_columns()
+        loads[1].wait()
+        columns[...] = mm(operator[...], picks).astype(BF16)
+        masked = (stack[: z.modes, :].astype(F32) * at.kept_columns()).astype(BF16)
+        lifted = nt(masked, operator[...]).astype(BF16)
         spread_corrections(z, at, slots, lent, lifted, left_static, right_static, spread)
     loads[0].wait()
     value = at.kept(mm(inverse[...], resid[...].astype(BF16)))
     if turn:
         value = value + MOMENTUM[turn] * direction[...]
     part[...] = value
-    loads[1].wait()
+    if turn:
+        loads[1].wait()
     product[...] = mm(operator[...], value.astype(BF16))
     if turn:
         store.wait()
@@ -358,19 +384,19 @@
         spread[segment * side : (segment + 1) * side, :] = total.astype(BF16)
 
 
-def main_kernel(z, turn, live, *refs):
+def main_kernel(z, turn, live, margin_in, *refs):
     last = turn == ITERS - 1
-    every, panels, spread, columns, margin_far, product, resid_in, *refs = refs
+    every, panels, spread, columns, product, resid_in, *refs = refs
     ahead_in, behind_in, left_got, right_got, *refs = refs
     far_left, far_right, left_static, right_static, *refs = refs
     if last:
         part, stack, solution_far, solution_out, resid_out, *refs = refs
         margin, error, resid, direction, solution, sem = refs
-        loads = start_all(sem, (margin_far, margin), (solution_far, solution))
+        loads = start_all(sem, (margin_in, margin), (solution_far, solution))
     else:
         part, stack, resid, every_out, first, second, *refs = refs
         far, (coarse_out, part_out, margin, error, copies, sem) = refs[:-6], refs[-6:]
-        loads = start_all(sem, (margin_far, margin))
+        loads = start_all(sem, (margin_in, margin))
     at = Place(z, live)
     side, owned, modes = z.side, z.owned, z.modes
 
@@ -402,7 +428,7 @@
     from_left2 = masked(at.has_left2, far_left[...]) + term(2)
     from_right2 = masked(at.has_right2, far_right[...]) + term(3)
     loads[0].wait()
-    at.lend(margin)
+    at.lend(margin[0, 0], margin[0, 1])
     to_right = (ahead_in[:side, :].astype(F32) + term(4)).astype(BF16)
     to_left = (behind_in[:side, :].astype(F32) + term(5)).astype(BF16)
     if last:
@@ -433,10 +459,10 @@
         store.wait()
         store_solution.wait()
     else:
-        value = mm(stack[...], resid[...].astype(BF16))
+        low = resid[...].astype(BF16)
         beta = MOMENTUM[turn + 1]
         momentum = beta * at.ahead(error), beta * at.behind(error)
-        store = send(z, at, value, momentum, copies, every_out, sem.at[2], first, second, far)
+        store = send(z, at, stack, low, momentum, copies, every_out, sem.at[2], first, second, far)
         coarse_out[...] = coarse
         at.add_lent(part_out, 1.0, from_left, from_right, part)
         store.wait()
@@ -472,38 +498,41 @@
         return [(i, (i + offset) % z.subs) for i in range(z.subs)]
 
     panel = coarse_inverse.reshape(-1, z.chunks, loads).swapaxes(0, 1)
-    slots, own, lent = run(
+    slots, lent, spot, operator_near, inverse_near = run(
         part(first_kernel),
         [
-            low(z.subs, z.wide + modes + z.blk, loads),
-            shape(owned, loads),
+            Far(low(z.subs, z.wide + modes + z.blk, loads)),
             low(2 * modes, side),
+            shape(1, margin_blocks.shape[-1], dtype=jnp.int32),
+            low(order, order),
+            low(order, order),
         ],
-        [Far(source), Far(vectors_t), Far(panel), margin],
-        scalars,
+        [Far(source), Far(vectors_t), Far(panel), margin, operator, inverse],
+        (),
         [
+            pltpu.VMEM((z.subs, z.wide + modes + z.blk, loads), BF16),
             pltpu.VMEM(source.shape, F32),
             pltpu.VMEM(vectors_t.shape, BF16),
             pltpu.VMEM(panel.shape, BF16),
             pick,
-            sems((4,)),
+            sems((8,)),
         ],
     )
     slots = lax.all_to_all(slots, "sub", 0, 0, tiled=True)
-    stack, columns, lifted, first, second = run(
+    stack, first, second = run(
         part(static_kernel),
-        [low(z.stack, order), low(order, 2 * side), low(modes, order)]
+        [low(z.stack, order)]
         + [low(2 * side + modes, loads)] * 2,
-        [operator, inverse, margin, vectors_t],
+        [operator_near, inverse_near, spot, vectors_t],
         scalars,
-        [square, square, pick, sems((3,))],
+        [pick, sems(())],
     )
     left_static, right_static = exchange(first, second)
     sent = [shape(order, loads), Far(low(devices, modes, loads))]
     sent += [low(2 * side, loads)] * 2 + [low(side, loads)] * (1 if z.folded else 2)
     copies = pltpu.VMEM((devices, modes, loads), BF16)
     resid, every, first, second, *far = run(
-        part(second_kernel), sent, [slots, own, stack], scalars, [copies, sems(())]
+        part(second_kernel), sent, [slots, source, stack], scalars, [copies, sems(())]
     )
     full = shape(order, loads)
     floor = pltpu.VMEM((order, loads), F32)
@@ -525,10 +554,10 @@
             outs = [full, full, Far(shape(owned, loads))]
             work = [square, square, floor, pltpu.VMEM((owned, loads), F32), sems((4,))]
         else:
-            args += [slots, lent, lifted, left_static, right_static]
+            args += [slots, lent, stack, spot, left_static, right_static]
             outs = [full, full, low(z.segments * side, 2 * z.window)]
-            outs += [low(z.window, z.subs * z.chunks * loads)]
-            work = [square, square, sems((2,))]
+            outs += [low(z.window, z.subs * z.chunks * loads), low(order, 2 * side)]
+            work = [square, square, pick, sems((3,))]
         error, product, *more = run(
             part(window_kernel, turn),
             outs,
@@ -540,8 +569,8 @@
         if turn:
             solution = Far(more[0])
         else:
-            spread, panels = more
-        args = [every, panels, spread, columns, margin, product, resid]
+            spread, panels, columns = more
+        args = [spot, every, panels, spread, columns, product, resid]
         args += [first, second, left_got, right_got, far_left, far_right]
         args += [left_static, right_static]
         if last:

time: 62.4 us -> 60.6 us (0.971)
  Pallas kernels: 19.9 us -> 17.6 us
    pallas_call x9, Pallas kernels: 19.9 us -> 17.6 us  [run(): pl.pallas_call(kernel, out_shape=[held(x) for x in outs], in_specs=[pl.Bl...]
    all_to_all x1, waiting for transfers between devices: 2.53 us -> 3.19 us  [body(): slots = lax.all_to_all(slots, 'sub', 0, 0, tiled=True)]
where the time goes in v6:
time: 60.6 us; the launch traced here: 60 us
  starting transfers between devices  34.8 us (57%)
  Pallas kernels  17.6 us (29%)
  waiting for transfers between devices  6.1 us (10%)
  between operations  1.45 us (2%)
    pallas_call x9, Pallas kernels, run(): pl.pallas_call(kernel, out_shape=[held(x) for x in outs], in_specs=[pl.Bl...  17.6 us
    all_to_all x3, starting transfers between devices, body(): every = lax.all_to_all(every, ('sub', 'grp'), 0, 0, tiled=True)  12.5 us
    ppermute x4, starting transfers between devices, exchange(): lax.ppermute(first, 'sub', ring(1))  6.33 us
    ppermute x4, starting transfers between devices, exchange(): lax.ppermute(second, 'sub', ring(-1))  5.53 us
    ppermute x3, starting transfers between devices, body(): far_left = far_right = lax.ppermute(far[0], 'sub', ring(2))  5.31 us
    all_to_all x1, starting transfers between devices, body(): slots = lax.all_to_all(slots, 'sub', 0, 0, tiled=True)  5.2 us
    all_to_all x1, waiting for transfers between devices, body(): slots = lax.all_to_all(slots, 'sub', 0, 0, tiled=True)  3.19 us
    ppermute x4, waiting for transfers between devices, exchange(): lax.ppermute(second, 'sub', ring(-1))  1.92 us
  transfers between devices with their start and end apart: 15, of which 7 were waited for; matrix products, arithmetic and copies ran while one was open for 0% of the time, Pallas kernels for 15%

profile of v6, /device:TPU:0, one launch (start us, length us, event | category | flops | bytes accessed | tf_op | source)
XLA Modules:
  0.0 60.0 jit_solution(9287179716411756800)
XLA Ops:
  0.6 1.7 %shard_map.86 = (bf16[4,144,128]{2,1,0:T(8,128)(2,1)}, bf16[32,128]{1,0:T(8,128)(2,1)S(1)}, s32[1,2]{1,0:T(1,128)S(1)}, bf16[640,640]{1,0:T(8,128)(2,1)S(1)}, bf16[640,640]{1,0:T(8,128)(2,1)S(1)}) custom-call(f32[512,128]{1,0:T(8,128)} %bitcast.13, bf16[16,640]{1,0:T(8,128)(2,1)} %bitcast.18, bf16[1,64,128]{2,1,0:T(8,128)(2,1)} %bitcast.28, ...), custom_call_target="tpu_custom_call" | custom-call | flops 4194304 | bytes 3731472 | tf_op jit(solution)/shard_map/pallas_call | solution.py:34
  2.4 0.0 copy-start.1
  2.4 5.2 %all-to-all-start = ((bf16[4,144,128]{2,1,0:T(8,128)(2,1)}), bf16[4,144,128]{2,1,0:T(8,128)(2,1)S(1)}, u32[]{:S(2)}, u32[]{:S(2)}) async-start(bf16[4,144,128]{2,1,0:T(8,128)(2,1)} %get-tuple-element.43), calls=%async_computation | async-start | bytes 294912 | tf_op jit(solution)/shard_map/all_to_all | solution.py:521
  8.2 0.0 copy-done.1
  8.3 0.0 copy-start
  8.3 1.2 %shard_map.87 = (bf16[528,640]{1,0:T(8,128)(2,1)S(1)}, bf16[272,128]{1,0:T(8,128)(2,1)S(1)}, bf16[272,128]{1,0:T(8,128)(2,1)S(1)}) custom-call(s32[1,1]{1,0:T(1,128)S(6)} %copy.17.live, bf16[640,640]{1,0:T(8,128)(2,1)S(1)} %get-tuple-element.44.operator, bf16[640,640]{1,0:T(8,128)(2,1)S(1)} %get-tuple-element.45.inverse, ...), custom_call_target="tpu_custom_call" | custom-call | flops 4194304 | bytes 2473992 | tf_op jit(solution)/shard_map/pallas_call | solution.py:34
  9.5 3.2 %all-to-all-done.slots.refs_0_ = bf16[4,144,128]{2,1,0:T(8,128)(2,1)S(1)} async-done(((bf16[4,144,128]{2,1,0:T(8,128)(2,1)}), bf16[4,144,128]{2,1,0:T(8,128)(2,1)S(1)}, u32[]{:S(2)}, u32[]{:S(2)}) %all-to-all-start) | async-done | bytes 147488 | tf_op jit(solution)/shard_map/all_to_all | solution.py:521
  12.7 0.0 copy-done
  12.7 0.9 %shard_map.88 = (f32[640,128]{1,0:T(8,128)S(1)}, bf16[32,16,128]{2,1,0:T(8,128)(2,1)}, bf16[256,128]{1,0:T(8,128)(2,1)S(1)}, bf16[256,128]{1,0:T(8,128)(2,1)S(1)}, bf16[128,128]{1,0:T(8,128)(2,1)S(1)}) custom-call(s32[1,1]{1,0:T(1,128)S(6)} %copy.17.live, bf16[4,144,128]{2,1,0:T(8,128)(2,1)S(1)} %all-to-all-done.slots.refs_0_, f32[512,128]{1,0:T(8,128)S(1)} %bitcast.14, ...), custom_call_target="tpu_custom_call" | custom-call | flops 4194304 | bytes 1708032 | tf_op jit(solution)/shard_map/pallas_call | solution.py:34
  13.6 4.4 %all-to-all-start.1 = ((bf16[32,16,128]{2,1,0:T(8,128)(2,1)}), bf16[32,16,128]{2,1,0:T(8,128)(2,1)S(1)}, u32[]{:S(2)}, u32[]{:S(2)}) async-start(bf16[32,16,128]{2,1,0:T(8,128)(2,1)} %get-tuple-element.47), calls=%async_computation.1 | async-start | bytes 262144 | tf_op jit(solution)/shard_map/all_to_all | solution.py:542
  18.0 1.8 %collective-permute-start = (bf16[272,128]{1,0:T(8,128)(2,1)S(1)}, bf16[272,128]{1,0:T(8,128)(2,1)S(1)}, u32[]{:S(2)}, u32[]{:S(2)}) collective-permute-start(bf16[272,128]{1,0:T(8,128)(2,1)S(1)} %get-tuple-element.50), channel_id=1, source_target_pairs={{0,1},{1,2},{2,3},{3,0},{4,5},{5,6},{6,7},{7,4},{8,9},{9,10},{10,1... | collective-permute-start | bytes 208904 | tf_op jit(solution)/shard_map/ppermute | solution.py:495
  19.8 1.2 %collective-permute-start.1 = (bf16[272,128]{1,0:T(8,128)(2,1)S(1)}, bf16[272,128]{1,0:T(8,128)(2,1)S(1)}, u32[]{:S(2)}, u32[]{:S(2)}) collective-permute-start(bf16[272,128]{1,0:T(8,128)(2,1)S(1)} %get-tuple-element.51), channel_id=1, source_target_pairs={{0,3},{1,0},{2,1},{3,2},{4,7},{5,4},{6,5},{7,6},{8,11},{9,8},{10,9... | collective-permute-start | bytes 208904 | tf_op jit(solution)/shard_map/ppermute | solution.py:495
  20.9 0.9 %collective-permute-start.2 = (bf16[256,128]{1,0:T(8,128)(2,1)S(1)}, bf16[256,128]{1,0:T(8,128)(2,1)S(1)}, u32[]{:S(2)}, u32[]{:S(2)}) collective-permute-start(bf16[256,128]{1,0:T(8,128)(2,1)S(1)} %get-tuple-element.56.refs_6_), channel_id=1, source_target_pairs={{0,1},{1,2},{2,3},{3,0},{4,5},{5,6},{6,7},{7,4},{8,9},{9,10},{10,1... | collective-permute-start | bytes 196616 | tf_op jit(solution)/shard_map/ppermute | solution.py:495
  21.8 2.1 %collective-permute-start.3 = (bf16[256,128]{1,0:T(8,128)(2,1)S(1)}, bf16[256,128]{1,0:T(8,128)(2,1)S(1)}, u32[]{:S(2)}, u32[]{:S(2)}) collective-permute-start(bf16[256,128]{1,0:T(8,128)(2,1)S(1)} %get-tuple-element.57.refs_7_), channel_id=1, source_target_pairs={{0,3},{1,0},{2,1},{3,2},{4,7},{5,4},{6,5},{7,6},{8,11},{9,8},{10,9... | collective-permute-start | bytes 196616 | tf_op jit(solution)/shard_map/ppermute | solution.py:495
  23.9 1.8 %collective-permute-start.4 = (bf16[128,128]{1,0:T(8,128)(2,1)S(1)}, bf16[128,128]{1,0:T(8,128)(2,1)S(1)}, u32[]{:S(2)}, u32[]{:S(2)}) collective-permute-start(bf16[128,128]{1,0:T(8,128)(2,1)S(1)} %get-tuple-element.58), channel_id=1, source_target_pairs={{0,2},{1,3},{2,0},{3,1},{4,6},{5,7},{6,4},{7,5},{8,10},{9,11},{10,... | collective-permute-start | bytes 98312 | tf_op jit(solution)/shard_map/ppermute | solution.py:546
  25.6 0.0 collective-permute-done.refs_4_.refs_12_
  25.6 0.8 %collective-permute-done.1.refs_5_.refs_13_ = bf16[272,128]{1,0:T(8,128)(2,1)S(1)} collective-permute-done((bf16[272,128]{1,0:T(8,128)(2,1)S(1)}, bf16[272,128]{1,0:T(8,128)(2,1)S(1)}, u32[]{:S(2)}, u32[]{:S(2)}) %collective-permute-start.1) | collective-permute-done | bytes 69664 | tf_op jit(solution)/shard_map/ppermute | solution.py:495
  26.4 3.0 %shard_map.89 = (f32[640,128]{1,0:T(8,128)S(1)}, f32[640,128]{1,0:T(8,128)S(1)}, bf16[896,128]{1,0:T(8,128)(2,1)S(1)}, bf16[64,512]{1,0:T(8,128)(2,1)S(1)}, bf16[640,256]{1,0:T(8,128)(2,1)S(1)}) custom-call(s32[1,1]{1,0:T(1,128)S(6)} %copy.17.live, f32[640,128]{1,0:T(8,128)S(1)} %get-tuple-element.48.resid.refs_5_, bf16[640,640]{1,0:T(8,128)(2,1)} %bitcast.25, ...), custom_call_target="tpu_custom_call" | custom-call | flops 4194304 | bytes 4214792 | tf_op jit(solution)/shard_map/pallas_call | solution.py:34
  29.4 0.0 collective-permute-done.4.refs_10_.refs_11_
  29.5 0.0 collective-permute-done.2.refs_8_
  29.5 0.0 collective-permute-done.3.refs_9_
  29.5 0.0 all-to-all-done.1
  29.5 2.0 %shard_map.90 = (f32[640,128]{1,0:T(8,128)S(1)}, bf16[32,16,128]{2,1,0:T(8,128)(2,1)}, bf16[256,128]{1,0:T(8,128)(2,1)S(1)}, bf16[256,128]{1,0:T(8,128)(2,1)S(1)...) custom-call(s32[1,1]{1,0:T(1,128)S(6)} %copy.17.live, ...), custom_call_target="tpu_custom_call", output_to_operand_aliasing={{6}: (16, {})} | custom-call | flops 4194304 | bytes 3846152 | tf_op jit(solution)/shard_map/pallas_call | solution.py:34
  31.5 4.1 %all-to-all-start.2 = ((bf16[32,16,128]{2,1,0:T(8,128)(2,1)}), bf16[32,16,128]{2,1,0:T(8,128)(2,1)S(1)}, u32[]{:S(2)}, u32[]{:S(2)}) async-start(bf16[32,16,128]{2,1,0:T(8,128)(2,1)} %get-tuple-element.60), calls=%async_computation.2 | async-start | bytes 262144 | tf_op jit(solution)/shard_map/all_to_all | solution.py:542
  35.6 1.8 %collective-permute-start.5 = (bf16[256,128]{1,0:T(8,128)(2,1)S(1)}, bf16[256,128]{1,0:T(8,128)(2,1)S(1)}, u32[]{:S(2)}, u32[]{:S(2)}) collective-permute-start(bf16[256,128]{1,0:T(8,128)(2,1)S(1)} %get-tuple-element.65.refs_6_), channel_id=1, source_target_pairs={{0,1},{1,2},{2,3},{3,0},{4,5},{5,6},{6,7},{7,4},{8,9},{9,10},{10,1... | collective-permute-start | bytes 196616 | tf_op jit(solution)/shard_map/ppermute | solution.py:495
  37.4 1.2 %collective-permute-start.6 = (bf16[256,128]{1,0:T(8,128)(2,1)S(1)}, bf16[256,128]{1,0:T(8,128)(2,1)S(1)}, u32[]{:S(2)}, u32[]{:S(2)}) collective-permute-start(bf16[256,128]{1,0:T(8,128)(2,1)S(1)} %get-tuple-element.66.refs_7_), channel_id=1, source_target_pairs={{0,3},{1,0},{2,1},{3,2},{4,7},{5,4},{6,5},{7,6},{8,11},{9,8},{10,9... | collective-permute-start | bytes 196616 | tf_op jit(solution)/shard_map/ppermute | solution.py:495
  38.6 1.8 %collective-permute-start.7 = (bf16[128,128]{1,0:T(8,128)(2,1)S(1)}, bf16[128,128]{1,0:T(8,128)(2,1)S(1)}, u32[]{:S(2)}, u32[]{:S(2)}) collective-permute-start(bf16[128,128]{1,0:T(8,128)(2,1)S(1)} %get-tuple-element.67), channel_id=1, source_target_pairs={{0,2},{1,3},{2,0},{3,1},{4,6},{5,7},{6,4},{7,5},{8,10},{9,11},{10,... | collective-permute-start | bytes 98312 | tf_op jit(solution)/shard_map/ppermute | solution.py:546
  40.3 2.2 %shard_map.91 = (f32[640,128]{1,0:T(8,128)S(1)}, f32[640,128]{1,0:T(8,128)S(1)}, f32[512,128]{1,0:T(8,128)}) custom-call(s32[1,1]{1,0:T(1,128)S(6)} %copy.17.live, f32[640,128]{1,0:T(8,128)S(1)} %get-tuple-element.61.resid.refs_5_, bf16[640,640]{1,0:T(8,128)(2,1)} %bitcast.26, bf16[640,640]{1,0:T(8,128)(2,1)} %bitcast.22, ...), custom_call_target="tpu_custom_call", output_to_operand_aliasing={{0}: (4, {})} | custom-call | flops 4194304 | bytes 3903488 | tf_op jit(solution)/shard_map/pallas_call | solution.py:34
  42.5 0.1 collective-permute-done.7.refs_10_.refs_11_
  42.6 0.0 collective-permute-done.5.refs_8_
  42.6 0.7 %collective-permute-done.6.refs_9_ = bf16[256,128]{1,0:T(8,128)(2,1)S(1)} collective-permute-done((bf16[256,128]{1,0:T(8,128)(2,1)S(1)}, bf16[256,128]{1,0:T(8,128)(2,1)S(1)}, u32[]{:S(2)}, u32[]{:S(2)}) %collective-permute-start.6) | collective-permute-done | bytes 65568 | tf_op jit(solution)/shard_map/ppermute | solution.py:495
  43.3 0.4 all-to-all-done.2
  43.8 2.0 %shard_map.92 = (f32[640,128]{1,0:T(8,128)S(1)}, bf16[32,16,128]{2,1,0:T(8,128)(2,1)}, bf16[256,128]{1,0:T(8,128)(2,1)S(1)}, bf16[256,128]{1,0:T(8,128)(2,1)S(1)...) custom-call(s32[1,1]{1,0:T(1,128)S(6)} %copy.17.live, ...), custom_call_target="tpu_custom_call", output_to_operand_aliasing={{6}: (16, {})} | custom-call | flops 4194304 | bytes 3846152 | tf_op jit(solution)/shard_map/pallas_call | solution.py:34
  45.7 4.0 %all-to-all-start.3 = ((bf16[32,16,128]{2,1,0:T(8,128)(2,1)}), bf16[32,16,128]{2,1,0:T(8,128)(2,1)S(1)}, u32[]{:S(2)}, u32[]{:S(2)}) async-start(bf16[32,16,128]{2,1,0:T(8,128)(2,1)} %get-tuple-element.69), calls=%async_computation.3 | async-start | bytes 262144 | tf_op jit(solution)/shard_map/all_to_all | solution.py:542
  49.7 1.8 %collective-permute-start.8 = (bf16[256,128]{1,0:T(8,128)(2,1)S(1)}, bf16[256,128]{1,0:T(8,128)(2,1)S(1)}, u32[]{:S(2)}, u32[]{:S(2)}) collective-permute-start(bf16[256,128]{1,0:T(8,128)(2,1)S(1)} %get-tuple-element.75.refs_6_), channel_id=1, source_target_pairs={{0,1},{1,2},{2,3},{3,0},{4,5},{5,6},{6,7},{7,4},{8,9},{9,10},{10,1... | collective-permute-start | bytes 196616 | tf_op jit(solution)/shard_map/ppermute | solution.py:495
  51.6 1.2 %collective-permute-start.9 = (bf16[256,128]{1,0:T(8,128)(2,1)S(1)}, bf16[256,128]{1,0:T(8,128)(2,1)S(1)}, u32[]{:S(2)}, u32[]{:S(2)}) collective-permute-start(bf16[256,128]{1,0:T(8,128)(2,1)S(1)} %get-tuple-element.76.refs_7_), channel_id=1, source_target_pairs={{0,3},{1,0},{2,1},{3,2},{4,7},{5,4},{6,5},{7,6},{8,11},{9,8},{10,9... | collective-permute-start | bytes 196616 | tf_op jit(solution)/shard_map/ppermute | solution.py:495
  52.7 1.8 %collective-permute-start.10 = (bf16[128,128]{1,0:T(8,128)(2,1)S(1)}, bf16[128,128]{1,0:T(8,128)(2,1)S(1)}, u32[]{:S(2)}, u32[]{:S(2)}) collective-permute-start(bf16[128,128]{1,0:T(8,128)(2,1)S(1)} %get-tuple-element.77), channel_id=1, source_target_pairs={{0,2},{1,3},{2,0},{3,1},{4,6},{5,7},{6,4},{7,5},{8,10},{9,11},{10,... | collective-permute-start | bytes 98312 | tf_op jit(solution)/shard_map/ppermute | solution.py:546
  54.5 2.5 %shard_map.93 = (f32[640,128]{1,0:T(8,128)S(1)}, f32[640,128]{1,0:T(8,128)S(1)}, f32[512,128]{1,0:T(8,128)}) custom-call(s32[1,1]{1,0:T(1,128)S(6)} %copy.17.live, f32[640,128]{1,0:T(8,128)S(1)} %get-tuple-element.70.resid.refs_5_, bf16[640,640]{1,0:T(8,128)(2,1)} %bitcast.27, bf16[640,640]{1,0:T(8,128)(2,1)} %bitcast.23, ...), custom_call_target="tpu_custom_call", output_to_operand_aliasing={{0}: (4, {})} | custom-call | flops 4194304 | bytes 4165632 | tf_op jit(solution)/shard_map/pallas_call | solution.py:34
  57.0 0.0 collective-permute-done.10.refs_10_.refs_11_
  57.0 0.0 collective-permute-done.8.refs_8_
  57.0 0.4 collective-permute-done.9.refs_9_
  57.5 0.4 all-to-all-done.3
  57.9 2.1 %shard_map.94 = (f32[512,128]{1,0:T(8,128)}, f32[512,128]{1,0:T(8,128)}) custom-call(s32[1,1]{1,0:T(1,128)S(6)} %copy.17.live, s32[1,2]{1,0:T(1,128)S(1)} %get-tuple-element.42.margin_in.refs_3_, bf16[512,128]{1,0:T(8,128)(2,1)S(1)} %bitcast.15, bf16[64,512]{1,0:T(8,128)(2,1)S(1)} %get-tuple-element.52.refs_1_, ...), custom_call_target="tpu_custom_call" | custom-call | flops 4194304 | bytes 3665928 | tf_op jit(solution)/shard_map/pallas_call | solution.py:34
Async XLA Ops:
  2.4 5.9 %copy-start.1 = (bf16[1,1,640,16]{2,3,1,0:T(8,128)(2,1)S(1)}, bf16[1,1,640,16]{2,3,1,0:T(8,128)(2,1)}, u32[]{:S(2)}) copy-start(bf16[1,1,640,16]{2,3,1,0:T(8,128)(2,1)} %param.12) | copy-start | bytes 61444
  2.4 10.3 %all-to-all-start = ((bf16[4,144,128]{2,1,0:T(8,128)(2,1)}), bf16[4,144,128]{2,1,0:T(8,128)(2,1)S(1)}, u32[]{:S(2)}, u32[]{:S(2)}) async-start(bf16[4,144,128]{2,1,0:T(8,128)(2,1)} %get-tuple-element.43), calls=%async_computation | async-start | bytes 294912 | tf_op jit(solution)/shard_map/all_to_all | solution.py:521
  8.3 4.4 %copy-start = (f32[1,1,512,128]{3,2,1,0:T(8,128)S(1)}, f32[1,1,512,128]{3,2,1,0:T(8,128)}, u32[]{:S(2)}) copy-start(f32[1,1,512,128]{3,2,1,0:T(8,128)} %param.7) | copy-start | bytes 786436
  13.6 15.9 %all-to-all-start.1 = ((bf16[32,16,128]{2,1,0:T(8,128)(2,1)}), bf16[32,16,128]{2,1,0:T(8,128)(2,1)S(1)}, u32[]{:S(2)}, u32[]{:S(2)}) async-start(bf16[32,16,128]{2,1,0:T(8,128)(2,1)} %get-tuple-element.47), calls=%async_computation.1 | async-start | bytes 262144 | tf_op jit(solution)/shard_map/all_to_all | solution.py:542
  18.0 7.7 %collective-permute-start = (bf16[272,128]{1,0:T(8,128)(2,1)S(1)}, bf16[272,128]{1,0:T(8,128)(2,1)S(1)}, u32[]{:S(2)}, u32[]{:S(2)}) collective-permute-start(bf16[272,128]{1,0:T(8,128)(2,1)S(1)} %get-tuple-element.50), channel_id=1, source_target_pairs={{0,1},{1,2},{2,3},{3,0},{4,5},{5,6},{6,7},{7,4},{8,9},{9,10},{10,1... | collective-permute-start | bytes 208904 | tf_op jit(solution)/shard_map/ppermute | solution.py:495
  19.8 6.6 %collective-permute-start.1 = (bf16[272,128]{1,0:T(8,128)(2,1)S(1)}, bf16[272,128]{1,0:T(8,128)(2,1)S(1)}, u32[]{:S(2)}, u32[]{:S(2)}) collective-permute-start(bf16[272,128]{1,0:T(8,128)(2,1)S(1)} %get-tuple-element.51), channel_id=1, source_target_pairs={{0,3},{1,0},{2,1},{3,2},{4,7},{5,4},{6,5},{7,6},{8,11},{9,8},{10,9... | collective-permute-start | bytes 208904 | tf_op jit(solution)/shard_map/ppermute | solution.py:495
  20.9 8.5 %collective-permute-start.2 = (bf16[256,128]{1,0:T(8,128)(2,1)S(1)}, bf16[256,128]{1,0:T(8,128)(2,1)S(1)}, u32[]{:S(2)}, u32[]{:S(2)}) collective-permute-start(bf16[256,128]{1,0:T(8,128)(2,1)S(1)} %get-tuple-element.56.refs_6_), channel_id=1, source_target_pairs={{0,1},{1,2},{2,3},{3,0},{4,5},{5,6},{6,7},{7,4},{8,9},{9,10},{10,1... | collective-permute-start | bytes 196616 | tf_op jit(solution)/shard_map/ppermute | solution.py:495
  21.8 7.7 %collective-permute-start.3 = (bf16[256,128]{1,0:T(8,128)(2,1)S(1)}, bf16[256,128]{1,0:T(8,128)(2,1)S(1)}, u32[]{:S(2)}, u32[]{:S(2)}) collective-permute-start(bf16[256,128]{1,0:T(8,128)(2,1)S(1)} %get-tuple-element.57.refs_7_), channel_id=1, source_target_pairs={{0,3},{1,0},{2,1},{3,2},{4,7},{5,4},{6,5},{7,6},{8,11},{9,8},{10,9... | collective-permute-start | bytes 196616 | tf_op jit(solution)/shard_map/ppermute | solution.py:495
  23.9 5.6 %collective-permute-start.4 = (bf16[128,128]{1,0:T(8,128)(2,1)S(1)}, bf16[128,128]{1,0:T(8,128)(2,1)S(1)}, u32[]{:S(2)}, u32[]{:S(2)}) collective-permute-start(bf16[128,128]{1,0:T(8,128)(2,1)S(1)} %get-tuple-element.58), channel_id=1, source_target_pairs={{0,2},{1,3},{2,0},{3,1},{4,6},{5,7},{6,4},{7,5},{8,10},{9,11},{10,... | collective-permute-start | bytes 98312 | tf_op jit(solution)/shard_map/ppermute | solution.py:546
  31.5 12.3 %all-to-all-start.2 = ((bf16[32,16,128]{2,1,0:T(8,128)(2,1)}), bf16[32,16,128]{2,1,0:T(8,128)(2,1)S(1)}, u32[]{:S(2)}, u32[]{:S(2)}) async-start(bf16[32,16,128]{2,1,0:T(8,128)(2,1)} %get-tuple-element.60), calls=%async_computation.2 | async-start | bytes 262144 | tf_op jit(solution)/shard_map/all_to_all | solution.py:542
  35.6 7.0 %collective-permute-start.5 = (bf16[256,128]{1,0:T(8,128)(2,1)S(1)}, bf16[256,128]{1,0:T(8,128)(2,1)S(1)}, u32[]{:S(2)}, u32[]{:S(2)}) collective-permute-start(bf16[256,128]{1,0:T(8,128)(2,1)S(1)} %get-tuple-element.65.refs_6_), channel_id=1, source_target_pairs={{0,1},{1,2},{2,3},{3,0},{4,5},{5,6},{6,7},{7,4},{8,9},{9,10},{10,1... | collective-permute-start | bytes 196616 | tf_op jit(solution)/shard_map/ppermute | solution.py:495
  37.4 5.9 %collective-permute-start.6 = (bf16[256,128]{1,0:T(8,128)(2,1)S(1)}, bf16[256,128]{1,0:T(8,128)(2,1)S(1)}, u32[]{:S(2)}, u32[]{:S(2)}) collective-permute-start(bf16[256,128]{1,0:T(8,128)(2,1)S(1)} %get-tuple-element.66.refs_7_), channel_id=1, source_target_pairs={{0,3},{1,0},{2,1},{3,2},{4,7},{5,4},{6,5},{7,6},{8,11},{9,8},{10,9... | collective-permute-start | bytes 196616 | tf_op jit(solution)/shard_map/ppermute | solution.py:495
  38.6 4.1 %collective-permute-start.7 = (bf16[128,128]{1,0:T(8,128)(2,1)S(1)}, bf16[128,128]{1,0:T(8,128)(2,1)S(1)}, u32[]{:S(2)}, u32[]{:S(2)}) collective-permute-start(bf16[128,128]{1,0:T(8,128)(2,1)S(1)} %get-tuple-element.67), channel_id=1, source_target_pairs={{0,2},{1,3},{2,0},{3,1},{4,6},{5,7},{6,4},{7,5},{8,10},{9,11},{10,... | collective-permute-start | bytes 98312 | tf_op jit(solution)/shard_map/ppermute | solution.py:546
  45.7 12.2 %all-to-all-start.3 = ((bf16[32,16,128]{2,1,0:T(8,128)(2,1)}), bf16[32,16,128]{2,1,0:T(8,128)(2,1)S(1)}, u32[]{:S(2)}, u32[]{:S(2)}) async-start(bf16[32,16,128]{2,1,0:T(8,128)(2,1)} %get-tuple-element.69), calls=%async_computation.3 | async-start | bytes 262144 | tf_op jit(solution)/shard_map/all_to_all | solution.py:542
  49.7 7.3 %collective-permute-start.8 = (bf16[256,128]{1,0:T(8,128)(2,1)S(1)}, bf16[256,128]{1,0:T(8,128)(2,1)S(1)}, u32[]{:S(2)}, u32[]{:S(2)}) collective-permute-start(bf16[256,128]{1,0:T(8,128)(2,1)S(1)} %get-tuple-element.75.refs_6_), channel_id=1, source_target_pairs={{0,1},{1,2},{2,3},{3,0},{4,5},{5,6},{6,7},{7,4},{8,9},{9,10},{10,1... | collective-permute-start | bytes 196616 | tf_op jit(solution)/shard_map/ppermute | solution.py:495
  51.6 5.9 %collective-permute-start.9 = (bf16[256,128]{1,0:T(8,128)(2,1)S(1)}, bf16[256,128]{1,0:T(8,128)(2,1)S(1)}, u32[]{:S(2)}, u32[]{:S(2)}) collective-permute-start(bf16[256,128]{1,0:T(8,128)(2,1)S(1)} %get-tuple-element.76.refs_7_), channel_id=1, source_target_pairs={{0,3},{1,0},{2,1},{3,2},{4,7},{5,4},{6,5},{7,6},{8,11},{9,8},{10,9... | collective-permute-start | bytes 196616 | tf_op jit(solution)/shard_map/ppermute | solution.py:495
  52.7 4.3 %collective-permute-start.10 = (bf16[128,128]{1,0:T(8,128)(2,1)S(1)}, bf16[128,128]{1,0:T(8,128)(2,1)S(1)}, u32[]{:S(2)}, u32[]{:S(2)}) collective-permute-start(bf16[128,128]{1,0:T(8,128)(2,1)S(1)} %get-tuple-element.77), channel_id=1, source_target_pairs={{0,2},{1,3},{2,0},{3,1},{4,6},{5,7},{6,4},{7,5},{8,10},{9,11},{10,... | collective-permute-start | bytes 98312 | tf_op jit(solution)/shard_map/ppermute | solution.py:546

commit v7 on v6

--- a/solution.py
+++ b/solution.py
@@ -86,6 +86,8 @@
         self.picked = 2 * self.side
         self.stack = self.modes + 2 * self.picked
         self.folded = self.subs == 4
+        self.lead = self.modes + self.blk
+        self.opening = 2 if self.folded else 1
         self.segments = max(6, 2 + self.order // self.side)
 
     def base(self, position):
@@ -158,15 +160,19 @@
         z = self.z
         return jnp.concatenate([ref[z.owned : z.owned + z.blk, :], self.left_block(ref)], axis=0)
 
-    def add_lent(self, target, scale, from_left, from_right, source=None):
+    def add_lent(self, target, scale, from_left, from_right, source=None, rims=True):
         z = self.z
         source = target if source is None else source
-        for spot, value in (
-            (slice(z.owned, z.owned + z.blk), from_left[z.blk :]),
-            (slice(z.owned + z.blk, z.order), from_right[z.blk :]),
+        pieces = [
             (pl.ds(self.give_left, z.blk), from_left[: z.blk]),
             (pl.ds(self.give_right, z.blk), from_right[: z.blk]),
-        ):
+        ]
+        if rims:
+            pieces += [
+                (slice(z.owned, z.owned + z.blk), from_left[z.blk :]),
+                (slice(z.owned + z.blk, z.order), from_right[z.blk :]),
+            ]
+        for spot, value in pieces:
             target[spot, :] = source[spot, :] + (value if scale == 1.0 else scale * value)
 
 
@@ -189,7 +195,10 @@
 def first_kernel(
     z, source_far, vectors_far, panel_far, margin_far, operator_far, inverse_far, *refs
 ):
-    slots_far, lent, spot, operator, inverse, slots, *scratch = refs
+    if z.folded:
+        ahead_out, behind_out, lent, spot, operator, inverse, *scratch = refs
+    else:
+        slots_far, lent, spot, operator, inverse, slots, *scratch = refs
     source, vectors_t, panel, margin, sem = scratch
     loads = start_all(
         sem,
@@ -214,18 +223,30 @@
     loads[3].wait()
     ahead = jnp.concatenate([ahead_vectors, at.right_block(source).astype(BF16)], axis=0)
     behind = jnp.concatenate([behind_vectors, at.left_block(source).astype(BF16)], axis=0)
-    for k in range(z.subs):
-        first = min(max(k - 2, 0), z.subs - z.near) * z.modes
-        for chunk in range(z.chunks):
-            slots[k, chunk * z.window : (chunk + 1) * z.window, :] = panel[
-                chunk, first : first + z.window, :
-            ]
-        slots[k, z.wide :, :] = jnp.where(k > at.position, ahead, behind)
-    store = pltpu.make_async_copy(slots, slots_far, sem.at[7])
-    store.start()
+    if z.folded:
+        for out, value in ((ahead_out, ahead), (behind_out, behind)):
+            out[: z.lead, :] = value
+            put_panel(z, out, z.lead, panel)
+    else:
+        for k in range(z.subs):
+            first = min(max(k - 2, 0), z.subs - z.near) * z.modes
+            for chunk in range(z.chunks):
+                slots[k, chunk * z.window : (chunk + 1) * z.window, :] = panel[
+                    chunk, first : first + z.window, :
+                ]
+            slots[k, z.wide :, :] = jnp.where(k > at.position, ahead, behind)
+        store = pltpu.make_async_copy(slots, slots_far, sem.at[7])
+        store.start()
     loads[5].wait()
     loads[6].wait()
-    store.wait()
+    if not z.folded:
+        store.wait()
+
+
+def put_panel(z, out, start, panel):
+    for chunk in range(z.chunks):
+        first = start + chunk * z.window
+        out[first : first + z.window, :] = panel[chunk, :, :]
 
 
 def static_kernel(z, live, operator, inverse, margin_in, vectors_t, *refs):
@@ -275,17 +296,23 @@
     first[:side, :], second[:side, :] = pieces[0], pieces[1]
     first[side:, :], second[side:, :] = pieces[2], pieces[3]
     if z.folded:
-        far[0][...] = jnp.where(at.has_right2, pieces[0], pieces[1])
+        far[0][:side, :] = jnp.where(at.has_right2, pieces[0], pieces[1])
     else:
         far[0][...], far[1][...] = pieces[0], pieces[1]
     return copy
 
 
-def second_kernel(z, live, slots, source, stack, resid, every_out, first, second, *rest):
+def second_kernel(z, live, source, stack, *refs):
+    at = Place(z, live)
+    if z.folded:
+        left_open, right_open, lent, panel, *refs = refs
+        left, right = left_open[z.modes : z.lead, :], right_open[z.modes : z.lead, :]
+    else:
+        slots, *refs = refs
+        left = slots[jnp.maximum(at.position - 1, 0), z.wide + z.modes :, :]
+        right = slots[jnp.minimum(at.position + 1, z.subs - 1), z.wide + z.modes :, :]
+    resid, every_out, first, second, *rest = refs
     far, (copies, sem) = rest[:-2], rest[-2:]
-    at = Place(z, live)
-    left = slots[jnp.maximum(at.position - 1, 0), z.wide + z.modes :, :]
-    right = slots[jnp.minimum(at.position + 1, z.subs - 1), z.wide + z.modes :, :]
     value = jnp.concatenate(
         [
             jnp.where(at.row_mask(), source[...], 0.0),
@@ -296,7 +323,12 @@
     )
     resid[...] = value
     low = value.astype(BF16)
-    send(z, at, stack, low, None, copies, every_out, sem, first, second, far).wait()
+    store = send(z, at, stack, low, None, copies, every_out, sem, first, second, far)
+    if z.folded:
+        mine = jnp.where(at.has_right2, lent[: z.modes, :], lent[z.modes :, :])
+        far[0][z.side : z.side + z.modes, :] = mine
+        put_panel(z, far[0], z.side + z.modes, panel)
+    store.wait()
 
 
 def window_kernel(z, turn, live, resid, inverse_far, operator_far, *refs):
@@ -308,8 +340,10 @@
         inverse, operator, direction, solution, sem = refs
         more = [(solution_far, solution)] if turn > 1 else []
     else:
-        slots, lent, stack, margin_in, left_static, right_static, *refs = refs
-        part, product, spread, panels, columns, inverse, operator, margin, sem = refs
+        opening, refs = refs[: z.opening], refs[z.opening :]
+        lent, stack, margin_in, left_static, right_static, *refs = refs
+        part, product, spread, columns, *refs = refs
+        panels, (inverse, operator, margin, sem) = refs[:-4], refs[-4:]
         more = [(margin_in, margin)]
     loads = start_all(sem, (inverse_far, inverse), (operator_far, operator), *more)
     at = Place(z, live)
@@ -325,19 +359,20 @@
         store = pltpu.make_async_copy(solution, solution_out, sem.at[3])
         store.start()
     else:
-        for k in range(z.subs):
-            for chunk in range(z.chunks):
-                start = (k * z.chunks + chunk) * z.loads
-                panels[:, start : start + z.loads] = slots[
-                    k, chunk * z.window : (chunk + 1) * z.window, :
-                ]
+        if not z.folded:
+            for k in range(z.subs):
+                for chunk in range(z.chunks):
+                    start = (k * z.chunks + chunk) * z.loads
+                    panels[0][:, start : start + z.loads] = opening[0][
+                        k, chunk * z.window : (chunk + 1) * z.window, :
+                    ]
         loads[2].wait()
         picks = Place(z, live, margin).lent_columns()
         loads[1].wait()
         columns[...] = mm(operator[...], picks).astype(BF16)
         masked = (stack[: z.modes, :].astype(F32) * at.kept_columns()).astype(BF16)
         lifted = nt(masked, operator[...]).astype(BF16)
-        spread_corrections(z, at, slots, lent, lifted, left_static, right_static, spread)
+        spread_corrections(z, at, opening, lent, lifted, left_static, right_static, spread)
     loads[0].wait()
     value = at.kept(mm(inverse[...], resid[...].astype(BF16)))
     if turn:
@@ -350,23 +385,25 @@
         store.wait()
 
 
-def spread_corrections(z, at, slots, lent, lifted, left_static, right_static, spread):
+def spread_corrections(z, at, opening, lent, lifted, left_static, right_static, spread):
     side, modes = z.side, z.modes
     row = lax.broadcasted_iota(jnp.int32, (modes, 2 * z.window), 0)
     col = lax.broadcasted_iota(jnp.int32, (modes, 2 * z.window), 1)
     base = z.base(at.position)
 
     def theirs(offset):
+        if z.folded:
+            return opening[0 if offset < 0 else 1][:modes, :]
         index = jnp.clip(at.position + offset, 0, z.subs - 1)
-        return slots[index, z.wide : z.wide + modes, :]
+        return opening[0][index, z.wide : z.wide + modes, :]
 
     left, right = left_static[2 * side :, :], right_static[2 * side :, :]
     halves = (
         [
             (theirs(-1), -1, at.has_left),
             (theirs(1), 1, at.has_right),
-            (theirs(-2), -2, at.has_left2),
-            (theirs(2), 2, at.has_right2),
+            None if z.folded else (theirs(-2), -2, at.has_left2),
+            None if z.folded else (theirs(2), 2, at.has_right2),
             (lent[:modes, :], 0, True),
             (lent[modes:, :], 0, True),
         ],
@@ -376,7 +413,7 @@
     for segment in range(z.segments):
         total = jnp.zeros((side, 2 * z.window), F32)
         for half, entries in enumerate(halves):
-            if segment < len(entries):
+            if segment < len(entries) and entries[segment] is not None:
                 transposed, offset, have = entries[segment]
                 first = half * z.window + (at.position + offset - base) * modes
                 place = jnp.where(have, 1.0, 0.0) * jnp.where(col == first + row, 1.0, 0.0)
@@ -386,9 +423,15 @@
 
 def main_kernel(z, turn, live, margin_in, *refs):
     last = turn == ITERS - 1
-    every, panels, spread, columns, product, resid_in, *refs = refs
+    gather = z.folded and not turn
+    if gather:
+        every, left_open, right_open, panel, spread, columns, product, resid_in, *refs = refs
+    else:
+        every, panels, spread, columns, product, resid_in, *refs = refs
     ahead_in, behind_in, left_got, right_got, *refs = refs
     far_left, far_right, left_static, right_static, *refs = refs
+    if z.folded:
+        far_static, *refs = refs
     if last:
         part, stack, solution_far, solution_out, resid_out, *refs = refs
         margin, error, resid, direction, solution, sem = refs
@@ -396,10 +439,30 @@
     else:
         part, stack, resid, every_out, first, second, *refs = refs
         far, (coarse_out, part_out, margin, error, copies, sem) = refs[:-6], refs[-6:]
+        if gather:
+            far, panels = far[:-1], far[-1]
         loads = start_all(sem, (margin_in, margin))
     at = Place(z, live)
     side, owned, modes = z.side, z.owned, z.modes
 
+    if gather:
+        start = z.side + modes
+        pieces = (
+            panel[...].reshape(z.wide, z.loads),
+            right_open[z.lead :, :],
+            far_left[start:, :],
+            left_open[z.lead :, :],
+        )
+        for k in range(z.subs):
+            turns = (k + z.subs - at.position) % z.subs
+            piece = pieces[0]
+            for index in range(1, z.subs):
+                piece = jnp.where(turns == index, pieces[index], piece)
+            for chunk in range(z.chunks):
+                start = (k * z.chunks + chunk) * z.loads
+                panels[:, start : start + z.loads] = piece[
+                    chunk * z.window : (chunk + 1) * z.window, :
+                ]
     coarse = jnp.zeros((z.window, z.loads), F32)
     for start in range(0, panels.shape[1], 4 * z.loads):
         stop = min(start + 4 * z.loads, panels.shape[1])
@@ -410,14 +473,14 @@
         [jnp.concatenate([coarse, nothing], axis=1), jnp.concatenate([nothing, coarse], axis=1)],
         axis=0,
     )
-    taken = mm(spread[...], twice)
+    rows = owned if last else z.order
+    taken = mm(spread[: max(6 * side, 2 * side + rows), :], twice)
 
     def term(segment):
         return taken[segment * side : (segment + 1) * side, : z.loads]
 
-    def other_term(start, rows):
-        return taken[start : start + rows, z.loads :]
-
+    def other_term(start, count):
+        return taken[start : start + count, z.loads :]
 
     def masked(have, value):
         return jnp.where(have, value.astype(F32), 0.0)
@@ -425,36 +488,54 @@
     from_left = masked(at.has_left, left_got[:side, :]) + term(0)
     from_right = masked(at.has_right, right_got[:side, :]) + term(1)
     halo = jnp.concatenate([from_left, from_right], axis=0)
-    from_left2 = masked(at.has_left2, far_left[...]) + term(2)
-    from_right2 = masked(at.has_right2, far_right[...]) + term(3)
+
+    def correction(offset):
+        index = jnp.clip(at.position + offset - z.base(at.position), 0, z.near - 1)
+        error[: z.window, :] = coarse.astype(F32)
+        return error[pl.ds(pl.multiple_of(index * modes, modes), modes), :].astype(BF16)
+
+    if z.folded:
+        there = correction(jnp.where(at.has_left2, -2, 2))
+        from_far = far_left[:side, :].astype(F32) + tn(far_static[side : side + modes, :], there)
+        from_left2, from_right2 = masked(at.has_left2, from_far), masked(at.has_right2, from_far)
+    else:
+        from_left2 = masked(at.has_left2, far_left[...]) + term(2)
+        from_right2 = masked(at.has_right2, far_right[...]) + term(3)
     loads[0].wait()
     at.lend(margin[0, 0], margin[0, 1])
     to_right = (ahead_in[:side, :].astype(F32) + term(4)).astype(BF16)
     to_left = (behind_in[:side, :].astype(F32) + term(5)).astype(BF16)
     if last:
-        index = at.position - z.base(at.position)
-        error[: z.window, :] = coarse.astype(F32)
-        own = error[pl.ds(pl.multiple_of(index * modes, modes), modes), :].astype(BF16)
-        direction[...] = part[...] + at.kept(tn(stack[:modes, :], own))
-        at.add_lent(direction, 1.0, from_left, from_right)
+        lifted = tn(stack[:modes, :owned], correction(0))
+        lifted = jnp.where(at.row_mask(), lifted, 0.0)
+        direction[...] = part[:owned, :] + lifted
+        at.add_lent(direction, 1.0, from_left, from_right, rims=False)
         loads[1].wait()
-        solution[...] = solution[...] + STEP_SIZES[turn] * direction[:owned, :]
+        solution[...] = solution[...] + STEP_SIZES[turn] * direction[...]
         store_solution = pltpu.make_async_copy(solution, solution_out, sem.at[2])
         store_solution.start()
 
+    count = z.blk if last else side
+
     def borrowed(have, got, statics, far, near, start):
-        rows = jnp.concatenate([statics[:side, :], statics[side : 2 * side, :]], axis=1)
-        value = mm(rows, jnp.concatenate([far.astype(BF16), near], axis=0))
-        return masked(have, value + got[side:, :].astype(F32)) + other_term(start, side)
-
-    applied = product[...] + other_term(2 * side, z.order) + mm(columns[...], halo.astype(BF16))
+        both = jnp.concatenate([statics[:count, :], statics[side : side + count, :]], axis=1)
+        value = mm(both, jnp.concatenate([far.astype(BF16), near], axis=0))
+        value = masked(have, value + got[side : side + count, :].astype(F32))
+        return value + other_term(start, count)
+
+    applied = product[:rows, :] + other_term(2 * side, rows)
+    applied = applied + mm(columns[:rows, :], halo.astype(BF16))
     left = borrowed(at.has_left, left_got, left_static, from_left2, to_left, 0)
     right = borrowed(at.has_right, right_got, right_static, from_right2, to_right, side)
-    error[...] = applied
-    resid[...] = resid_in[...] - STEP_SIZES[turn] * at.kept(applied)
-    at.add_lent(resid, -STEP_SIZES[turn], left, right)
     if last:
-        store = pltpu.make_async_copy(resid.at[pl.ds(0, owned), :], resid_out, sem.at[3])
+        applied = jnp.where(at.row_mask(), applied, 0.0)
+        resid[...] = resid_in[:owned, :] - STEP_SIZES[turn] * applied
+    else:
+        error[...] = applied
+        resid[...] = resid_in[...] - STEP_SIZES[turn] * at.kept(applied)
+    at.add_lent(resid, -STEP_SIZES[turn], left, right, rims=not last)
+    if last:
+        store = pltpu.make_async_copy(resid, resid_out, sem.at[3])
         store.start()
         store.wait()
         store_solution.wait()
@@ -498,10 +579,11 @@
         return [(i, (i + offset) % z.subs) for i in range(z.subs)]
 
     panel = coarse_inverse.reshape(-1, z.chunks, loads).swapaxes(0, 1)
-    slots, lent, spot, operator_near, inverse_near = run(
+    lead = z.lead + z.wide
+    *opening, lent, spot, operator_near, inverse_near = run(
         part(first_kernel),
-        [
-            Far(low(z.subs, z.wide + modes + z.blk, loads)),
+        ([low(lead, loads)] * 2 if z.folded else [Far(low(z.subs, lead, loads))])
+        + [
             low(2 * modes, side),
             shape(1, margin_blocks.shape[-1], dtype=jnp.int32),
             low(order, order),
@@ -509,8 +591,8 @@
         ],
         [Far(source), Far(vectors_t), Far(panel), margin, operator, inverse],
         (),
-        [
-            pltpu.VMEM((z.subs, z.wide + modes + z.blk, loads), BF16),
+        ([] if z.folded else [pltpu.VMEM((z.subs, lead, loads), BF16)])
+        + [
             pltpu.VMEM(source.shape, F32),
             pltpu.VMEM(vectors_t.shape, BF16),
             pltpu.VMEM(panel.shape, BF16),
@@ -518,7 +600,10 @@
             sems((8,)),
         ],
     )
-    slots = lax.all_to_all(slots, "sub", 0, 0, tiled=True)
+    if z.folded:
+        opening = exchange(*opening)
+    else:
+        opening = [lax.all_to_all(opening[0], "sub", 0, 0, tiled=True)]
     stack, first, second = run(
         part(static_kernel),
         [low(z.stack, order)]
@@ -532,7 +617,11 @@
     sent += [low(2 * side, loads)] * 2 + [low(side, loads)] * (1 if z.folded else 2)
     copies = pltpu.VMEM((devices, modes, loads), BF16)
     resid, every, first, second, *far = run(
-        part(second_kernel), sent, [slots, source, stack], scalars, [copies, sems(())]
+        part(second_kernel),
+        sent[:4] + [low(side + modes + z.wide, loads)] if z.folded else sent,
+        [source, stack, *opening] + ([lent, panel] if z.folded else []),
+        scalars,
+        [copies, sems(())],
     )
     full = shape(order, loads)
     floor = pltpu.VMEM((order, loads), F32)
@@ -540,13 +629,14 @@
     for turn in range(ITERS):
         last = turn == ITERS - 1
         every = lax.all_to_all(every, ("sub", "grp"), 0, 0, tiled=True)
-        every = every.reshape(devices * modes, loads)
-        left_got, right_got = exchange(first, second)
+        left_got = lax.ppermute(first, "sub", ring(1))
+        right_got = lax.ppermute(second, "sub", ring(-1))
         if z.folded:
             far_left = far_right = lax.ppermute(far[0], "sub", ring(2))
         else:
             far_left = lax.ppermute(far[0], "sub", ring(2))
             far_right = lax.ppermute(far[1], "sub", ring(-2))
+        every = every.reshape(devices * modes, loads)
         args = [resid, inverse, operator]
         if turn:
             args += [error, coarse, stack]
@@ -554,9 +644,11 @@
             outs = [full, full, Far(shape(owned, loads))]
             work = [square, square, floor, pltpu.VMEM((owned, loads), F32), sems((4,))]
         else:
-            args += [slots, lent, stack, spot, left_static, right_static]
-            outs = [full, full, low(z.segments * side, 2 * z.window)]
-            outs += [low(z.window, z.subs * z.chunks * loads), low(order, 2 * side)]
+            args += [*opening, lent, stack, spot, left_static, right_static]
+            far_static = [far_left] if z.folded else []
+            outs = [full, full, low(z.segments * side, 2 * z.window), low(order, 2 * side)]
+            packed = low(z.window, z.subs * z.chunks * loads)
+            outs += [] if z.folded else [packed]
             work = [square, square, pick, sems((3,))]
         error, product, *more = run(
             part(window_kernel, turn),
@@ -569,20 +661,22 @@
         if turn:
             solution = Far(more[0])
         else:
-            spread, panels, columns = more
-        args = [spot, every, panels, spread, columns, product, resid]
+            spread, columns, *panels = more
+            panels = panels or [*opening, panel]
+        args = [spot, every, *panels, spread, columns, product, resid]
         args += [first, second, left_got, right_got, far_left, far_right]
-        args += [left_static, right_static]
+        args += [left_static, right_static, *far_static]
         if last:
             solution, resid = run(
                 part(main_kernel, turn),
                 [Far(shape(owned, loads))] * 2,
                 args + [error, stack, solution],
                 scalars,
-                [pick, floor, floor, floor, pltpu.VMEM((owned, loads), F32), sems((4,))],
+                [pick, floor] + [pltpu.VMEM((owned, loads), F32)] * 3 + [sems((4,))],
             )
         else:
-            outs = sent + [low(z.window, loads), full]
+            gather = z.folded and not turn
+            outs = sent + [packed] * gather + [low(z.window, loads), full]
             resid, every, first, second, *far, coarse, error = run(
                 part(main_kernel, turn),
                 outs,
@@ -591,6 +685,9 @@
                 [pick, floor, copies, sems((3,))],
                 aliases={len(scalars) + len(args): len(outs) - 1},
             )
+            if gather:
+                *far, panels = far
+                panels = [panels]
     return (solution[None, None], resid[None, None])
 
 

time: 60.6 us -> 58.4 us (0.964)
  waiting for transfers between devices: 6.1 us -> 3.96 us
    ppermute x0 -> x6, starting transfers between devices: none -> 8.88 us  [the longest x3 4.51 us: body(): left_got = lax.ppermute(first, 'sub', ring(1))]
    all_to_all x1 -> x0, starting transfers between devices: 5.2 us -> none  [body(): slots = lax.all_to_all(slots, 'sub', 0, 0, tiled=True)]
    ppermute x4 -> x2, starting transfers between devices: 5.53 us -> 2.18 us  [exchange(): lax.ppermute(second, 'sub', ring(-1))]
    all_to_all x1 -> x0, waiting for transfers between devices: 3.19 us -> none  [body(): slots = lax.all_to_all(slots, 'sub', 0, 0, tiled=True)]
    ppermute x4 -> x2, starting transfers between devices: 6.33 us -> 4.84 us  [exchange(): lax.ppermute(first, 'sub', ring(1))]
    all_to_all x3, starting transfers between devices: 12.5 us -> 13.9 us  [body(): every = lax.all_to_all(every, ('sub', 'grp'), 0, 0, tiled=True)]
    ppermute x0 -> x6, waiting for transfers between devices: none -> 1.14 us  [the longest x3 1.13 us: body(): right_got = lax.ppermute(second, 'sub', ring(-1))]
    ppermute x4 -> x2, waiting for transfers between devices: 1.92 us -> 1.82 us  [exchange(): lax.ppermute(second, 'sub', ring(-1))]
  transfers between devices with their start and end apart: 15 -> 16, of which waited for: 7 -> 7; matrix products, arithmetic and copies ran while one was open for 0% -> 0% of each run, Pallas kernels for 15% -> 15%
where the time goes in v7:
time: 58.4 us; the launch traced here: 58 us
  starting transfers between devices  35.1 us (60%)
  Pallas kernels  17.4 us (30%)
  waiting for transfers between devices  3.96 us (7%)
  between operations  1.47 us (3%)
    pallas_call x9, Pallas kernels, run(): pl.pallas_call(kernel, out_shape=[held(x) for x in outs], in_specs=[pl.Bl...  17.4 us
    all_to_all x3, starting transfers between devices, body(): every = lax.all_to_all(every, ('sub', 'grp'), 0, 0, tiled=True)  13.9 us
    ppermute x3, starting transfers between devices, body(): far_left = far_right = lax.ppermute(far[0], 'sub', ring(2))  5.31 us
    ppermute x2, starting transfers between devices, exchange(): lax.ppermute(first, 'sub', ring(1))  4.84 us
    ppermute x3, starting transfers between devices, body(): left_got = lax.ppermute(first, 'sub', ring(1))  4.51 us
    ppermute x3, starting transfers between devices, body(): right_got = lax.ppermute(second, 'sub', ring(-1))  4.37 us
    ppermute x2, starting transfers between devices, exchange(): lax.ppermute(second, 'sub', ring(-1))  2.18 us
    ppermute x2, waiting for transfers between devices, exchange(): lax.ppermute(second, 'sub', ring(-1))  1.82 us
  transfers between devices with their start and end apart: 16, of which 7 were waited for; matrix products, arithmetic and copies ran while one was open for 0% of the time, Pallas kernels for 15%

profile of v7, /device:TPU:0, one launch (start us, length us, event | category | flops | bytes accessed | tf_op | source)
XLA Modules:
  0.0 58.0 jit_solution(15557509386401875463)
XLA Ops:
  0.6 0.0 copy-start.2
  0.6 1.6 %shard_map.86 = (bf16[144,128]{1,0:T(8,128)(2,1)S(1)}, bf16[144,128]{1,0:T(8,128)(2,1)S(1)}, bf16[32,128]{1,0:T(8,128)(2,1)S(1)}, s32[1,2]{1,0:T(1,128)S(1)}, bf...) custom-call(f32[512,128]{1,0:T(8,128)} %bitcast.13, bf16[16,640]{1,0:T(8,128)(2,1)} %bitcast.21, ...), custom_call_target="tpu_custom_call" | custom-call | flops 4194304 | bytes 3657744 | tf_op jit(solution)/shard_map/pallas_call | solution.py:34
  2.2 3.0 %collective-permute-start = (bf16[144,128]{1,0:T(8,128)(2,1)S(1)}, bf16[144,128]{1,0:T(8,128)(2,1)S(1)}, u32[]{:S(2)}, u32[]{:S(2)}) collective-permute-start(bf16[144,128]{1,0:T(8,128)(2,1)S(1)} %get-tuple-element.47), channel_id=1, source_target_pairs={{0,1},{1,2},{2,3},{3,0},{4,5},{5,6},{6,7},{7,4},{8,9},{9,10},{10,1... | collective-permute-start | bytes 110600 | tf_op jit(solution)/shard_map/ppermute | solution.py:576
  5.3 1.0 %collective-permute-start.1 = (bf16[144,128]{1,0:T(8,128)(2,1)S(1)}, bf16[144,128]{1,0:T(8,128)(2,1)S(1)}, u32[]{:S(2)}, u32[]{:S(2)}) collective-permute-start(bf16[144,128]{1,0:T(8,128)(2,1)S(1)} %get-tuple-element.48), channel_id=1, source_target_pairs={{0,3},{1,0},{2,1},{3,2},{4,7},{5,4},{6,5},{7,6},{8,11},{9,8},{10,9... | collective-permute-start | bytes 110600 | tf_op jit(solution)/shard_map/ppermute | solution.py:576
  6.9 0.0 copy-done.2
  6.9 0.0 copy-start
  7.0 0.0 copy-start.1
  7.0 1.2 %shard_map.87 = (bf16[528,640]{1,0:T(8,128)(2,1)S(1)}, bf16[272,128]{1,0:T(8,128)(2,1)S(1)}, bf16[272,128]{1,0:T(8,128)(2,1)S(1)}) custom-call(s32[1,1]{1,0:T(1,128)S(6)} %copy.17.live, bf16[640,640]{1,0:T(8,128)(2,1)S(1)} %get-tuple-element.44.operator, bf16[640,640]{1,0:T(8,128)(2,1)S(1)} %get-tuple-element.45.inverse, ...), custom_call_target="tpu_custom_call" | custom-call | flops 4194304 | bytes 2473992 | tf_op jit(solution)/shard_map/pallas_call | solution.py:34
  8.2 0.0 collective-permute-done.refs_0_.refs_1_
  8.2 1.0 %collective-permute-done.1.refs_1_.refs_2_ = bf16[144,128]{1,0:T(8,128)(2,1)S(1)} collective-permute-done((bf16[144,128]{1,0:T(8,128)(2,1)S(1)}, bf16[144,128]{1,0:T(8,128)(2,1)S(1)}, u32[]{:S(2)}, u32[]{:S(2)}) %collective-permute-start.1) | collective-permute-done | bytes 36896 | tf_op jit(solution)/shard_map/ppermute | solution.py:576
  9.2 0.0 copy-done
  9.2 0.0 copy-done.1
  9.2 0.9 %shard_map.88 = (f32[640,128]{1,0:T(8,128)S(1)}, bf16[32,16,128]{2,1,0:T(8,128)(2,1)}, bf16[256,128]{1,0:T(8,128)(2,1)S(1)}, bf16[256,128]{1,0:T(8,128)(2,1)S(1)}, bf16[208,128]{1,0:T(8,128)(2,1)S(1)}) custom-call(s32[1,1]{1,0:T(1,128)S(6)} %copy.17.live, f32[512,128]{1,0:T(8,128)S(1)} %bitcast.14, ...), custom_call_target="tpu_custom_call" | custom-call | flops 4194304 | bytes 1679360 | tf_op jit(solution)/shard_map/pallas_call | solution.py:34
  10.2 5.8 %all-to-all-start = ((bf16[32,16,128]{2,1,0:T(8,128)(2,1)}), bf16[32,16,128]{2,1,0:T(8,128)(2,1)S(1)}, u32[]{:S(2)}, u32[]{:S(2)}) async-start(bf16[32,16,128]{2,1,0:T(8,128)(2,1)} %get-tuple-element.50), calls=%async_computation | async-start | bytes 262144 | tf_op jit(solution)/shard_map/all_to_all | solution.py:631
  16.0 1.8 %collective-permute-start.2 = (bf16[272,128]{1,0:T(8,128)(2,1)S(1)}, bf16[272,128]{1,0:T(8,128)(2,1)S(1)}, u32[]{:S(2)}, u32[]{:S(2)}) collective-permute-start(bf16[272,128]{1,0:T(8,128)(2,1)S(1)} %get-tuple-element.52), channel_id=1, source_target_pairs={{0,1},{1,2},{2,3},{3,0},{4,5},{5,6},{6,7},{7,4},{8,9},{9,10},{10,1... | collective-permute-start | bytes 208904 | tf_op jit(solution)/shard_map/ppermute | solution.py:576
  17.8 1.2 %collective-permute-start.3 = (bf16[272,128]{1,0:T(8,128)(2,1)S(1)}, bf16[272,128]{1,0:T(8,128)(2,1)S(1)}, u32[]{:S(2)}, u32[]{:S(2)}) collective-permute-start(bf16[272,128]{1,0:T(8,128)(2,1)S(1)} %get-tuple-element.53), channel_id=1, source_target_pairs={{0,3},{1,0},{2,1},{3,2},{4,7},{5,4},{6,5},{7,6},{8,11},{9,8},{10,9... | collective-permute-start | bytes 208904 | tf_op jit(solution)/shard_map/ppermute | solution.py:576
  18.9 0.9 %collective-permute-start.4 = (bf16[256,128]{1,0:T(8,128)(2,1)S(1)}, bf16[256,128]{1,0:T(8,128)(2,1)S(1)}, u32[]{:S(2)}, u32[]{:S(2)}) collective-permute-start(bf16[256,128]{1,0:T(8,128)(2,1)S(1)} %get-tuple-element.57.refs_8_), channel_id=1, source_target_pairs={{0,1},{1,2},{2,3},{3,0},{4,5},{5,6},{6,7},{7,4},{8,9},{9,10},{10,1... | collective-permute-start | bytes 196616 | tf_op jit(solution)/shard_map/ppermute | solution.py:632
  19.8 2.1 %collective-permute-start.5 = (bf16[256,128]{1,0:T(8,128)(2,1)S(1)}, bf16[256,128]{1,0:T(8,128)(2,1)S(1)}, u32[]{:S(2)}, u32[]{:S(2)}) collective-permute-start(bf16[256,128]{1,0:T(8,128)(2,1)S(1)} %get-tuple-element.58.refs_9_), channel_id=1, source_target_pairs={{0,3},{1,0},{2,1},{3,2},{4,7},{5,4},{6,5},{7,6},{8,11},{9,8},{10,9... | collective-permute-start | bytes 196616 | tf_op jit(solution)/shard_map/ppermute | solution.py:633
  21.9 1.8 %collective-permute-start.6 = (bf16[208,128]{1,0:T(8,128)(2,1)S(1)}, bf16[208,128]{1,0:T(8,128)(2,1)S(1)}, u32[]{:S(2)}, u32[]{:S(2)}) collective-permute-start(bf16[208,128]{1,0:T(8,128)(2,1)S(1)} %get-tuple-element.59), channel_id=1, source_target_pairs={{0,2},{1,3},{2,0},{3,1},{4,6},{5,7},{6,4},{7,5},{8,10},{9,11},{10,... | collective-permute-start | bytes 159752 | tf_op jit(solution)/shard_map/ppermute | solution.py:635
  23.6 0.0 collective-permute-done.2.refs_5_.refs_14_.refs_12_
  23.6 0.8 %collective-permute-done.3.refs_6_.refs_15_.refs_13_ = bf16[272,128]{1,0:T(8,128)(2,1)S(1)} collective-permute-done((bf16[272,128]{1,0:T(8,128)(2,1)S(1)}, bf16[272,128]{1,0:T(8,128)(2,1)S(1)}, u32[]{:S(2)}, u32[]{:S(2)}) %collective-permute-start.3) | collective-permute-done | bytes 69664 | tf_op jit(solution)/shard_map/ppermute | solution.py:576
  24.4 3.0 %shard_map.89 = (f32[640,128]{1,0:T(8,128)S(1)}, f32[640,128]{1,0:T(8,128)S(1)}, bf16[896,128]{1,0:T(8,128)(2,1)S(1)}, bf16[640,256]{1,0:T(8,128)(2,1)S(1)}) custom-call(s32[1,1]{1,0:T(1,128)S(6)} %copy.17.live, f32[640,128]{1,0:T(8,128)S(1)} %get-tuple-element.51.resid.refs_7_, bf16[640,640]{1,0:T(8,128)(2,1)} %bitcast.28, bf16[640,640]{1,0:T(8,128)(2,1)} %bitcast.24, ...), custom_call_target="tpu_custom_call" | custom-call | flops 4194304 | bytes 4075528 | tf_op jit(solution)/shard_map/pallas_call | solution.py:34
  27.4 0.0 collective-permute-done.6.refs_12_.refs_13_.refs_16_.refs_14_
  27.5 0.0 collective-permute-done.4.refs_10_
  27.5 0.0 collective-permute-done.5.refs_11_
  27.5 0.0 all-to-all-done
  27.5 1.7 %shard_map.90 = (f32[640,128]{1,0:T(8,128)S(1)}, bf16[32,16,128]{2,1,0:T(8,128)(2,1)}, bf16[256,128]{1,0:T(8,128)(2,1)S(1)}, bf16[256,128]{1,0:T(8,128)(2,1)S(1)...) custom-call(s32[1,1]{1,0:T(1,128)S(6)} %copy.17.live, ...), custom_call_target="tpu_custom_call", output_to_operand_aliasing={{7}: (19, {})} | custom-call | flops 4194304 | bytes 4030472 | tf_op jit(solution)/shard_map/pallas_call | solution.py:34
  29.2 4.1 %all-to-all-start.1 = ((bf16[32,16,128]{2,1,0:T(8,128)(2,1)}), bf16[32,16,128]{2,1,0:T(8,128)(2,1)S(1)}, u32[]{:S(2)}, u32[]{:S(2)}) async-start(bf16[32,16,128]{2,1,0:T(8,128)(2,1)} %get-tuple-element.61), calls=%async_computation.1 | async-start | bytes 262144 | tf_op jit(solution)/shard_map/all_to_all | solution.py:631
  33.4 1.8 %collective-permute-start.7 = (bf16[256,128]{1,0:T(8,128)(2,1)S(1)}, bf16[256,128]{1,0:T(8,128)(2,1)S(1)}, u32[]{:S(2)}, u32[]{:S(2)}) collective-permute-start(bf16[256,128]{1,0:T(8,128)(2,1)S(1)} %get-tuple-element.67.refs_6_), channel_id=1, source_target_pairs={{0,1},{1,2},{2,3},{3,0},{4,5},{5,6},{6,7},{7,4},{8,9},{9,10},{10,1... | collective-permute-start | bytes 196616 | tf_op jit(solution)/shard_map/ppermute | solution.py:632
  35.2 1.2 %collective-permute-start.8 = (bf16[256,128]{1,0:T(8,128)(2,1)S(1)}, bf16[256,128]{1,0:T(8,128)(2,1)S(1)}, u32[]{:S(2)}, u32[]{:S(2)}) collective-permute-start(bf16[256,128]{1,0:T(8,128)(2,1)S(1)} %get-tuple-element.68.refs_7_), channel_id=1, source_target_pairs={{0,3},{1,0},{2,1},{3,2},{4,7},{5,4},{6,5},{7,6},{8,11},{9,8},{10,9... | collective-permute-start | bytes 196616 | tf_op jit(solution)/shard_map/ppermute | solution.py:633
  36.3 1.8 %collective-permute-start.9 = (bf16[128,128]{1,0:T(8,128)(2,1)S(1)}, bf16[128,128]{1,0:T(8,128)(2,1)S(1)}, u32[]{:S(2)}, u32[]{:S(2)}) collective-permute-start(bf16[128,128]{1,0:T(8,128)(2,1)S(1)} %get-tuple-element.69), channel_id=1, source_target_pairs={{0,2},{1,3},{2,0},{3,1},{4,6},{5,7},{6,4},{7,5},{8,10},{9,11},{10,... | collective-permute-start | bytes 98312 | tf_op jit(solution)/shard_map/ppermute | solution.py:635
  38.1 2.2 %shard_map.91 = (f32[640,128]{1,0:T(8,128)S(1)}, f32[640,128]{1,0:T(8,128)S(1)}, f32[512,128]{1,0:T(8,128)}) custom-call(s32[1,1]{1,0:T(1,128)S(6)} %copy.17.live, f32[640,128]{1,0:T(8,128)S(1)} %get-tuple-element.63.resid.refs_5_, bf16[640,640]{1,0:T(8,128)(2,1)} %bitcast.29, bf16[640,640]{1,0:T(8,128)(2,1)} %bitcast.25, ...), custom_call_target="tpu_custom_call", output_to_operand_aliasing={{0}: (4, {})} | custom-call | flops 4194304 | bytes 3903488 | tf_op jit(solution)/shard_map/pallas_call | solution.py:34
  40.3 0.1 collective-permute-done.9.refs_10_.refs_11_
  40.4 0.0 collective-permute-done.7.refs_8_
  40.4 0.7 %collective-permute-done.8.refs_9_ = bf16[256,128]{1,0:T(8,128)(2,1)S(1)} collective-permute-done((bf16[256,128]{1,0:T(8,128)(2,1)S(1)}, bf16[256,128]{1,0:T(8,128)(2,1)S(1)}, u32[]{:S(2)}, u32[]{:S(2)}) %collective-permute-start.8) | collective-permute-done | bytes 65568 | tf_op jit(solution)/shard_map/ppermute | solution.py:633
  41.1 0.4 all-to-all-done.1
  41.5 1.8 %shard_map.92 = (f32[640,128]{1,0:T(8,128)S(1)}, bf16[32,16,128]{2,1,0:T(8,128)(2,1)}, bf16[256,128]{1,0:T(8,128)(2,1)S(1)}, bf16[256,128]{1,0:T(8,128)(2,1)S(1)...) custom-call(s32[1,1]{1,0:T(1,128)S(6)} %copy.17.live, ...), custom_call_target="tpu_custom_call", output_to_operand_aliasing={{6}: (17, {})} | custom-call | flops 4194304 | bytes 3899400 | tf_op jit(solution)/shard_map/pallas_call | solution.py:34
  43.4 4.0 %all-to-all-start.2 = ((bf16[32,16,128]{2,1,0:T(8,128)(2,1)}), bf16[32,16,128]{2,1,0:T(8,128)(2,1)S(1)}, u32[]{:S(2)}, u32[]{:S(2)}) async-start(bf16[32,16,128]{2,1,0:T(8,128)(2,1)} %get-tuple-element.71), calls=%async_computation.2 | async-start | bytes 262144 | tf_op jit(solution)/shard_map/all_to_all | solution.py:631
  47.4 1.8 %collective-permute-start.10 = (bf16[256,128]{1,0:T(8,128)(2,1)S(1)}, bf16[256,128]{1,0:T(8,128)(2,1)S(1)}, u32[]{:S(2)}, u32[]{:S(2)}) collective-permute-start(bf16[256,128]{1,0:T(8,128)(2,1)S(1)} %get-tuple-element.77.refs_6_), channel_id=1, source_target_pairs={{0,1},{1,2},{2,3},{3,0},{4,5},{5,6},{6,7},{7,4},{8,9},{9,10},{10,1... | collective-permute-start | bytes 196616 | tf_op jit(solution)/shard_map/ppermute | solution.py:632
  49.2 1.2 %collective-permute-start.11 = (bf16[256,128]{1,0:T(8,128)(2,1)S(1)}, bf16[256,128]{1,0:T(8,128)(2,1)S(1)}, u32[]{:S(2)}, u32[]{:S(2)}) collective-permute-start(bf16[256,128]{1,0:T(8,128)(2,1)S(1)} %get-tuple-element.78.refs_7_), channel_id=1, source_target_pairs={{0,3},{1,0},{2,1},{3,2},{4,7},{5,4},{6,5},{7,6},{8,11},{9,8},{10,9... | collective-permute-start | bytes 196616 | tf_op jit(solution)/shard_map/ppermute | solution.py:633
  50.3 1.8 %collective-permute-start.12 = (bf16[128,128]{1,0:T(8,128)(2,1)S(1)}, bf16[128,128]{1,0:T(8,128)(2,1)S(1)}, u32[]{:S(2)}, u32[]{:S(2)}) collective-permute-start(bf16[128,128]{1,0:T(8,128)(2,1)S(1)} %get-tuple-element.79), channel_id=1, source_target_pairs={{0,2},{1,3},{2,0},{3,1},{4,6},{5,7},{6,4},{7,5},{8,10},{9,11},{10,... | collective-permute-start | bytes 98312 | tf_op jit(solution)/shard_map/ppermute | solution.py:635
  52.1 2.5 %shard_map.93 = (f32[640,128]{1,0:T(8,128)S(1)}, f32[640,128]{1,0:T(8,128)S(1)}, f32[512,128]{1,0:T(8,128)}) custom-call(s32[1,1]{1,0:T(1,128)S(6)} %copy.17.live, f32[640,128]{1,0:T(8,128)S(1)} %get-tuple-element.72.resid.refs_5_, bf16[640,640]{1,0:T(8,128)(2,1)} %bitcast.30, bf16[640,640]{1,0:T(8,128)(2,1)} %bitcast.26, ...), custom_call_target="tpu_custom_call", output_to_operand_aliasing={{0}: (4, {})} | custom-call | flops 4194304 | bytes 4165632 | tf_op jit(solution)/shard_map/pallas_call | solution.py:34
  54.6 0.0 collective-permute-done.12.refs_10_.refs_11_
  54.6 0.0 collective-permute-done.10.refs_8_
  54.6 0.4 collective-permute-done.11.refs_9_
  55.1 0.4 all-to-all-done.2
  55.5 2.5 %shard_map.94 = (f32[512,128]{1,0:T(8,128)}, f32[512,128]{1,0:T(8,128)}) custom-call(s32[1,1]{1,0:T(1,128)S(6)} %copy.17.live, s32[1,2]{1,0:T(1,128)S(1)} %get-tuple-element.43.margin_in.refs_4_, bf16[512,128]{1,0:T(8,128)(2,1)S(1)} %bitcast.16, bf16[64,512]{1,0:T(8,128)(2,1)S(1)} %get-tuple-element.62.refs_1_, ...), custom_call_target="tpu_custom_call" | custom-call | flops 4194304 | bytes 3719176 | tf_op jit(solution)/shard_map/pallas_call | solution.py:34
Async XLA Ops:
  0.6 6.3 %copy-start.2 = (bf16[1,1,640,16]{2,3,1,0:T(8,128)(2,1)S(1)}, bf16[1,1,640,16]{2,3,1,0:T(8,128)(2,1)}, u32[]{:S(2)}) copy-start(bf16[1,1,640,16]{2,3,1,0:T(8,128)(2,1)} %param.12) | copy-start | bytes 61444
  2.2 5.9 %collective-permute-start = (bf16[144,128]{1,0:T(8,128)(2,1)S(1)}, bf16[144,128]{1,0:T(8,128)(2,1)S(1)}, u32[]{:S(2)}, u32[]{:S(2)}) collective-permute-start(bf16[144,128]{1,0:T(8,128)(2,1)S(1)} %get-tuple-element.47), channel_id=1, source_target_pairs={{0,1},{1,2},{2,3},{3,0},{4,5},{5,6},{6,7},{7,4},{8,9},{9,10},{10,1... | collective-permute-start | bytes 110600 | tf_op jit(solution)/shard_map/ppermute | solution.py:576
  5.3 4.0 %collective-permute-start.1 = (bf16[144,128]{1,0:T(8,128)(2,1)S(1)}, bf16[144,128]{1,0:T(8,128)(2,1)S(1)}, u32[]{:S(2)}, u32[]{:S(2)}) collective-permute-start(bf16[144,128]{1,0:T(8,128)(2,1)S(1)} %get-tuple-element.48), channel_id=1, source_target_pairs={{0,3},{1,0},{2,1},{3,2},{4,7},{5,4},{6,5},{7,6},{8,11},{9,8},{10,9... | collective-permute-start | bytes 110600 | tf_op jit(solution)/shard_map/ppermute | solution.py:576
  6.9 2.3 %copy-start = (f32[1,1,512,128]{3,2,1,0:T(8,128)S(1)}, f32[1,1,512,128]{3,2,1,0:T(8,128)}, u32[]{:S(2)}) copy-start(f32[1,1,512,128]{3,2,1,0:T(8,128)} %param.7) | copy-start | bytes 786436
  7.0 2.3 %copy-start.1 = (bf16[64,128]{1,0:T(8,128)(2,1)S(1)}, bf16[64,128]{1,0:T(8,128)(2,1)}, u32[]{:S(2)}) copy-start(bf16[64,128]{1,0:T(8,128)(2,1)} %param.13) | copy-start | bytes 49156
  10.2 17.3 %all-to-all-start = ((bf16[32,16,128]{2,1,0:T(8,128)(2,1)}), bf16[32,16,128]{2,1,0:T(8,128)(2,1)S(1)}, u32[]{:S(2)}, u32[]{:S(2)}) async-start(bf16[32,16,128]{2,1,0:T(8,128)(2,1)} %get-tuple-element.50), calls=%async_computation | async-start | bytes 262144 | tf_op jit(solution)/shard_map/all_to_all | solution.py:631
  16.0 7.7 %collective-permute-start.2 = (bf16[272,128]{1,0:T(8,128)(2,1)S(1)}, bf16[272,128]{1,0:T(8,128)(2,1)S(1)}, u32[]{:S(2)}, u32[]{:S(2)}) collective-permute-start(bf16[272,128]{1,0:T(8,128)(2,1)S(1)} %get-tuple-element.52), channel_id=1, source_target_pairs={{0,1},{1,2},{2,3},{3,0},{4,5},{5,6},{6,7},{7,4},{8,9},{9,10},{10,1... | collective-permute-start | bytes 208904 | tf_op jit(solution)/shard_map/ppermute | solution.py:576
  17.8 6.6 %collective-permute-start.3 = (bf16[272,128]{1,0:T(8,128)(2,1)S(1)}, bf16[272,128]{1,0:T(8,128)(2,1)S(1)}, u32[]{:S(2)}, u32[]{:S(2)}) collective-permute-start(bf16[272,128]{1,0:T(8,128)(2,1)S(1)} %get-tuple-element.53), channel_id=1, source_target_pairs={{0,3},{1,0},{2,1},{3,2},{4,7},{5,4},{6,5},{7,6},{8,11},{9,8},{10,9... | collective-permute-start | bytes 208904 | tf_op jit(solution)/shard_map/ppermute | solution.py:576
  18.9 8.5 %collective-permute-start.4 = (bf16[256,128]{1,0:T(8,128)(2,1)S(1)}, bf16[256,128]{1,0:T(8,128)(2,1)S(1)}, u32[]{:S(2)}, u32[]{:S(2)}) collective-permute-start(bf16[256,128]{1,0:T(8,128)(2,1)S(1)} %get-tuple-element.57.refs_8_), channel_id=1, source_target_pairs={{0,1},{1,2},{2,3},{3,0},{4,5},{5,6},{6,7},{7,4},{8,9},{9,10},{10,1... | collective-permute-start | bytes 196616 | tf_op jit(solution)/shard_map/ppermute | solution.py:632
  19.8 7.7 %collective-permute-start.5 = (bf16[256,128]{1,0:T(8,128)(2,1)S(1)}, bf16[256,128]{1,0:T(8,128)(2,1)S(1)}, u32[]{:S(2)}, u32[]{:S(2)}) collective-permute-start(bf16[256,128]{1,0:T(8,128)(2,1)S(1)} %get-tuple-element.58.refs_9_), channel_id=1, source_target_pairs={{0,3},{1,0},{2,1},{3,2},{4,7},{5,4},{6,5},{7,6},{8,11},{9,8},{10,9... | collective-permute-start | bytes 196616 | tf_op jit(solution)/shard_map/ppermute | solution.py:633
  21.9 5.6 %collective-permute-start.6 = (bf16[208,128]{1,0:T(8,128)(2,1)S(1)}, bf16[208,128]{1,0:T(8,128)(2,1)S(1)}, u32[]{:S(2)}, u32[]{:S(2)}) collective-permute-start(bf16[208,128]{1,0:T(8,128)(2,1)S(1)} %get-tuple-element.59), channel_id=1, source_target_pairs={{0,2},{1,3},{2,0},{3,1},{4,6},{5,7},{6,4},{7,5},{8,10},{9,11},{10,... | collective-permute-start | bytes 159752 | tf_op jit(solution)/shard_map/ppermute | solution.py:635
  29.2 12.3 %all-to-all-start.1 = ((bf16[32,16,128]{2,1,0:T(8,128)(2,1)}), bf16[32,16,128]{2,1,0:T(8,128)(2,1)S(1)}, u32[]{:S(2)}, u32[]{:S(2)}) async-start(bf16[32,16,128]{2,1,0:T(8,128)(2,1)} %get-tuple-element.61), calls=%async_computation.1 | async-start | bytes 262144 | tf_op jit(solution)/shard_map/all_to_all | solution.py:631
  33.4 7.0 %collective-permute-start.7 = (bf16[256,128]{1,0:T(8,128)(2,1)S(1)}, bf16[256,128]{1,0:T(8,128)(2,1)S(1)}, u32[]{:S(2)}, u32[]{:S(2)}) collective-permute-start(bf16[256,128]{1,0:T(8,128)(2,1)S(1)} %get-tuple-element.67.refs_6_), channel_id=1, source_target_pairs={{0,1},{1,2},{2,3},{3,0},{4,5},{5,6},{6,7},{7,4},{8,9},{9,10},{10,1... | collective-permute-start | bytes 196616 | tf_op jit(solution)/shard_map/ppermute | solution.py:632
  35.2 5.9 %collective-permute-start.8 = (bf16[256,128]{1,0:T(8,128)(2,1)S(1)}, bf16[256,128]{1,0:T(8,128)(2,1)S(1)}, u32[]{:S(2)}, u32[]{:S(2)}) collective-permute-start(bf16[256,128]{1,0:T(8,128)(2,1)S(1)} %get-tuple-element.68.refs_7_), channel_id=1, source_target_pairs={{0,3},{1,0},{2,1},{3,2},{4,7},{5,4},{6,5},{7,6},{8,11},{9,8},{10,9... | collective-permute-start | bytes 196616 | tf_op jit(solution)/shard_map/ppermute | solution.py:633
  36.3 4.1 %collective-permute-start.9 = (bf16[128,128]{1,0:T(8,128)(2,1)S(1)}, bf16[128,128]{1,0:T(8,128)(2,1)S(1)}, u32[]{:S(2)}, u32[]{:S(2)}) collective-permute-start(bf16[128,128]{1,0:T(8,128)(2,1)S(1)} %get-tuple-element.69), channel_id=1, source_target_pairs={{0,2},{1,3},{2,0},{3,1},{4,6},{5,7},{6,4},{7,5},{8,10},{9,11},{10,... | collective-permute-start | bytes 98312 | tf_op jit(solution)/shard_map/ppermute | solution.py:635
  43.4 12.2 %all-to-all-start.2 = ((bf16[32,16,128]{2,1,0:T(8,128)(2,1)}), bf16[32,16,128]{2,1,0:T(8,128)(2,1)S(1)}, u32[]{:S(2)}, u32[]{:S(2)}) async-start(bf16[32,16,128]{2,1,0:T(8,128)(2,1)} %get-tuple-element.71), calls=%async_computation.2 | async-start | bytes 262144 | tf_op jit(solution)/shard_map/all_to_all | solution.py:631
  47.4 7.3 %collective-permute-start.10 = (bf16[256,128]{1,0:T(8,128)(2,1)S(1)}, bf16[256,128]{1,0:T(8,128)(2,1)S(1)}, u32[]{:S(2)}, u32[]{:S(2)}) collective-permute-start(bf16[256,128]{1,0:T(8,128)(2,1)S(1)} %get-tuple-element.77.refs_6_), channel_id=1, source_target_pairs={{0,1},{1,2},{2,3},{3,0},{4,5},{5,6},{6,7},{7,4},{8,9},{9,10},{10,1... | collective-permute-start | bytes 196616 | tf_op jit(solution)/shard_map/ppermute | solution.py:632
  49.2 5.9 %collective-permute-start.11 = (bf16[256,128]{1,0:T(8,128)(2,1)S(1)}, bf16[256,128]{1,0:T(8,128)(2,1)S(1)}, u32[]{:S(2)}, u32[]{:S(2)}) collective-permute-start(bf16[256,128]{1,0:T(8,128)(2,1)S(1)} %get-tuple-element.78.refs_7_), channel_id=1, source_target_pairs={{0,3},{1,0},{2,1},{3,2},{4,7},{5,4},{6,5},{7,6},{8,11},{9,8},{10,9... | collective-permute-start | bytes 196616 | tf_op jit(solution)/shard_map/ppermute | solution.py:633
  50.3 4.3 %collective-permute-start.12 = (bf16[128,128]{1,0:T(8,128)(2,1)S(1)}, bf16[128,128]{1,0:T(8,128)(2,1)S(1)}, u32[]{:S(2)}, u32[]{:S(2)}) collective-permute-start(bf16[128,128]{1,0:T(8,128)(2,1)S(1)} %get-tuple-element.79), channel_id=1, source_target_pairs={{0,2},{1,3},{2,0},{3,1},{4,6},{5,7},{6,4},{7,5},{8,10},{9,11},{10,... | collective-permute-start | bytes 98312 | tf_op jit(solution)/shard_map/ppermute | solution.py:635
